TPU v7x, 32 devices: a whole 2x2x4 slice. The times are simulated.
32 devices in a mesh: dp: 8 (over z, x), tensor: 4 (over y, core).
Axes of the slice: x: 2, y: 2, z: 4, core: 2. Of those that a mesh axis runs over, the one named last changes fastest.
Arguments:
- inputs: bfloat16 [3, 2048, 2048], P(None, ('dp', 'tensor')), may hold values from -6 to 6
- cotangent: bfloat16 [3, 2048, 2048], P(None, ('dp', 'tensor')), may hold values from -6 to 6
- doc_ids: int32 [3, 2048], replicated, may hold values from 0 to 7, never falling along the last dimension, each value on 1 to 1280 neighbouring positions
- attn_gain: bfloat16 [2048], P('dp'), may hold values from 0.5 to 1.5
- attn_shift: bfloat16 [2048], P('dp'), may hold values from -3 to 3
- w_query: bfloat16 [2048, 2048], P('dp', 'tensor'), may hold values from -0.125 to 0.125
- w_keyval: bfloat16 [2048, 256], P('dp'), may hold values from -0.125 to 0.125
- w_attn_out: bfloat16 [2048, 2048], P('tensor', 'dp'), may hold values from -2 to 2
- mlp_gain: bfloat16 [2048], P('dp'), may hold values from 0.5 to 1.5
- mlp_shift: bfloat16 [2048], P('dp'), may hold values from -3 to 3
- w_expand: bfloat16 [2048, 8192], P('dp', 'tensor'), may hold values from -0.125 to 0.125
- w_reduce: bfloat16 [8192, 2048], P('tensor', 'dp'), may hold values from -0.0625 to 0.0625
Outputs:
- outputs: bfloat16 [3, 2048, 2048], P(None, ('dp', 'tensor'))
- grad_inputs: float32 [3, 2048, 2048], P(None, ('dp', 'tensor'))
- grad_attn_gain: float32 [2048], P(('dp', 'tensor'))
- grad_attn_shift: float32 [2048], P(('dp', 'tensor'))
- grad_query: float32 [2048, 2048], P('dp', 'tensor')
- grad_keyval: float32 [2048, 256], P(('dp', 'tensor'))
- grad_attn_out: float32 [2048, 2048], P('tensor', 'dp')
- grad_mlp_gain: float32 [2048], P(('dp', 'tensor'))
- grad_mlp_shift: float32 [2048], P(('dp', 'tensor'))
- grad_expand: float32 [2048, 8192], P('dp', 'tensor')
- grad_reduce: float32 [8192, 2048], P('tensor', 'dp')
Inputs may be any that keep to these rules, and one draw needn't show every extreme that they name: `doc_ids`: within each row the ids never fall; each document spans 1 to 1280 tokens, and one spans exactly 1280.
All inputs are finite; a program needn't handle non-finite values.
Results may differ from a plain program's by a relative error of at most 0.02.
Values may be sent and summed in bfloat16 or wider, within the bound.
A program may use at most 120 MiB of HBM per device.

v0:
```python
import math

import jax
import jax.numpy as jnp
from jax import lax
from jax.sharding import PartitionSpec as P

BLOCK = 256


EPSILON = 1e-05
NEG_FILL = -1e30


def layer_norm(values, gain, shift):
    center = jnp.mean(values, axis=-1, keepdims=True)
    centered = values - center
    variance = jnp.mean(centered * centered, axis=-1, keepdims=True)
    return centered * lax.rsqrt(variance + EPSILON) * gain + shift


def gelu_tanh(values):
    return jax.nn.gelu(values, approximate=True)


def block_scores(queries, key_piece, query_doc, key_doc, query_blk, key_blk, score_scale):
    raw = (
        jnp.einsum("ghd,kd->ghk", queries, key_piece, preferred_element_type=jnp.float32)
        * score_scale
    )
    allowed = (query_doc[:, None] == key_doc[None, :]) & (key_blk[None, :] <= query_blk[:, None])
    return (jnp.where(allowed[:, None, :], raw, NEG_FILL), allowed[:, None, :])


def split_blocks(keys_vals, doc_row, key_blk, group_rows):
    block_count = keys_vals.shape[0] // group_rows
    return (
        keys_vals.reshape(block_count, group_rows, keys_vals.shape[1]),
        doc_row.reshape(block_count, group_rows),
        key_blk.reshape(block_count, group_rows),
    )


def attend_forward(queries, keys_vals, query_doc, doc_row, query_blk, key_blk):
    group_rows, local_heads, head_dim = queries.shape
    score_scale = 1.0 / math.sqrt(head_dim)
    pieces_all = split_blocks(keys_vals, doc_row, key_blk, group_rows)

    def stats_step(state_pair, pieces):
        running_top, running_sum = state_pair
        kv_piece, doc_piece, blk_piece = pieces
        scores, allowed = block_scores(
            queries, kv_piece[:, :head_dim], query_doc, doc_piece, query_blk, blk_piece, score_scale
        )
        new_top = jnp.maximum(running_top, jnp.max(scores, axis=-1))
        weights = jnp.where(allowed, jnp.exp(scores - new_top[..., None]), 0.0)
        new_sum = running_sum * jnp.exp(running_top - new_top) + jnp.sum(weights, axis=-1)
        return ((new_top, new_sum), None)

    start_top = jnp.full((group_rows, local_heads), NEG_FILL, jnp.float32)
    start_sum = jnp.zeros((group_rows, local_heads), jnp.float32)
    (running_top, running_sum), unused = lax.scan(stats_step, (start_top, start_sum), pieces_all)
    log_total = running_top + jnp.log(running_sum)

    def mix_step(mixed_low, pieces):
        kv_piece, doc_piece, blk_piece = pieces
        scores, allowed = block_scores(
            queries, kv_piece[:, :head_dim], query_doc, doc_piece, query_blk, blk_piece, score_scale
        )
        probs = jnp.where(allowed, jnp.exp(scores - log_total[..., None]), 0.0)
        mixed_low = mixed_low + jnp.einsum(
            "ghk,kd->ghd",
            probs.astype(jnp.bfloat16),
            kv_piece[:, head_dim:],
            preferred_element_type=jnp.float32,
        )
        return (mixed_low, None)

    zero_mix = jnp.zeros((group_rows, local_heads, head_dim), jnp.float32)
    mixed_low, unused = lax.scan(mix_step, zero_mix, pieces_all)
    return (log_total, mixed_low)


def attend_backward(
    queries, keys_vals, grad_mixed, log_total, row_delta, query_doc, doc_row, query_blk, key_blk
):
    group_rows, local_heads, head_dim = queries.shape
    score_scale = 1.0 / math.sqrt(head_dim)
    pieces_all = split_blocks(keys_vals, doc_row, key_blk, group_rows)

    def grad_step(grad_queries, pieces):
        kv_piece, doc_piece, blk_piece = pieces
        keys_piece = kv_piece[:, :head_dim]
        values_piece = kv_piece[:, head_dim:]
        scores, allowed = block_scores(
            queries, keys_piece, query_doc, doc_piece, query_blk, blk_piece, score_scale
        )
        probs = jnp.where(allowed, jnp.exp(scores - log_total[..., None]), 0.0)
        grad_probs = jnp.einsum(
            "ghd,kd->ghk", grad_mixed, values_piece, preferred_element_type=jnp.float32
        )
        grad_scores = (probs * (grad_probs - row_delta[..., None])).astype(jnp.bfloat16)
        grad_queries = (
            grad_queries
            + jnp.einsum("ghk,kd->ghd", grad_scores, keys_piece, preferred_element_type=jnp.float32)
            * score_scale
        )
        grad_keys = (
            jnp.einsum("ghk,ghd->kd", grad_scores, queries, preferred_element_type=jnp.float32)
            * score_scale
        )
        grad_values = jnp.einsum(
            "ghk,ghd->kd",
            probs.astype(jnp.bfloat16),
            grad_mixed,
            preferred_element_type=jnp.float32,
        )
        return (grad_queries, jnp.concatenate([grad_keys, grad_values], axis=-1))

    zero_grad = jnp.zeros((group_rows, local_heads, head_dim), jnp.float32)
    grad_queries, grad_blocks = lax.scan(grad_step, zero_grad, pieces_all)
    return (grad_queries, grad_blocks.reshape(keys_vals.shape[0], 2 * head_dim))


def local(
    inputs,
    cotangent,
    doc_ids,
    attn_gain,
    attn_shift,
    w_query,
    w_keyval,
    w_attn_out,
    mlp_gain,
    mlp_shift,
    w_expand,
    w_reduce,
):

    def fetch():
        return (
            lax.all_gather(w_query, "dp", axis=0, tiled=True),
            lax.all_gather(w_keyval, "dp", axis=0, tiled=True),
            lax.all_gather(w_attn_out, "dp", axis=1, tiled=True),
            lax.all_gather(w_expand, "dp", axis=0, tiled=True),
            lax.all_gather(w_reduce, "dp", axis=1, tiled=True),
            lax.all_gather(attn_gain, "dp", axis=0, tiled=True),
            lax.all_gather(attn_shift, "dp", axis=0, tiled=True),
            lax.all_gather(mlp_gain, "dp", axis=0, tiled=True),
            lax.all_gather(mlp_shift, "dp", axis=0, tiled=True),
        )

    tensor_count = lax.axis_size("tensor")
    dp_rank = lax.axis_index("dp")
    micro_count, own_rows, width = inputs.shape
    group_rows = own_rows * tensor_count
    seq_len = doc_ids.shape[1]
    head_dim = w_keyval.shape[1] // 2
    local_heads = w_query.shape[1] // head_dim
    local_units = w_expand.shape[1]
    query_pos = dp_rank * group_rows + jnp.arange(group_rows, dtype=jnp.int32)
    query_blk = query_pos // BLOCK
    key_blk = jnp.arange(seq_len, dtype=jnp.int32) // BLOCK
    acc_query = jnp.zeros((width, local_heads * head_dim), jnp.float32)
    acc_attn_out = jnp.zeros((local_heads * head_dim, width), jnp.float32)
    acc_expand = jnp.zeros((width, local_units), jnp.float32)
    acc_reduce = jnp.zeros((local_units, width), jnp.float32)
    acc_keyval = jnp.zeros((width, 2 * head_dim), jnp.float32)
    acc_gain_one = jnp.zeros((width,), jnp.float32)
    acc_shift_one = jnp.zeros((width,), jnp.float32)
    acc_gain_two = jnp.zeros((width,), jnp.float32)
    acc_shift_two = jnp.zeros((width,), jnp.float32)
    result_rows = []
    grad_rows = []
    for micro_batch in range(micro_count):
        fetched = fetch()
        (
            wq_full,
            wkv_full,
            wo_full,
            wexp_full,
            wred_full,
            gain_one,
            shift_one,
            gain_two,
            shift_two,
        ) = fetched
        tokens = inputs[micro_batch].astype(jnp.float32)
        doc_row = doc_ids[micro_batch]
        query_doc = lax.dynamic_slice_in_dim(doc_row, dp_rank * group_rows, group_rows)
        normed_full, norm_pull_one = jax.vjp(
            layer_norm, tokens, gain_one.astype(jnp.float32), shift_one.astype(jnp.float32)
        )
        normed_own = normed_full.astype(jnp.bfloat16)
        normed = lax.all_gather(normed_own, "tensor", axis=0, tiled=True)
        queries = (
            jnp.dot(normed, wq_full, preferred_element_type=jnp.float32)
            .astype(jnp.bfloat16)
            .reshape(group_rows, local_heads, head_dim)
        )
        kv_group = jnp.dot(normed, wkv_full, preferred_element_type=jnp.float32).astype(
            jnp.bfloat16
        )
        keys_vals = lax.all_gather(kv_group, "dp", axis=0, tiled=True)
        log_total, mixed_low = attend_forward(
            queries, keys_vals, query_doc, doc_row, query_blk, key_blk
        )
        mixed = mixed_low.astype(jnp.bfloat16).reshape(group_rows, local_heads * head_dim)
        branch = lax.psum_scatter(
            jnp.dot(mixed, wo_full, preferred_element_type=jnp.float32).astype(jnp.bfloat16),
            "tensor",
            scatter_dimension=0,
            tiled=True,
        ).astype(jnp.float32)
        middle = tokens + branch
        normed_two_full, norm_pull_two = jax.vjp(
            layer_norm, middle, gain_two.astype(jnp.float32), shift_two.astype(jnp.float32)
        )
        normed_two, cot_rows = (
            lax.all_gather(normed_two_full.astype(jnp.bfloat16), "tensor", axis=0, tiled=True),
            lax.all_gather(cotangent[micro_batch], "tensor", axis=0, tiled=True),
        )
        hidden = jnp.dot(normed_two, wexp_full, preferred_element_type=jnp.float32)
        gelu_value, gelu_pull = jax.vjp(gelu_tanh, hidden)
        active = gelu_value.astype(jnp.bfloat16)
        reduced = lax.psum_scatter(
            jnp.dot(active, wred_full, preferred_element_type=jnp.float32).astype(jnp.bfloat16),
            "tensor",
            scatter_dimension=0,
            tiled=True,
        ).astype(jnp.float32)
        result_rows.append((middle + reduced).astype(jnp.bfloat16))
        back = fetch()
        wq_back, wkv_back, wo_back, wexp_back, wred_back = (
            back[0],
            back[1],
            back[2],
            back[3],
            back[4],
        )
        acc_reduce = acc_reduce + jnp.einsum(
            "gf,gd->fd", active, cot_rows, preferred_element_type=jnp.float32
        )
        grad_active = jnp.einsum(
            "gd,fd->gf", cot_rows, wred_back, preferred_element_type=jnp.float32
        )
        grad_hidden = gelu_pull(grad_active)[0].astype(jnp.bfloat16)
        acc_expand = acc_expand + jnp.einsum(
            "gd,gf->df", normed_two, grad_hidden, preferred_element_type=jnp.float32
        )
        grad_normed_two = lax.psum_scatter(
            jnp.einsum(
                "gf,df->gd", grad_hidden, wexp_back, preferred_element_type=jnp.float32
            ).astype(jnp.bfloat16),
            "tensor",
            scatter_dimension=0,
            tiled=True,
        ).astype(jnp.float32)
        grad_mid_norm, grad_gain_two, grad_shift_two = norm_pull_two(grad_normed_two)
        acc_gain_two = acc_gain_two + grad_gain_two
        acc_shift_two = acc_shift_two + grad_shift_two
        grad_middle = cotangent[micro_batch].astype(jnp.float32) + grad_mid_norm
        grad_branch = lax.all_gather(grad_middle.astype(jnp.bfloat16), "tensor", axis=0, tiled=True)
        acc_attn_out = acc_attn_out + jnp.einsum(
            "gc,gd->cd", mixed, grad_branch, preferred_element_type=jnp.float32
        )
        grad_mixed = (
            jnp.einsum("gd,cd->gc", grad_branch, wo_back, preferred_element_type=jnp.float32)
            .astype(jnp.bfloat16)
            .reshape(group_rows, local_heads, head_dim)
        )
        row_delta = jnp.sum(grad_mixed.astype(jnp.float32) * mixed_low, axis=-1)
        grad_queries, grad_kv_rows = attend_backward(
            queries,
            keys_vals,
            grad_mixed,
            log_total,
            row_delta,
            query_doc,
            doc_row,
            query_blk,
            key_blk,
        )
        grad_kv_own = lax.psum_scatter(
            grad_kv_rows, ("dp", "tensor"), scatter_dimension=0, tiled=True
        ).astype(jnp.bfloat16)
        grad_q_low = grad_queries.astype(jnp.bfloat16).reshape(group_rows, local_heads * head_dim)
        acc_query = acc_query + jnp.einsum(
            "gd,gc->dc", normed, grad_q_low, preferred_element_type=jnp.float32
        )
        acc_keyval = acc_keyval + jnp.einsum(
            "td,tc->dc", normed_own, grad_kv_own, preferred_element_type=jnp.float32
        )
        grad_from_query = lax.psum_scatter(
            jnp.einsum("gc,dc->gd", grad_q_low, wq_back, preferred_element_type=jnp.float32).astype(
                jnp.bfloat16
            ),
            "tensor",
            scatter_dimension=0,
            tiled=True,
        ).astype(jnp.float32)
        grad_normed = grad_from_query + jnp.einsum(
            "tc,dc->td", grad_kv_own, wkv_back, preferred_element_type=jnp.float32
        )
        grad_tok_norm, grad_gain_one, grad_shift_one = norm_pull_one(grad_normed)
        acc_gain_one = acc_gain_one + grad_gain_one
        acc_shift_one = acc_shift_one + grad_shift_one
        grad_rows.append(grad_middle + grad_tok_norm)
    grad_query, grad_attn_out, grad_expand, grad_reduce = (
        lax.psum_scatter(
            acc_query.astype(jnp.bfloat16), "dp", scatter_dimension=0, tiled=True
        ).astype(jnp.float32),
        lax.psum_scatter(
            acc_attn_out.astype(jnp.bfloat16), "dp", scatter_dimension=1, tiled=True
        ).astype(jnp.float32),
        lax.psum_scatter(
            acc_expand.astype(jnp.bfloat16), "dp", scatter_dimension=0, tiled=True
        ).astype(jnp.float32),
        lax.psum_scatter(
            acc_reduce.astype(jnp.bfloat16), "dp", scatter_dimension=1, tiled=True
        ).astype(jnp.float32),
    )
    grad_keyval, grad_attn_gain, grad_attn_shift, grad_mlp_gain, grad_mlp_shift = (
        lax.psum_scatter(acc_keyval, ("dp", "tensor"), scatter_dimension=0, tiled=True),
        lax.psum_scatter(acc_gain_one, ("dp", "tensor"), scatter_dimension=0, tiled=True),
        lax.psum_scatter(acc_shift_one, ("dp", "tensor"), scatter_dimension=0, tiled=True),
        lax.psum_scatter(acc_gain_two, ("dp", "tensor"), scatter_dimension=0, tiled=True),
        lax.psum_scatter(acc_shift_two, ("dp", "tensor"), scatter_dimension=0, tiled=True),
    )
    return (
        jnp.stack(result_rows),
        jnp.stack(grad_rows),
        grad_attn_gain,
        grad_attn_shift,
        grad_query,
        grad_keyval,
        grad_attn_out,
        grad_mlp_gain,
        grad_mlp_shift,
        grad_expand,
        grad_reduce,
    )


def solution(mesh):
    placed = (
        P(None, ("dp", "tensor"), None),
        P(None, ("dp", "tensor"), None),
        P(),
        P("dp"),
        P("dp"),
        P("dp", "tensor"),
        P("dp", None),
        P("tensor", "dp"),
        P("dp"),
        P("dp"),
        P("dp", "tensor"),
        P("tensor", "dp"),
    )
    return jax.shard_map(
        local,
        mesh=mesh,
        in_specs=placed,
        out_specs=(
            P(None, ("dp", "tensor"), None),
            P(None, ("dp", "tensor"), None),
            P(("dp", "tensor")),
            P(("dp", "tensor")),
            P("dp", "tensor"),
            P(("dp", "tensor"), None),
            P("tensor", "dp"),
            P(("dp", "tensor")),
            P(("dp", "tensor")),
            P("dp", "tensor"),
            P("tensor", "dp"),
        ),
        check_vma=False,
    )
```

profile of v0, /device:TPU:0, one launch (start us, length us, event | category | flops | bytes accessed | tf_op | source)
XLA Modules:
  0.0 2168.7 jit_solution(1634423567724420899)
XLA Ops:
  11.1 22.2 %all-gather.4 = bf16[8,1,256]{2,1,0:T(2,128)(2,1)S(1)} all-gather(bf16[1,1,256]{2,1,0:T(2,128)(2,1)S(1)} %reshape.761), channel_id=1, replica_groups=mesh['dp'=8,'tensor'=4] {'dp'}, dimensions={0}, use_global_device_ids=true | all-gather | bytes 4608 | tf_op jit(solution)/shard_map/all_gather | solution.py:148
  33.4 16.3 all-gather.3
  53.1 14.1 all-gather.28.cloned.1.call-done
  67.2 42.3 %all-gather.30.cloned.1.call-done = bf16[2048,256]{1,0:T(8,128)(2,1)} async-done(((bf16[256,256]{1,0:T(8,128)(2,1)}), bf16[2048,256]{1,0:T(8,128)(2,1)}) %all-gather.30.cloned.1.call-update) | async-done | bytes 1048592 | tf_op jit(solution)/shard_map/all_gather | solution.py:143
  113.0 46.7 %all-gather.34.cloned.1.call-done = bf16[2048,512]{1,0:T(8,128)(2,1)} async-done(((bf16[256,512]{1,0:T(8,128)(2,1)}), bf16[2048,512]{1,0:T(8,128)(2,1)}) %all-gather.34.cloned.1.call-update) | async-done | bytes 2097168 | tf_op jit(solution)/shard_map/all_gather | solution.py:142
  162.1 38.9 %all-gather.32.cloned.1.call-done = bf16[2048,256]{1,0:T(8,128)(2,1)} async-done(((bf16[256,256]{1,0:T(8,128)(2,1)}), bf16[2048,256]{1,0:T(8,128)(2,1)}) %all-gather.32.cloned.1.call-update) | async-done | bytes 1048592 | tf_op jit(solution)/shard_map/all_gather | solution.py:204
  200.9 13.6 while.111
  214.6 15.4 while.112
  230.1 22.6 %all-gather.36.cloned.1.call-done = bf16[512,2048]{1,0:T(8,128)(2,1)} async-done(((bf16[512,256]{1,0:T(8,128)(2,1)}), bf16[512,2048]{1,0:T(8,128)(2,1)}) %all-gather.36.cloned.1.call-update) | async-done | bytes 2097168 | tf_op jit(solution)/shard_map/all_gather | solution.py:144
  256.2 23.1 %reduce-scatter.21.cloned.1.call-done = bf16[64,2048]{1,0:T(8,128)(2,1)} async-done(((bf16[256,2048]{1,0:T(8,128)(2,1)}), bf16[64,2048]{1,0:T(8,128)(2,1)}) %reduce-scatter.21.cloned.1.call-update) | async-done | bytes 262160 | tf_op jit(solution)/shard_map/reduce_scatter | solution.py:209
  283.2 16.1 all-gather.50.cloned.1.call-done
  305.0 12.7 all-gather.44.cloned.1.call-done
  321.7 39.2 %all-gather.52.cloned.1.call-done = bf16[2048,256]{1,0:T(8,128)(2,1)} async-done(((bf16[256,256]{1,0:T(8,128)(2,1)}), bf16[2048,256]{1,0:T(8,128)(2,1)}) %all-gather.52.cloned.1.call-update) | async-done | bytes 1048592 | tf_op jit(solution)/shard_map/all_gather | solution.py:204
  360.8 13.6 while.115
  374.5 15.4 while.116
  389.9 12.7 all-gather.46.cloned.1.call-done
  402.6 13.7 while.113
  419.4 28.2 %while.114 = (s32[]{:T(128)}, f32[256,4,128]{2,0,1:T(8,128)}, s32[256]{0:T(256)S(1)}, s32[8,256]{1,0:T(8,128)S(1)}, s32[8,256]{1,0:T(8,128)S(1)}, /*index=5*/bf1...) while((s32[]{:T(128)}, f32[256,4,128]{2,0,1:T(8,128)}, ...), condition=%wide.region_19.20_spmd.clone, body=%wide.region_18.19_spmd.clone.sunk | while | flops 135991296 | bytes 1848459 | solution.py:80
  450.6 18.4 all-gather.6
  469.0 16.7 all-gather.5
  494.7 10.9 all-gather.54.cloned.1.call-done
  505.6 127.2 %all-gather.40.cloned.1.call-done = bf16[2048,2048]{1,0:T(8,128)(2,1)} async-done(((bf16[256,2048]{1,0:T(8,128)(2,1)}), bf16[2048,2048]{1,0:T(8,128)(2,1)}) %all-gather.40.cloned.1.call-update) | async-done | bytes 8388624 | tf_op jit(solution)/shard_map/all_gather | solution.py:145
  649.1 127.5 %all-gather.42.cloned.1.call-done = bf16[2048,2048]{1,0:T(8,128)(2,1)} async-done(((bf16[2048,256]{1,0:T(8,128)(2,1)}), bf16[2048,2048]{1,0:T(8,128)(2,1)}) %all-gather.42.cloned.1.call-update) | async-done | bytes 8388624 | tf_op jit(solution)/shard_map/all_gather | solution.py:146
  801.0 10.9 all-gather.64.cloned.1.call-done
  837.7 10.8 all-gather.62.cloned.1.call-done
  887.7 16.5 reduce-scatter.39.cloned.1.call-done
  904.2 27.6 %reduce-scatter.33.cloned.1.call-done = bf16[64,2048]{1,0:T(8,128)(2,1)} async-done(((bf16[256,2048]{1,0:T(8,128)(2,1)}), bf16[64,2048]{1,0:T(8,128)(2,1)}) %reduce-scatter.33.cloned.1.call-update) | async-done | bytes 262160 | tf_op jit(solution)/shard_map/reduce_scatter | solution.py:251
  935.4 23.7 %reduce-scatter.27.cloned.1.call-done = bf16[64,2048]{1,0:T(8,128)(2,1)} async-done(((bf16[256,2048]{1,0:T(8,128)(2,1)}), bf16[64,2048]{1,0:T(8,128)(2,1)}) %reduce-scatter.27.cloned.1.call-update) | async-done | bytes 262160 | tf_op jit(solution)/shard_map/reduce_scatter | solution.py:226
  959.2 27.6 %reduce-scatter.23.cloned.1.call-done = bf16[64,2048]{1,0:T(8,128)(2,1)} async-done(((bf16[256,2048]{1,0:T(8,128)(2,1)}), bf16[64,2048]{1,0:T(8,128)(2,1)}) %reduce-scatter.23.cloned.1.call-update) | async-done | bytes 262160 | tf_op jit(solution)/shard_map/reduce_scatter | solution.py:226
  989.5 24.6 %reduce-scatter.31.cloned.1.call-done = bf16[64,2048]{1,0:T(8,128)(2,1)} async-done(((bf16[256,2048]{1,0:T(8,128)(2,1)}), bf16[64,2048]{1,0:T(8,128)(2,1)}) %reduce-scatter.31.cloned.1.call-update) | async-done | bytes 262160 | tf_op jit(solution)/shard_map/reduce_scatter | solution.py:226
  1022.0 12.2 all-gather.56.cloned.1.call-done
  1038.9 45.6 %while.117 = (s32[]{:T(128)}, f32[256,4,128]{2,0,1:T(8,128)S(1)}, f32[8,256,256]{2,1,0:T(8,128)}, s32[256]{0:T(256)S(1)}, s32[8,256]{1,0:T(8,128)S(1)}, /*index=...) while((s32[]{:T(128)}, f32[256,4,128]{2,0,1:T(8,128)S(1)}, ...), condition=%wide.region_41.42_spmd.clone, body=%wide.region_40.41_spmd.clone.sunk | while | flops 338333696 | bytes 9258151 | solution.py:121
  1091.8 45.5 %while.118 = (s32[]{:T(128)}, f32[256,4,128]{2,0,1:T(8,128)S(1)}, f32[8,256,256]{2,1,0:T(8,128)}, s32[256]{0:T(256)S(1)}, s32[8,256]{1,0:T(8,128)S(1)}, /*index=...) while((s32[]{:T(128)}, f32[256,4,128]{2,0,1:T(8,128)S(1)}, ...), condition=%wide.region_51.52_spmd.clone, body=%wide.region_50.51_spmd.clone.sunk | while | flops 338333696 | bytes 9258151 | solution.py:121
  1145.0 30.4 %while.119 = (s32[]{:T(128)}, f32[256,4,128]{2,0,1:T(8,128)S(1)}, f32[8,256,256]{2,1,0:T(8,128)}, s32[256]{0:T(256)S(1)}, s32[8,256]{1,0:T(8,128)S(1)}, /*index=...) while((s32[]{:T(128)}, f32[256,4,128]{2,0,1:T(8,128)S(1)}, ...), condition=%wide.region_61.62_spmd.clone, body=%wide.region_60.61_spmd.clone.sunk | while | flops 338333696 | bytes 9258151 | solution.py:121
  1198.6 9.8 fusion.140
  1216.7 16.0 add_convert_fusion
  1251.6 15.7 add_convert_fusion.1
  1270.9 91.4 %reduce-scatter.43.cloned.1.call-done = f32[64,256]{1,0:T(8,128)} async-done(((f32[2048,256]{1,0:T(8,128)}), f32[64,256]{1,0:T(8,128)}) %reduce-scatter.43.cloned.1.call-update) | async-done | bytes 65552 | tf_op jit(solution)/shard_map/reduce_scatter | solution.py:284
  1364.4 133.0 %reduce-scatter.49.cloned.1.call-done = f32[64,256]{1,0:T(8,128)} async-done(((f32[2048,256]{1,0:T(8,128)}), f32[64,256]{1,0:T(8,128)}) %reduce-scatter.49.cloned.1.call-update) | async-done | bytes 65552 | tf_op jit(solution)/shard_map/reduce_scatter | solution.py:284
  1502.2 19.0 reduce-scatter.47.cloned.1.call-done
  1522.5 26.2 %reduce-scatter.41.cloned.1.call-done = bf16[64,2048]{1,0:T(8,128)(2,1)} async-done(((bf16[256,2048]{1,0:T(8,128)(2,1)}), bf16[64,2048]{1,0:T(8,128)(2,1)}) %reduce-scatter.41.cloned.1.call-update) | async-done | bytes 262160 | tf_op jit(solution)/shard_map/reduce_scatter | solution.py:294
  1551.2 25.1 %reduce-scatter.35.cloned.1.call-done = bf16[64,2048]{1,0:T(8,128)(2,1)} async-done(((bf16[256,2048]{1,0:T(8,128)(2,1)}), bf16[64,2048]{1,0:T(8,128)(2,1)}) %reduce-scatter.35.cloned.1.call-update) | async-done | bytes 262160 | tf_op jit(solution)/shard_map/reduce_scatter | solution.py:294
  1580.1 40.2 %all-reduce.4 = (f32[2048]{0:T(1024)S(1)}, f32[2048]{0:T(1024)S(1)}, f32[2048]{0:T(1024)S(1)}, f32[2048]{0:T(1024)S(1)}) all-reduce(f32[2048]{0:T(1024)S(1)} %add_add_fusion.9, f32[2048]{0:T(1024)S(1)} %add_add_fusion.8, f32[2048]{0:T(1024)S(1)} %add_add_fusion.7, ...), channel_id=20, replica_groups=mesh['dp'=8,'tensor'=4] {'dp','tensor'}, use_global_device_ids=true, to_apply=%region_69.70.clone | all-reduce | flops 8192 | bytes 65536
  1622.7 25.2 %reduce-scatter.51.cloned.1.call-done = bf16[256,512]{1,0:T(8,128)(2,1)} async-done(((bf16[2048,512]{1,0:T(8,128)(2,1)}), bf16[256,512]{1,0:T(8,128)(2,1)}) %reduce-scatter.51.cloned.1.call-update) | async-done | bytes 262160 | tf_op jit(solution)/shard_map/reduce_scatter | solution.py:310
  1649.7 69.1 %reduce-scatter.55.cloned.1.call-done = bf16[512,256]{1,0:T(8,128)(2,1)} async-done(((bf16[512,2048]{1,0:T(8,128)(2,1)}), bf16[512,256]{1,0:T(8,128)(2,1)}) %reduce-scatter.55.cloned.1.call-update) | async-done | bytes 262160 | tf_op jit(solution)/shard_map/reduce_scatter | solution.py:313
  1723.6 147.8 %reduce-scatter.59.cloned.1.call-done = bf16[2048,256]{1,0:T(8,128)(2,1)} async-done(((bf16[2048,2048]{1,0:T(8,128)(2,1)}), bf16[2048,256]{1,0:T(8,128)(2,1)}) %reduce-scatter.59.cloned.1.call-update) | async-done | bytes 1048592 | tf_op jit(solution)/shard_map/reduce_scatter | solution.py:319
  1874.1 148.9 %reduce-scatter.57.cloned.1.call-done = bf16[256,2048]{1,0:T(8,128)(2,1)} async-done(((bf16[2048,2048]{1,0:T(8,128)(2,1)}), bf16[256,2048]{1,0:T(8,128)(2,1)}) %reduce-scatter.57.cloned.1.call-update) | async-done | bytes 1048592 | tf_op jit(solution)/shard_map/reduce_scatter | solution.py:316
  2025.7 135.9 %reduce-scatter.53.cloned.1.call-done = f32[64,256]{1,0:T(8,128)} async-done(((f32[2048,256]{1,0:T(8,128)}), f32[64,256]{1,0:T(8,128)}) %reduce-scatter.53.cloned.1.call-update) | async-done | bytes 65552 | tf_op jit(solution)/shard_map/reduce_scatter | solution.py:324
  (1043 shorter events, 483.4 us)
Async XLA Ops:
  7.2 60.0 %all-gather.28.cloned.1.call-start = ((), (), s32[]{:S(2)}) async-start(), calls=%async_computation.20 | async-start | bytes 1310720 | tf_op jit(solution)/shard_map/all_gather | solution.py:195
  9.9 103.0 %copy-start.69 = (s32[3,2048]{1,0:T(4,128)S(1)}, s32[3,2048]{1,0:T(4,128)}, u32[]{:S(2)}) copy-start(s32[3,2048]{1,0:T(4,128)} %param.32) | copy-start | bytes 73732
  9.9 102.9 %copy-start.74 = (f32[64]{0:T(128)}, f32[64]{0:T(128)S(1)}, u32[]{:S(2)}) copy-start(f32[64]{0:T(128)S(1)} %broadcast_multiply_fusion.5) | copy-start | bytes 772
  11.1 150.9 %copy-start.82 = (f32[64]{0:T(128)}, f32[64]{0:T(128)S(1)}, u32[]{:S(2)}) copy-start(f32[64]{0:T(128)S(1)} %fusion.188) | copy-start | bytes 772
  11.1 101.7 %copy-start.76 = (f32[64]{0:T(128)}, f32[64]{0:T(128)S(1)}, u32[]{:S(2)}) copy-start(f32[64]{0:T(128)S(1)} %fusion.219) | copy-start | bytes 772
  49.7 231.6 %copy-start.64 = (f32[8,1,256]{2,1,0:T(1,128)}, f32[8,1,256]{2,1,0:T(1,128)S(1)}, u32[]{:S(2)}) copy-start(f32[8,1,256]{2,1,0:T(1,128)S(1)} %convert_element_type.374) | copy-start | bytes 24580
  51.5 57.9 %all-gather.30.cloned.1.call-start = ((), (), s32[]{:S(2)}) async-start(), calls=%async_computation.21 | async-start | bytes 1179648 | tf_op jit(solution)/shard_map/all_gather | solution.py:143
  52.3 107.4 %all-gather.34.cloned.1.call-start = ((), (), s32[]{:S(2)}) async-start(), calls=%async_computation.23 | async-start | bytes 2359296 | tf_op jit(solution)/shard_map/all_gather | solution.py:142
  53.0 147.9 %all-gather.32.cloned.1.call-start = ((), (), s32[]{:S(2)}) async-start(), calls=%async_computation.22 | async-start | bytes 1179648 | tf_op jit(solution)/shard_map/all_gather | solution.py:204
  112.1 140.5 %all-gather.36.cloned.1.call-start = ((), (), s32[]{:S(2)}) async-start(), calls=%async_computation.24 | async-start | bytes 2359296 | tf_op jit(solution)/shard_map/all_gather | solution.py:144
  112.7 166.6 %reduce-scatter.21.cloned.1.call-start = ((), (), s32[]{:S(2)}) async-start(), calls=%async_computation.25 | async-start | bytes 1310720 | tf_op jit(solution)/shard_map/reduce_scatter | solution.py:209
  256.1 43.2 %all-gather.50.cloned.1.call-start = ((), (), s32[]{:S(2)}) async-start(), calls=%async_computation.35 | async-start | bytes 1310720 | tf_op jit(solution)/shard_map/all_gather | solution.py:195
  282.5 35.3 %all-gather.44.cloned.1.call-start = ((), (), s32[]{:S(2)}) async-start(), calls=%async_computation.30 | async-start | bytes 1310720 | tf_op jit(solution)/shard_map/all_gather | solution.py:195
  283.2 77.6 %all-gather.52.cloned.1.call-start = ((), (), s32[]{:S(2)}) async-start(), calls=%async_computation.36 | async-start | bytes 1179648 | tf_op jit(solution)/shard_map/all_gather | solution.py:204
  301.8 100.8 %all-gather.46.cloned.1.call-start = ((), (), s32[]{:S(2)}) async-start(), calls=%async_computation.31 | async-start | bytes 1179648 | tf_op jit(solution)/shard_map/all_gather | solution.py:204
  321.6 164.2 %reduce-scatter.29.cloned.1.call-start = ((), (), s32[]{:S(2)}) async-start(), calls=%async_computation.37 | async-start | bytes 1310720 | tf_op jit(solution)/shard_map/reduce_scatter | solution.py:209
  419.3 66.5 %reduce-scatter.25.cloned.1.call-start = ((), (), s32[]{:S(2)}) async-start(), calls=%async_computation.32 | async-start | bytes 1310720 | tf_op jit(solution)/shard_map/reduce_scatter | solution.py:209
  450.5 55.0 %all-gather.54.cloned.1.call-start = ((), (), s32[]{:S(2)}) async-start(), calls=%async_computation.38 | async-start | bytes 1310720 | tf_op jit(solution)/shard_map/all_gather | solution.py:220
  490.0 142.7 %all-gather.40.cloned.1.call-start = ((), (), s32[]{:S(2)}) async-start(), calls=%async_computation.27 | async-start | bytes 9437184 | tf_op jit(solution)/shard_map/all_gather | solution.py:145
  490.6 158.6 %all-gather.66.cloned.1.call-start = ((), (), s32[]{:S(2)}) async-start(), calls=%async_computation.59 | async-start | bytes 1310720 | tf_op jit(solution)/shard_map/all_gather | solution.py:221
  491.5 285.1 %all-gather.42.cloned.1.call-start = ((), (), s32[]{:S(2)}) async-start(), calls=%async_computation.28 | async-start | bytes 9437184 | tf_op jit(solution)/shard_map/all_gather | solution.py:146
  492.1 301.6 %all-gather.48.cloned.1.call-start = ((), (), s32[]{:S(2)}) async-start(), calls=%async_computation.33 | async-start | bytes 1310720 | tf_op jit(solution)/shard_map/all_gather | solution.py:220
  492.7 319.2 %all-gather.64.cloned.1.call-start = ((), (), s32[]{:S(2)}) async-start(), calls=%async_computation.58 | async-start | bytes 1310720 | tf_op jit(solution)/shard_map/all_gather | solution.py:221
  493.3 337.0 %all-gather.38.cloned.1.call-start = ((), (), s32[]{:S(2)}) async-start(), calls=%async_computation.26 | async-start | bytes 1310720 | tf_op jit(solution)/shard_map/all_gather | solution.py:220
  494.0 354.5 %all-gather.62.cloned.1.call-start = ((), (), s32[]{:S(2)}) async-start(), calls=%async_computation.57 | async-start | bytes 1310720 | tf_op jit(solution)/shard_map/all_gather | solution.py:221
  494.6 393.1 %reduce-scatter.45.cloned.1.call-start = ((), (), s32[]{:S(2)}) async-start(), calls=%async_computation.48 | async-start | bytes 1310720 | tf_op jit(solution)/shard_map/reduce_scatter | solution.py:251
  788.8 115.4 %reduce-scatter.39.cloned.1.call-start = ((), (), s32[]{:S(2)}) async-start(), calls=%async_computation.44 | async-start | bytes 1310720 | tf_op jit(solution)/shard_map/reduce_scatter | solution.py:251
  827.4 104.4 %reduce-scatter.33.cloned.1.call-start = ((), (), s32[]{:S(2)}) async-start(), calls=%async_computation.40 | async-start | bytes 1310720 | tf_op jit(solution)/shard_map/reduce_scatter | solution.py:251
  864.3 94.8 %reduce-scatter.27.cloned.1.call-start = ((), (), s32[]{:S(2)}) async-start(), calls=%async_computation.34 | async-start | bytes 1310720 | tf_op jit(solution)/shard_map/reduce_scatter | solution.py:226
  872.0 114.8 %reduce-scatter.23.cloned.1.call-start = ((), (), s32[]{:S(2)}) async-start(), calls=%async_computation.29 | async-start | bytes 1310720 | tf_op jit(solution)/shard_map/reduce_scatter | solution.py:226
  879.7 134.4 %reduce-scatter.31.cloned.1.call-start = ((), (), s32[]{:S(2)}) async-start(), calls=%async_computation.39 | async-start | bytes 1310720 | tf_op jit(solution)/shard_map/reduce_scatter | solution.py:226
  887.6 146.7 %all-gather.56.cloned.1.call-start = ((), (), s32[]{:S(2)}) async-start(), calls=%async_computation.41 | async-start | bytes 1310720 | tf_op jit(solution)/shard_map/all_gather | solution.py:263
  1017.4 67.1 %all-gather.58.cloned.1.call-start = ((), (), s32[]{:S(2)}) async-start(), calls=%async_computation.45 | async-start | bytes 1310720 | tf_op jit(solution)/shard_map/all_gather | solution.py:263
  1018.2 119.1 %all-gather.60.cloned.1.call-start = ((), (), s32[]{:S(2)}) async-start(), calls=%async_computation.49 | async-start | bytes 1310720 | tf_op jit(solution)/shard_map/all_gather | solution.py:263
  1022.0 245.6 %reduce-scatter.37.cloned.1.call-start = ((), (), s32[]{:S(2)}) async-start(), calls=%async_computation.43 | async-start | bytes 2162688 | tf_op jit(solution)/shard_map/reduce_scatter | solution.py:284
  1090.2 272.1 %reduce-scatter.43.cloned.1.call-start = ((), (), s32[]{:S(2)}) async-start(), calls=%async_computation.47 | async-start | bytes 2162688 | tf_op jit(solution)/shard_map/reduce_scatter | solution.py:284
  1143.0 354.4 %reduce-scatter.49.cloned.1.call-start = ((), (), s32[]{:S(2)}) async-start(), calls=%async_computation.51 | async-start | bytes 2162688 | tf_op jit(solution)/shard_map/reduce_scatter | solution.py:284
  1175.4 345.7 %reduce-scatter.47.cloned.1.call-start = ((), (), s32[]{:S(2)}) async-start(), calls=%async_computation.50 | async-start | bytes 1310720 | tf_op jit(solution)/shard_map/reduce_scatter | solution.py:294
  1178.9 369.8 %reduce-scatter.41.cloned.1.call-start = ((), (), s32[]{:S(2)}) async-start(), calls=%async_computation.46 | async-start | bytes 1310720 | tf_op jit(solution)/shard_map/reduce_scatter | solution.py:294
  1182.6 393.6 %reduce-scatter.35.cloned.1.call-start = ((), (), s32[]{:S(2)}) async-start(), calls=%async_computation.42 | async-start | bytes 1310720 | tf_op jit(solution)/shard_map/reduce_scatter | solution.py:294
  1186.3 461.5 %reduce-scatter.51.cloned.1.call-start = ((), (), s32[]{:S(2)}) async-start(), calls=%async_computation.52 | async-start | bytes 2359296 | tf_op jit(solution)/shard_map/reduce_scatter | solution.py:310
  1191.6 527.1 %reduce-scatter.55.cloned.1.call-start = ((), (), s32[]{:S(2)}) async-start(), calls=%async_computation.54 | async-start | bytes 2359296 | tf_op jit(solution)/shard_map/reduce_scatter | solution.py:313
  1197.0 674.4 %reduce-scatter.59.cloned.1.call-start = ((), (), s32[]{:S(2)}) async-start(), calls=%async_computation.56 | async-start | bytes 9437184 | tf_op jit(solution)/shard_map/reduce_scatter | solution.py:319
  1232.8 790.2 %reduce-scatter.57.cloned.1.call-start = ((), (), s32[]{:S(2)}) async-start(), calls=%async_computation.55 | async-start | bytes 9437184 | tf_op jit(solution)/shard_map/reduce_scatter | solution.py:316
  1267.4 894.3 %reduce-scatter.53.cloned.1.call-start = ((), (), s32[]{:S(2)}) async-start(), calls=%async_computation.53 | async-start | bytes 2162688 | tf_op jit(solution)/shard_map/reduce_scatter | solution.py:324
  1270.9 226.5 %copy-start.26 = (bf16[64,2048]{1,0:T(8,128)(2,1)S(1)}, bf16[64,2048]{1,0:T(8,128)(2,1)}, u32[]{:S(2)}) copy-start(bf16[64,2048]{1,0:T(8,128)(2,1)} %get-tuple-element.1304) | copy-start | bytes 786436
  1578.5 142.0 %copy-start.16 = (f32[64,2048]{1,0:T(8,128)S(1)}, f32[64,2048]{1,0:T(8,128)}, u32[]{:S(2)}) copy-start(f32[64,2048]{1,0:T(8,128)} %copy-done.15) | copy-start | bytes 1572868
  1578.5 142.0 %copy-start.18 = (f32[64,2048]{1,0:T(8,128)S(1)}, f32[64,2048]{1,0:T(8,128)}, u32[]{:S(2)}) copy-start(f32[64,2048]{1,0:T(8,128)} %get-tuple-element.1308) | copy-start | bytes 1572868
  (84 other events, 1606.0 us)
Sparse Core Ops, SparseCore 0:
  51.7 15.4 all-gather.27
  69.3 40.1 all-gather.29
  111.6 48.0 all-gather.33
  162.2 38.6 all-gather.31
  202.8 49.8 all-gather.35
  256.2 23.0 reduce-scatter.20
  282.6 16.7 all-gather.49
  301.0 16.7 all-gather.43
  320.6 40.1 all-gather.51
  363.6 38.9 all-gather.45
  419.4 23.6 reduce-scatter.28
  450.6 23.6 reduce-scatter.24
  490.1 15.4 all-gather.53
  507.8 124.9 all-gather.39
  634.2 14.9 all-gather.65
  651.2 125.3 all-gather.41
  778.7 14.9 all-gather.47
  795.2 16.7 all-gather.63
  813.6 16.7 all-gather.37
  831.8 16.7 all-gather.61
  851.8 24.8 reduce-scatter.44
  879.3 24.8 reduce-scatter.38
  906.9 24.8 reduce-scatter.32
  934.2 24.8 reduce-scatter.26
  961.8 24.8 reduce-scatter.22
  989.2 24.9 reduce-scatter.30
  1017.5 16.6 all-gather.55
  1035.9 16.7 all-gather.57
  1054.3 16.7 all-gather.59
  1090.3 137.0 reduce-scatter.36
  1229.6 132.6 reduce-scatter.42
  1364.7 132.6 reduce-scatter.48
  1500.3 20.7 reduce-scatter.46
  1523.8 24.8 reduce-scatter.40
  1551.3 24.9 reduce-scatter.34
  1580.0 67.8 reduce-scatter.50
  1651.7 67.0 reduce-scatter.54
  1722.8 148.5 reduce-scatter.58
  1874.9 148.0 reduce-scatter.56
  2025.9 135.7 reduce-scatter.52
where the time goes:
time: 2180 us; the launch traced here: 2170 us
  waiting for transfers between devices  1530 us (70%)
  matrix products  327 us (15%)
  local copies, waits for them, and re-layouts  117 us (5%)
  blocking collectives  114 us (5%)
  other arithmetic  54.4 us (2%)
    reduce_scatter x3, waiting for transfers between devices, local(): lax.psum_scatter(grad_kv_rows, ('dp', 'tensor'), scatter_dimension=0, til...  224 us
    reduce_scatter x1, waiting for transfers between devices, local(): lax.psum_scatter(acc_expand.astype(jnp.bfloat16), 'dp', scatter_dimension...  149 us
    reduce_scatter x1, waiting for transfers between devices, local(): lax.psum_scatter(acc_reduce.astype(jnp.bfloat16), 'dp', scatter_dimension...  148 us
    reduce_scatter x1, waiting for transfers between devices, local(): lax.psum_scatter(acc_keyval, ('dp', 'tensor'), scatter_dimension=0, tiled...  136 us
    all_gather x1, waiting for transfers between devices, fetch(): lax.all_gather(w_reduce, 'dp', axis=1, tiled=True)  128 us
    all_gather x1, waiting for transfers between devices, fetch(): lax.all_gather(w_expand, 'dp', axis=0, tiled=True)  127 us
    all_gather x3, waiting for transfers between devices, local(): keys_vals = lax.all_gather(kv_group, 'dp', axis=0, tiled=True)  90.7 us
    reduce_scatter x3, waiting for transfers between devices, local(): lax.psum_scatter(jnp.dot(active, wred_full, preferred_element_type=jnp.fl...  76 us
  transfers between devices with their start and end apart: 40, of which 34 were waited for; matrix products, arithmetic and copies ran while one was open for 21% of the time, Pallas kernels for 0%

commit v1 on v0

v1 whole, which is shorter than its diff:
```python
import functools
import math

import jax
import jax.numpy as jnp
from jax import lax
from jax.experimental import pallas as pl
from jax.experimental.pallas import tpu as pltpu
from jax.sharding import PartitionSpec as P

BLOCK = 256
EPSILON = 1e-05
NEG_FILL = -1e30
MESH = pl.DeviceIdType.MESH
ANY = pl.BlockSpec(memory_space=pl.ANY)
BF16 = jnp.bfloat16
F32 = jnp.float32


def layer_norm(values, gain, shift):
    center = jnp.mean(values, axis=-1, keepdims=True)
    centered = values - center
    variance = jnp.mean(centered * centered, axis=-1, keepdims=True)
    return centered * lax.rsqrt(variance + EPSILON) * gain + shift


def gelu_tanh(values):
    return jax.nn.gelu(values, approximate=True)


class Net:
    def __init__(self, nz, ny, send, recv, local):
        dp, tensor = lax.axis_index("dp"), lax.axis_index("tensor")
        self.nz, self.ny = nz, ny
        self.z, self.x = lax.div(dp, 2), lax.rem(dp, 2)
        self.y, self.c = lax.div(tensor, 2), lax.rem(tensor, 2)
        self.tensor = tensor
        self.send, self.recv, self.local = send, recv, local
        self.used = [0, 0]
        self.keys = {}

    def flip(self, value, by):
        return value + by - 2 * by * value if by else value

    def xy(self, dx, dy):
        return self.flip(self.x, dx), lax.rem(self.y + dy, self.ny) if dy else self.y

    def rank(self, dx=0, dy=0, dc=0):
        x, y = self.xy(dx, dy)
        return x * (2 * self.ny) + y * 2 + self.flip(self.c, dc)

    def device(self, dx=0, dy=0, dc=0, z=None):
        x, y = self.xy(dx, dy)
        return ((self.z if z is None else z) * 2 + x, y * 2 + self.flip(self.c, dc))

    def slot(self, key):
        if key not in self.keys:
            self.keys[key] = self.used[0]
            self.used[0] += 1
        return self.keys[key]

    def remote(self, key, src, dst, device):
        at = self.slot(key)
        return pltpu.make_async_remote_copy(
            src_ref=src,
            dst_ref=dst,
            send_sem=self.send.at[at],
            recv_sem=self.recv.at[at],
            device_id=device,
            device_id_type=MESH,
        )

    def copy(self, src, dst):
        at = self.used[1]
        self.used[1] += 1
        return pltpu.make_async_copy(src, dst, self.local.at[at])


def add_rows(dst, terms, rows=16):
    lead, height, _ = dst.shape
    rows = min(rows, height)
    steps = height // rows

    def body(step, carry):
        at, off = lax.div(step, steps), pl.multiple_of(lax.rem(step, steps) * rows, rows)
        total = terms[0][at, pl.ds(off, rows), :].astype(F32)
        for term in terms[1:]:
            total = total + term[at, pl.ds(off, rows), :].astype(F32)
        dst[at, pl.ds(off, rows), :] = total.astype(dst.dtype)
        return carry

    lax.fori_loop(0, lead * steps, body, 0)


class FaceGather:
    moves = ("x", "y", "c")

    def __init__(self, own, nz, ny):
        self.ins = [own]
        m, t, d = own.shape
        self.outs = [(jax.ShapeDtypeStruct((m, 4 * ny * t, d), own.dtype), ANY)]
        self.scratch = []
        self.half = t // 2
        self.remotes, self.locals = 8 * ny, 1

    def run(self, net, ins, outs, scratch):
        (own,), (out,), half = ins, outs, self.half
        dys = range(1, net.ny)

        def piece(dx, dy, h):
            return out.at[:, pl.ds(pl.multiple_of(net.rank(dx, dy) * 2 * half + h * half, half), half), :]

        mine = [own.at[:, pl.ds(h * half, half), :] for h in (0, 1)]
        keep = net.copy(own, out.at[:, pl.ds(pl.multiple_of(net.rank() * 2 * half, half), 2 * half), :])
        keep.start()
        sent = {}

        def send(key, src, dst, device):
            sent[key] = net.remote((id(self), key), src, dst, device)
            sent[key].start()

        send(("x", 0), mine[0], piece(0, 0, 0), net.device(1, 0))
        for dy in dys:
            send(("y", dy, 1), mine[1], piece(0, 0, 1), net.device(0, dy))
        send(("x", 1), mine[1], piece(0, 0, 1), net.device(1, 0))
        for dy in dys:
            send(("y", dy, 0), mine[0], piece(0, 0, 0), net.device(0, dy))
        for h in (0, 1):
            send(("c", h), mine[h], piece(0, 0, h), net.device(0, 0, 1))

        def share(key, dx, dy, h):
            send(("c",) + key, piece(dx, dy, h), piece(dx, dy, h), net.device(0, 0, 1))

        yield
        sent["x", 0].wait_recv()
        for dy in dys:
            send(("xy", dy), piece(1, 0, 0), piece(1, 0, 0), net.device(0, dy))
        share(("x", 0), 1, 0, 0)
        for dy in dys:
            yield
            sent["y", dy, 1].wait_recv()
            send(("yx", dy), piece(0, -dy % net.ny, 1), piece(0, -dy % net.ny, 1), net.device(1, 0))
            share(("y", dy, 1), 0, -dy % net.ny, 1)
        yield
        sent["x", 1].wait_recv()
        share(("x", 1), 1, 0, 1)
        for dy in dys:
            yield
            sent["y", dy, 0].wait_recv()
            share(("y", dy, 0), 0, -dy % net.ny, 0)
        for dy in dys:
            yield
            sent["xy", dy].wait_recv()
            share(("xy", dy), 1, -dy % net.ny, 0)
            yield
            sent["yx", dy].wait_recv()
            share(("yx", dy), 1, -dy % net.ny, 1)
        yield
        for key, copy in sent.items():
            if key[0] == "c":
                copy.wait_recv()
        for copy in sent.values():
            copy.wait_send()
        keep.wait()


class FaceScatter:
    moves = ("x", "y", "c")

    def __init__(self, part, nz, ny, dtype=F32):
        self.ins = [part]
        m, rows, d = part.shape
        t = rows // (4 * ny)
        self.outs = [(jax.ShapeDtypeStruct((m, t, d), dtype), pl.BlockSpec(memory_space=pltpu.VMEM))]
        half = t // 2
        self.half = half
        self.scratch = [
            pltpu.VMEM((2 * ny, m, t, d), BF16),
            pltpu.VMEM((2 * ny, m, t, d), BF16),
            pltpu.VMEM((ny, m, half, d), BF16),
            pltpu.VMEM((ny, m, half, d), BF16),
            pltpu.VMEM((2, m, half, d), BF16),
            pltpu.VMEM((2, ny, m, half, d), BF16),
        ]
        self.remotes, self.locals = 6 * ny + 4, 2 * ny

    def run(self, net, ins, outs, scratch):
        (part,), (out,), half = ins, outs, self.half
        work, from_core, x_diag, y_diag, x_in, y_in = scratch
        ny = net.ny
        dys = range(1, ny)
        order = [(1, dy) for dy in dys] + [(1, 0)] + [(0, dy) for dy in dys] + [(0, 0)]
        sent, loads = {}, {}

        def send(key, src, dst, device):
            sent[key] = net.remote((id(self), key), src, dst, device)
            sent[key].start()

        def rows(dx, dy, dc):
            return part.at[:, pl.ds(pl.multiple_of(net.rank(dx, dy, dc) * 2 * half, half), 2 * half), :]

        for dx, dy in order:
            at = dx * ny + dy
            loads[at] = net.copy(rows(dx, dy, 0), work.at[at])
            loads[at].start()
            send(("c", at), rows(dx, dy, 1), from_core.at[at], net.device(0, 0, 1))
        for dx, dy in order:
            at = dx * ny + dy
            yield
            loads[at].wait()
            sent["c", at].wait_recv()
            add_rows(work.at[at], [work.at[at], from_core.at[at]])
            top, low = work.at[at, :, pl.ds(0, half), :], work.at[at, :, pl.ds(half, half), :]
            if dx and dy:
                send(("xd", dy), top, x_diag.at[dy], net.device(1, 0))
                send(("yd", dy), low, y_diag.at[dy], net.device(0, dy))
            elif dx:
                send(("x", 0), top, x_in.at[0], net.device(1, 0))
            elif dy:
                send(("y", dy, 1), low, y_in.at[1, dy], net.device(0, dy))
        for dy in dys:
            yield
            sent["xd", dy].wait_recv()
            top = work.at[dy, :, pl.ds(0, half), :]
            add_rows(top, [top, x_diag.at[dy]])
            send(("y", dy, 0), top, y_in.at[0, dy], net.device(0, dy))
        low = work.at[ny, :, pl.ds(half, half), :]
        for dy in dys:
            yield
            sent["yd", dy].wait_recv()
            add_rows(low, [low, y_diag.at[dy]])
        send(("x", 1), low, x_in.at[1], net.device(1, 0))
        for h in (0, 1):
            yield
            sent["x", h].wait_recv()
            for dy in dys:
                sent["y", dy, h].wait_recv()
            side = pl.ds(h * half, half)
            add_rows(
                out.at[:, side, :],
                [work.at[0, :, side, :], x_in.at[h]] + [y_in.at[h, dy] for dy in dys],
            )
        for copy in sent.values():
            copy.wait_send()


class LineGather:
    moves = ("x", "line", "c")

    def __init__(self, shards, kinds, nz, ny):
        self.ins, self.kinds = list(shards), list(kinds)
        self.outs, self.scratch = [], []
        for shard, kind in zip(shards, kinds):
            rows, columns = shard.shape
            if kind == "row":
                shape = (rows * 2 * nz, columns // 2)
            elif kind == "col":
                shape = (rows // 2, columns * 2 * nz)
            else:
                shape = (rows * 2 * nz, columns)
            self.outs.append((jax.ShapeDtypeStruct(shape, shard.dtype), ANY))
        count = len(self.ins)
        self.remotes = count * (1 + 4 * (nz - 1)) + kinds.count("both") * (1 + 4 * (nz - 1))
        self.locals = count

    def run(self, net, ins, outs, scratch):
        nz, z = net.nz, net.z
        sent, locals_, shared = [], [], []
        weights = []
        for at, (shard, out, kind) in enumerate(zip(ins, outs, self.kinds)):
            rows, columns = shard.shape

            if kind == "row":
                half = columns // 2

                def mine(dx, shard=shard, half=half):
                    return shard.at[:, pl.ds(pl.multiple_of(net.flip(net.x, dx) * half, half), half)]

                def block(line, dx, out=out, rows=rows):
                    first = (line * 2 + net.flip(net.x, dx)) * rows
                    return out.at[pl.ds(pl.multiple_of(first, rows), rows), :]

            elif kind == "col":
                half = rows // 2

                def mine(dx, shard=shard, half=half):
                    return shard.at[pl.ds(pl.multiple_of(net.flip(net.x, dx) * half, half), half), :]

                def block(line, dx, out=out, columns=columns):
                    first = (line * 2 + net.flip(net.x, dx)) * columns
                    return out.at[:, pl.ds(pl.multiple_of(first, columns), columns)]

            else:
                half = rows // 2

                def mine(dx, shard=shard, half=half):
                    return shard.at[pl.ds(pl.multiple_of(net.c * half, half), half), :]

                def block(line, dx, out=out, rows=rows, half=half):
                    first = (line * 2 + net.flip(net.x, dx)) * rows + net.c * half
                    return out.at[pl.ds(pl.multiple_of(first, half), half), :]

            weights.append((at, kind, mine, block))

        def hop(at, dx, step, up, block, src=None):
            origin = z - (step - 1) if up else z + (step - 1)
            there = z + 1 if up else z - 1
            copy = net.remote(
                (id(self), at, dx, step, up),
                block(origin, dx) if src is None else src,
                block(origin, dx),
                net.device(z=there),
            )
            fits = (origin >= 0) & (there < nz) if up else (origin < nz) & (there >= 0)
            return copy, fits

        def start(at, dx, step, up, block, src=None):
            copy, fits = hop(at, dx, step, up, block, src)
            pl.when(fits)(copy.start)
            sent.append((copy, fits))

        def arrived(at, dx, step, up, block, kind):
            copy, _ = hop(at, dx, step, up, block)
            origin = z - step if up else z + step
            fits = origin >= 0 if up else origin < nz
            pl.when(fits)(copy.wait_recv)
            if kind == "both":
                share = net.remote(
                    (id(self), "c", at, dx, step, up), block(origin, dx), block(origin, dx), net.device(0, 0, 1)
                )
                pl.when(fits)(share.start)
                shared.append((share, fits))

        swaps = {}
        for at, kind, mine, block in weights:
            swaps[at] = net.remote((id(self), at, "x"), mine(1), block(z, 0), net.device(1, 0))
            swaps[at].start()
            for up in (True, False):
                start(at, 0, 1, up, block, mine(0))
        for at, kind, mine, block in weights:
            if kind == "both":
                whole = ins[at].shape[0]
                into = outs[at].at[pl.ds(pl.multiple_of((z * 2 + net.x) * whole, whole), whole), :]
                locals_.append(net.copy(ins[at], into))
            else:
                locals_.append(net.copy(mine(0), block(z, 0)))
            locals_[-1].start()
        for at, kind, mine, block in weights:
            yield
            swaps[at].wait_recv()
            for up in (True, False):
                start(at, 1, 1, up, block)
            if kind == "both":
                share = net.remote((id(self), "c", at), block(z, 1), block(z, 1), net.device(0, 0, 1))
                share.start()
                shared.append((share, None))
        for step in range(1, nz):
            for at, kind, mine, block in weights:
                for dx in (0, 1):
                    yield
                    for up in (True, False):
                        arrived(at, dx, step, up, block, kind)
                        if step < nz - 1:
                            start(at, dx, step + 1, up, block)
        yield
        for copy, fits in shared:
            if fits is None:
                copy.wait()
            else:
                pl.when(fits)(copy.wait)
        for copy, fits in sent:
            pl.when(fits)(copy.wait_send)
        for copy in swaps.values():
            copy.wait_send()
        for copy in locals_:
            copy.wait()


class LineScatter:
    moves = ("x", "line")

    def __init__(self, parts, kinds, nz, ny):
        self.ins, self.kinds = list(parts), list(kinds)
        self.outs, self.scratch = [], []
        for part, kind in zip(parts, kinds):
            rows, columns = part.shape
            shape = (rows // (2 * nz), columns) if kind == "row" else (rows, columns // (2 * nz))
            self.outs.append((jax.ShapeDtypeStruct((2,) + shape, BF16), ANY))
            for lead in (nz, nz, nz, 1):
                self.scratch.append(pltpu.VMEM((lead, 2) + shape, BF16))
        count = len(self.ins)
        self.remotes = count * (1 + 4 * (nz - 1))
        self.locals = count * (2 * nz + 1)

    def run(self, net, ins, outs, scratch):
        nz, z = net.nz, net.z
        sent, loads, stores = [], {}, []
        grads = []
        for at, (part, out, kind) in enumerate(zip(ins, outs, self.kinds)):
            work, down, up, mine = scratch[4 * at : 4 * at + 4]
            _, _, rows, columns = work.shape

            def block(line, dx, part=part, kind=kind, rows=rows, columns=columns):
                size = rows if kind == "row" else columns
                first = pl.ds(pl.multiple_of((line * 2 + net.flip(net.x, dx)) * size, size), size)
                return part.at[first, :] if kind == "row" else part.at[:, first]

            grads.append((at, out, work, down, up, mine))
            order = []
            for k in range(nz):
                order += [k, nz - 1 - k]
            for line in dict.fromkeys(order):
                for dx in (1, 0):
                    loads[at, line, dx] = net.copy(block(line, dx), work.at[line, dx])
                    loads[at, line, dx].start()

        for k in range(nz - 1):
            for dx in (1, 0):
                for at, out, work, down, up, mine in grads:
                    yield
                    for line, slots, toward in ((k, down, -1), (nz - 1 - k, up, 1)):
                        here, inbox = work.at[line, dx], slots.at[line, dx]
                        copy = net.remote(
                            (id(self), at, line, dx, toward), here, inbox, net.device(z=z + toward)
                        )
                        first = z == (nz - 1 if toward < 0 else 0)
                        sends = z > line if toward < 0 else z < line

                        def step(copy=copy, here=here, inbox=inbox, first=first, load=loads[at, line, dx]):
                            load.wait()

                            @pl.when(jnp.logical_not(first))
                            def _():
                                copy.wait_recv()
                                add_rows(_lead(here), [_lead(here), _lead(inbox)])

                            copy.start()

                        pl.when(sends)(step)
                        sent.append((copy, sends))
        swaps = []
        for dx in (1, 0):
            for at, out, work, down, up, mine in grads:
                yield
                total = mine.at[0, dx]
                for line in range(nz):

                    @pl.when(z == line)
                    def _(line=line, at=at, total=total, work=work, down=down, up=up):
                        loads[at, line, dx].wait()
                        terms = [_lead(work.at[line, dx])]
                        if line < nz - 1:
                            net.remote(
                                (id(self), at, line, dx, -1), total, down.at[line, dx], net.device(z=z - 1)
                            ).wait_recv()
                            terms.append(_lead(down.at[line, dx]))
                        if line > 0:
                            net.remote(
                                (id(self), at, line, dx, 1), total, up.at[line, dx], net.device(z=z + 1)
                            ).wait_recv()
                            terms.append(_lead(up.at[line, dx]))
                        add_rows(_lead(total), terms)

                if dx:
                    swaps.append(net.remote((id(self), at, "x"), total, out.at[net.x], net.device(1, 0)))
                    swaps[-1].start()
                else:
                    stores.append(net.copy(total, out.at[net.x]))
                    stores[-1].start()
        yield
        for copy, sends in sent:
            pl.when(sends)(copy.wait_send)
        for copy in swaps:
            copy.wait()
        for copy in stores:
            copy.wait()


def _lead(ref):
    return Lead(ref)


class Lead:
    def __init__(self, ref):
        self.ref, self.shape, self.dtype = ref, (1,) + tuple(ref.shape), ref.dtype

    def __getitem__(self, index):
        return self.ref[index[1], index[2]]

    def __setitem__(self, index, value):
        self.ref[index[1], index[2]] = value


class KeysGather:
    moves = ("x", "line", "c")

    def __init__(self, face, nz, ny):
        m, rows, width = face.shape
        self.ins = [face]
        self.outs = [(jax.ShapeDtypeStruct((m, nz * rows, width), face.dtype), ANY)]
        self.scratch = []
        self.remotes, self.locals = 4 * (nz - 1), 1

    def run(self, net, ins, outs, scratch):
        (face,), (out,) = ins, outs
        nz, z = net.nz, net.z
        _, rows, width = face.shape
        part, side = rows // 2, width // 2

        def block(line, dx, dc):
            first = pl.multiple_of(line * rows + net.flip(net.x, dx) * part, part)
            column = pl.multiple_of(net.flip(net.c, dc) * side, side)
            return out.at[:, pl.ds(first, part), pl.ds(column, side)]

        own = face.at[
            :,
            pl.ds(pl.multiple_of(net.x * part, part), part),
            pl.ds(pl.multiple_of(net.c * side, side), side),
        ]
        sent, shared = [], []

        def line_copy(step):
            origin = z - (step - 1)
            src = own if step == 1 else block(origin, 0, 0)
            return net.remote((id(self), step), src, block(origin, 0, 0), net.device(z=z + 1))

        def start(step):
            copy, fits = line_copy(step), (z - (step - 1) >= 0) & (z + 1 < nz)
            pl.when(fits)(copy.start)
            sent.append((copy, fits))

        start(1)
        keep = net.copy(face, out.at[:, pl.ds(pl.multiple_of(z * rows, rows), rows), :])
        keep.start()
        later = []
        for step in range(1, nz):
            yield
            fits = z - step >= 0
            pl.when(fits)(line_copy(step).wait_recv)
            if step < nz - 1:
                start(step + 1)
            here = block(z - step, 0, 0)
            across = net.remote((id(self), "x", step), here, here, net.device(1, 0))
            beside = net.remote((id(self), "c", step), here, here, net.device(0, 0, 1))
            for copy in (across, beside):
                pl.when(fits)(copy.start)
                sent.append((copy, fits))
            later.append((step, fits, across))
            shared.append((beside, fits))
        for step, fits, across in later:
            yield
            pl.when(fits)(across.wait_recv)
            there = block(z - step, 1, 0)
            beside = net.remote((id(self), "xc", step), there, there, net.device(0, 0, 1))
            pl.when(fits)(beside.start)
            sent.append((beside, fits))
            shared.append((beside, fits))
        yield
        for copy, fits in shared:
            pl.when(fits)(copy.wait_recv)
        for copy, fits in sent:
            pl.when(fits)(copy.wait_send)
        keep.wait()


class WholeScatter(FaceScatter):
    moves = ("x", "y", "c", "z")

    def __init__(self, part, nz, ny):
        m, _, rows, d = part.shape
        super().__init__(part.reshape(m * nz, rows, d), nz, ny)
        t = rows // (4 * ny)
        self.m, self.nz = m, nz
        self.outs = [(jax.ShapeDtypeStruct((m, t, d), F32), pl.BlockSpec(memory_space=pltpu.VMEM))]
        self.scratch = self.scratch + [pltpu.VMEM((m * nz, t, d), BF16), pltpu.VMEM((nz, m, t, d), BF16)]
        self.remotes = self.remotes + nz * m
        self.locals = self.locals + m

    def run(self, net, ins, outs, scratch):
        face, inbox = scratch[-2:]
        yield from super().run(net, ins, [face], scratch[:-2])
        nz, m = self.nz, self.m
        copies = []
        for far in range(1, nz):
            line = lax.rem(net.z + far, nz)
            for at in range(m):
                copies.append(
                    pltpu.make_async_remote_copy(
                        src_ref=face.at[at * nz + line],
                        dst_ref=inbox.at[far, at],
                        send_sem=net.send.at[net.slot((id(self), "z", far, at))],
                        recv_sem=net.recv.at[net.slot((id(self), "z", far, at))],
                        device_id=net.device(z=line),
                        device_id_type=MESH,
                    )
                )
                copies[-1].start()
        own = []
        for at in range(m):
            own.append(net.copy(face.at[at * nz + net.z], inbox.at[0, at]))
            own[-1].start()
        yield
        for copy in own:
            copy.wait()
        for copy in copies:
            copy.wait()
        add_rows(outs[0], [inbox.at[far] for far in range(nz)])


class PlaneGather:
    moves = ("plane",)

    def __init__(self, own, nz, ny):
        self.ins = [own]
        self.outs = [(jax.ShapeDtypeStruct((2 * nz,) + own.shape, own.dtype), ANY)]
        self.scratch = []
        self.remotes, self.locals = 2 * nz, 1

    def run(self, net, ins, outs, scratch):
        (own,), (out,) = ins, outs
        here = out.at[net.z * 2 + net.x]
        copies = []
        for far in range(net.nz):
            for dx in (0, 1):
                if far or dx:
                    line = lax.rem(net.z + far, net.nz)
                    copies.append(net.remote((id(self), far, dx), own, here, net.device(dx, z=line)))
                    copies[-1].start()
        keep = net.copy(own, here)
        keep.start()
        yield
        for copy in copies:
            copy.wait()
        keep.wait()


class SmallScatter:
    moves = ("face", "z")

    def __init__(self, part, nz, ny):
        ranks, _, rows, width = part.shape
        self.ins = [part]
        vmem = pl.BlockSpec(memory_space=pltpu.VMEM)
        self.outs = [(jax.ShapeDtypeStruct((rows, width), F32), vmem)]
        self.scratch = [
            pltpu.VMEM((ranks, nz, rows, width), F32),
            pltpu.VMEM((nz, rows, width), F32),
            pltpu.VMEM((nz, rows, width), F32),
        ]
        self.remotes, self.locals = ranks + nz, 2

    def run(self, net, ins, outs, scratch):
        (part,), (out,) = ins, outs
        inbox, total, line_in = scratch
        ny, nz = net.ny, net.nz
        copies = []
        for dx in (0, 1):
            for dy in range(ny):
                for dc in (0, 1):
                    if dx or dy or dc:
                        at = (dx * ny + dy) * 2 + dc
                        copies.append(
                            net.remote(
                                (id(self), at), part.at[net.rank(dx, dy, dc)], inbox.at[at], net.device(dx, dy, dc)
                            )
                        )
                        copies[-1].start()
        keep = net.copy(part.at[net.rank()], inbox.at[0])
        keep.start()
        yield
        keep.wait()
        for copy in copies:
            copy.wait()
        total[...] = jnp.sum(inbox[...], axis=0)
        lines = []
        for far in range(1, nz):
            line = lax.rem(net.z + far, nz)
            lines.append(net.remote((id(self), "z", far), total.at[line], line_in.at[far], net.device(z=line)))
            lines[-1].start()
        own = net.copy(total.at[net.z], line_in.at[0])
        own.start()
        yield
        own.wait()
        for copy in lines:
            copy.wait()
        out[...] = jnp.sum(line_in[...], axis=0)


def exchange(plans, nz, ny, collective_id, name):
    moves = set()
    for plan in plans:
        moves |= set(plan.moves)
    remotes = sum(plan.remotes for plan in plans)
    locals_ = max(1, sum(plan.locals for plan in plans))
    ins = [array for plan in plans for array in plan.ins]
    outs = [out for plan in plans for out in plan.outs]
    scratch = [entry for plan in plans for entry in plan.scratch]

    def kernel(*refs):
        in_refs, refs = refs[: len(ins)], refs[len(ins) :]
        out_refs, refs = refs[: len(outs)], refs[len(outs) :]
        scratch_refs, (send, recv, local) = refs[: len(scratch)], refs[len(scratch) :]
        net = Net(nz, ny, send, recv, local)
        peers = {}
        for far in range(nz):
            for dx in (0, 1):
                for dy in range(ny):
                    for dc in (0, 1):
                        kinds = set()
                        if not far:
                            kinds.add("face")
                            if dx and not dy and not dc:
                                kinds.add("x")
                            if dy and not dx and not dc:
                                kinds.add("y")
                            if dc and not dx and not dy:
                                kinds.add("c")
                        if far and not dx and not dy and not dc:
                            kinds.add("z")
                            if far in (1, nz - 1):
                                kinds.add("line")
                        if not dy and not dc:
                            kinds.add("plane")
                        if (far or dx or dy or dc) and kinds & moves:
                            line = lax.rem(net.z + far, nz) if far else None
                            peers[far, dx, dy, dc] = net.device(dx, dy, dc, line)
        barrier = pltpu.get_barrier_semaphore()
        for device in peers.values():
            pl.semaphore_signal(barrier, inc=1, device_id=device, device_id_type=MESH)
        pl.semaphore_wait(barrier, len(peers))
        running = []
        for plan in plans:
            mine = []
            for refs_of, count in ((in_refs, plan.ins), (out_refs, plan.outs), (scratch_refs, plan.scratch)):
                mine.append(list(refs_of[: len(count)]))
            in_refs = in_refs[len(plan.ins) :]
            out_refs = out_refs[len(plan.outs) :]
            scratch_refs = scratch_refs[len(plan.scratch) :]
            running.append(plan.run(net, *mine))
        while running:
            for steps in list(running):
                try:
                    next(steps)
                except StopIteration:
                    running.remove(steps)

    results = pl.pallas_call(
        kernel,
        out_shape=[shape for shape, _ in outs],
        in_specs=[ANY] * len(ins),
        out_specs=[spec for _, spec in outs],
        scratch_shapes=scratch
        + [
            pltpu.SemaphoreType.DMA((remotes,)),
            pltpu.SemaphoreType.DMA((remotes,)),
            pltpu.SemaphoreType.DMA((locals_,)),
        ],
        compiler_params=pltpu.CompilerParams(
            collective_id=collective_id, has_side_effects=True, vmem_limit_bytes=56 << 20
        ),
        name=name,
    )(*ins)
    results = list(results)
    grouped = []
    for plan in plans:
        grouped.append(results[: len(plan.outs)])
        results = results[len(plan.outs) :]
    return grouped


def masked_scores(queries, keys, query_doc, key_doc, scale):
    raw = lax.dot_general(queries, keys, (((1,), (1,)), ((), ())), preferred_element_type=F32) * scale
    return jnp.where(query_doc == key_doc, raw, NEG_FILL)


def attend_forward(queries, keys_vals, query_doc, key_doc, bounds, heads, head_dim):
    micro_count, rows, _ = queries.shape
    blocks = rows // BLOCK
    scale = 1.0 / math.sqrt(head_dim)
    tall = heads * BLOCK

    def kernel(bounds_ref, q_ref, kv_ref, qd_ref, kd_ref, out_ref, log_ref):
        at = pl.program_id(0) * blocks + pl.program_id(1)
        low, high = bounds_ref[2 * at], bounds_ref[2 * at + 1]
        queries = jnp.concatenate([q_ref[0, :, h * head_dim : (h + 1) * head_dim] for h in range(heads)], axis=0)
        doc = jnp.concatenate([qd_ref[0]] * heads, axis=0)

        def body(block, carry):
            top, total, mixed = carry
            first = pl.multiple_of(block * BLOCK, BLOCK)
            keys = kv_ref[0, pl.ds(first, BLOCK), :head_dim]
            values = kv_ref[0, pl.ds(first, BLOCK), head_dim:]
            scores = masked_scores(queries, keys, doc, kd_ref[0, :, pl.ds(first, BLOCK)], scale)
            new_top = jnp.maximum(top, jnp.max(scores, axis=-1, keepdims=True))
            weights = jnp.where(scores == NEG_FILL, 0.0, jnp.exp(scores - new_top))
            fade = jnp.exp(top - new_top)
            total = total * fade + jnp.sum(weights, axis=-1, keepdims=True)
            mixed = mixed * fade + jnp.dot(weights.astype(BF16), values, preferred_element_type=F32)
            return new_top, total, mixed

        top, total, mixed = lax.fori_loop(
            low,
            high,
            body,
            (
                jnp.full((tall, 1), NEG_FILL, F32),
                jnp.zeros((tall, 1), F32),
                jnp.zeros((tall, head_dim), F32),
            ),
        )
        mixed = (mixed / total).astype(BF16)
        for h in range(heads):
            out_ref[0, :, h * head_dim : (h + 1) * head_dim] = mixed[h * BLOCK : (h + 1) * BLOCK]
        log_ref[0, 0] = top + jnp.log(total)

    return pl.pallas_call(
        kernel,
        out_shape=[
            jax.ShapeDtypeStruct(queries.shape, BF16),
            jax.ShapeDtypeStruct((micro_count, blocks, tall, 1), F32),
        ],
        grid_spec=pltpu.PrefetchScalarGridSpec(
            num_scalar_prefetch=1,
            grid=(micro_count, blocks),
            in_specs=[
                pl.BlockSpec((1, BLOCK, heads * head_dim), lambda m, b, _: (m, b, 0)),
                pl.BlockSpec((1,) + keys_vals.shape[1:], lambda m, b, _: (m, 0, 0)),
                pl.BlockSpec((1, BLOCK, 1), lambda m, b, _: (m, b, 0)),
                pl.BlockSpec((1, 1, keys_vals.shape[1]), lambda m, b, _: (m, 0, 0)),
            ],
            out_specs=[
                pl.BlockSpec((1, BLOCK, heads * head_dim), lambda m, b, _: (m, b, 0)),
                pl.BlockSpec((1, 1, tall, 1), lambda m, b, _: (m, b, 0, 0)),
            ],
        ),
        compiler_params=pltpu.CompilerParams(vmem_limit_bytes=40 << 20),
        name="attend_forward",
    )(bounds, queries, keys_vals, query_doc, key_doc)


def attend_backward(queries, keys_vals, mixed, grad_mixed, log_total, query_doc, key_doc, bounds, heads, head_dim):
    micro_count, rows, _ = queries.shape
    blocks = rows // BLOCK
    seq_len = keys_vals.shape[1]
    scale = 1.0 / math.sqrt(head_dim)
    tall = heads * BLOCK

    def kernel(bounds_ref, q_ref, kv_ref, o_ref, do_ref, log_ref, qd_ref, kd_ref, gq_ref, gkv_ref, acc_ref):
        at = pl.program_id(0) * blocks + pl.program_id(1)
        low, high = bounds_ref[2 * at], bounds_ref[2 * at + 1]

        def stack(ref):
            return jnp.concatenate([ref[0, :, h * head_dim : (h + 1) * head_dim] for h in range(heads)], axis=0)

        @pl.when(pl.program_id(1) == 0)
        def _():
            acc_ref[...] = jnp.zeros_like(acc_ref)

        queries, grad = stack(q_ref), stack(do_ref)
        delta = jnp.sum(grad.astype(F32) * stack(o_ref).astype(F32), axis=-1, keepdims=True)
        doc = jnp.concatenate([qd_ref[0]] * heads, axis=0)
        log_total = log_ref[0, 0]

        def body(block, grad_queries):
            first = pl.multiple_of(block * BLOCK, BLOCK)
            keys = kv_ref[0, pl.ds(first, BLOCK), :head_dim]
            values = kv_ref[0, pl.ds(first, BLOCK), head_dim:]
            scores = masked_scores(queries, keys, doc, kd_ref[0, :, pl.ds(first, BLOCK)], scale)
            probs = jnp.where(scores == NEG_FILL, 0.0, jnp.exp(scores - log_total))
            grad_probs = lax.dot_general(grad, values, (((1,), (1,)), ((), ())), preferred_element_type=F32)
            grad_scores = (probs * (grad_probs - delta)).astype(BF16)
            across = (((0,), (0,)), ((), ()))
            acc_ref[pl.ds(first, BLOCK), :head_dim] += (
                lax.dot_general(grad_scores, queries, across, preferred_element_type=F32) * scale
            )
            acc_ref[pl.ds(first, BLOCK), head_dim:] += lax.dot_general(
                probs.astype(BF16), grad, across, preferred_element_type=F32
            )
            return grad_queries + jnp.dot(grad_scores, keys, preferred_element_type=F32)

        grad_queries = lax.fori_loop(low, high, body, jnp.zeros((tall, head_dim), F32))
        grad_queries = (grad_queries * scale).astype(BF16)
        for h in range(heads):
            gq_ref[0, :, h * head_dim : (h + 1) * head_dim] = grad_queries[h * BLOCK : (h + 1) * BLOCK]

        @pl.when(pl.program_id(1) == blocks - 1)
        def _():
            gkv_ref[0] = acc_ref[...].astype(BF16)

    wide = pl.BlockSpec((1, BLOCK, heads * head_dim), lambda m, b, _: (m, b, 0))
    row = pl.BlockSpec((1, seq_len, 2 * head_dim), lambda m, b, _: (m, 0, 0))
    return pl.pallas_call(
        kernel,
        out_shape=[
            jax.ShapeDtypeStruct(queries.shape, BF16),
            jax.ShapeDtypeStruct(keys_vals.shape, BF16),
        ],
        grid_spec=pltpu.PrefetchScalarGridSpec(
            num_scalar_prefetch=1,
            grid=(micro_count, blocks),
            in_specs=[
                wide,
                row,
                wide,
                wide,
                pl.BlockSpec((1, 1, tall, 1), lambda m, b, _: (m, b, 0, 0)),
                pl.BlockSpec((1, BLOCK, 1), lambda m, b, _: (m, b, 0)),
                pl.BlockSpec((1, 1, seq_len), lambda m, b, _: (m, 0, 0)),
            ],
            out_specs=[wide, row],
            scratch_shapes=[pltpu.VMEM((seq_len, 2 * head_dim), F32)],
        ),
        compiler_params=pltpu.CompilerParams(vmem_limit_bytes=40 << 20),
        name="attend_backward",
    )(bounds, queries, keys_vals, mixed, grad_mixed, log_total, query_doc, key_doc)


def local(
    inputs,
    cotangent,
    doc_ids,
    attn_gain,
    attn_shift,
    w_query,
    w_keyval,
    w_attn_out,
    mlp_gain,
    mlp_shift,
    w_expand,
    w_reduce,
):
    nz = lax.axis_size("dp") // 2
    tensor_count = lax.axis_size("tensor")
    ny = tensor_count // 2
    ranks = 2 * tensor_count
    micro_count, own_rows, width = inputs.shape
    face_rows = own_rows * ranks
    tokens = micro_count * face_rows
    seq_len = doc_ids.shape[1]
    head_dim = w_keyval.shape[1] // 2
    heads = w_query.shape[1] // (2 * head_dim)
    z = lax.axis_index("dp") // 2
    swap = functools.partial(exchange, nz=nz, ny=ny)
    on = (nz, ny)

    def dot(a, b):
        return jnp.dot(a, b, preferred_element_type=F32)

    def dot_bt(a, b):
        return lax.dot_general(a, b, (((1,), (1,)), ((), ())), preferred_element_type=F32)

    def dot_at(a, b):
        return lax.dot_general(a, b, (((0,), (0,)), ((), ())), preferred_element_type=F32)

    norms = jnp.stack([attn_gain, attn_shift, mlp_gain, mlp_shift])
    norms = jnp.concatenate([norms, jnp.zeros((4, norms.shape[1]), BF16)])
    (face_in,), (wq, wo, wkv), (norms,) = swap(
        [
            FaceGather(inputs, *on),
            LineGather([w_query, w_attn_out, w_keyval], ["row", "col", "both"], *on),
            PlaneGather(norms, *on),
        ],
        collective_id=1,
        name="gather_attention",
    )
    norms = norms[:, :4].transpose(1, 0, 2).reshape(4, width).astype(F32)
    gain_one, shift_one, gain_two, shift_two = norms[0], norms[1], norms[2], norms[3]

    normed = layer_norm(face_in.astype(F32), gain_one, shift_one).astype(BF16).reshape(tokens, width)
    queries = dot(normed, wq).astype(BF16).reshape(micro_count, face_rows, heads * head_dim)
    keys_face = dot(normed, wkv).astype(BF16).reshape(micro_count, face_rows, 2 * head_dim)
    ((keys_vals,),) = swap([KeysGather(keys_face, *on)], collective_id=2, name="gather_keys")

    query_doc = lax.dynamic_slice_in_dim(doc_ids, z * face_rows, face_rows, axis=1)
    blocks = face_rows // BLOCK
    last_doc = doc_ids[:, BLOCK - 1 :: BLOCK]
    first_doc = query_doc[:, ::BLOCK]
    lows = jnp.sum((last_doc[:, None, :] < first_doc[:, :, None]).astype(jnp.int32), axis=-1)
    highs = jnp.broadcast_to(z * blocks + jnp.arange(blocks, dtype=jnp.int32) + 1, lows.shape)
    bounds = jnp.stack([lows, highs], axis=-1).reshape(-1)
    docs = (query_doc[:, :, None], doc_ids[:, None, :], bounds, heads, head_dim)
    mixed, log_total = attend_forward(queries, keys_vals, *docs)
    mixed_flat = mixed.reshape(tokens, heads * head_dim)

    branch = dot(mixed_flat, wo).astype(BF16).reshape(micro_count, face_rows, width)
    (branch,), (cot_face,), (wexp,) = swap(
        [FaceScatter(branch, *on), FaceGather(cotangent, *on), LineGather([w_expand], ["row"], *on)],
        collective_id=3,
        name="scatter_branch",
    )
    own_in = inputs.astype(F32)
    middle = own_in + branch
    normed_two_full, norm_pull_two = jax.vjp(layer_norm, middle, gain_two, shift_two)
    (normed_two,), (wred,) = swap(
        [FaceGather(normed_two_full.astype(BF16), *on), LineGather([w_reduce], ["col"], *on)],
        collective_id=4,
        name="gather_normed_two",
    )
    normed_two = normed_two.reshape(tokens, width)
    cot_flat = cot_face.reshape(tokens, width)
    gelu_value, gelu_pull = jax.vjp(gelu_tanh, dot(normed_two, wexp))
    active = gelu_value.astype(BF16)
    part_reduce = dot_at(active, cot_flat).astype(BF16)
    grad_hidden = gelu_pull(dot_bt(cot_flat, wred))[0].astype(BF16)
    grad_normed_two = dot_bt(grad_hidden, wexp).astype(BF16).reshape(micro_count, face_rows, width)
    part_expand = dot_at(normed_two, grad_hidden).astype(BF16)
    reduced = dot(active, wred).astype(BF16).reshape(micro_count, face_rows, width)
    (grad_normed_two,), (grad_reduce,) = swap(
        [FaceScatter(grad_normed_two, *on), LineScatter([part_reduce], ["col"], *on)],
        collective_id=5,
        name="scatter_normed_two",
    )
    grad_mid_norm, grad_gain_two, grad_shift_two = norm_pull_two(grad_normed_two)
    grad_middle = cotangent.astype(F32) + grad_mid_norm
    (grad_branch,), (reduced,), (grad_expand,) = swap(
        [
            FaceGather(grad_middle.astype(BF16), *on),
            FaceScatter(reduced, *on),
            LineScatter([part_expand], ["row"], *on),
        ],
        collective_id=6,
        name="gather_branch",
    )
    outputs = (middle + reduced).astype(BF16)
    grad_branch = grad_branch.reshape(tokens, width)
    part_attn_out = dot_at(mixed_flat, grad_branch).astype(BF16)
    grad_mixed = dot_bt(grad_branch, wo).astype(BF16).reshape(mixed.shape)
    grad_queries, grad_keys = attend_backward(queries, keys_vals, mixed, grad_mixed, log_total, *docs)
    grad_queries = grad_queries.reshape(tokens, heads * head_dim)
    part_query = dot_at(normed, grad_queries).astype(BF16)
    from_query = dot_bt(grad_queries, wq).astype(BF16).reshape(micro_count, face_rows, width)
    (from_query,), (grad_keys,), (grad_attn_out, grad_query) = swap(
        [
            FaceScatter(from_query, *on),
            WholeScatter(grad_keys.reshape(micro_count, nz, face_rows, 2 * head_dim), *on),
            LineScatter([part_attn_out, part_query], ["col", "row"], *on),
        ],
        collective_id=7,
        name="scatter_query",
    )
    grad_keys = grad_keys.astype(BF16).reshape(micro_count * own_rows, 2 * head_dim)
    normed_own, norm_pull_one = jax.vjp(layer_norm, own_in, gain_one, shift_one)
    grad_normed = from_query + dot_bt(grad_keys, wkv).reshape(from_query.shape)
    grad_tok_norm, grad_gain_one, grad_shift_one = norm_pull_one(grad_normed)
    part_keyval = dot_at(normed_own.astype(BF16).reshape(-1, width), grad_keys).astype(BF16)
    own_width = width // (nz * ranks)
    small = jnp.stack([grad_gain_one, grad_shift_one, grad_gain_two, grad_shift_two])
    small = small.reshape(4, nz, ranks, own_width).transpose(2, 1, 0, 3)
    small = jnp.pad(small, ((0, 0), (0, 0), (0, 4), (0, 128 - own_width)))
    (grad_keyval,), (small,) = swap(
        [WholeScatter(part_keyval.reshape(1, nz, width // nz, 2 * head_dim), *on), SmallScatter(small, *on)],
        collective_id=8,
        name="scatter_small",
    )
    small = small[:4, :own_width]

    def by_row(halves):
        return jnp.concatenate([halves[0], halves[1]], axis=1).astype(F32)

    def by_column(halves):
        return halves.reshape(-1, halves.shape[-1]).astype(F32)

    return (
        outputs,
        grad_middle + grad_tok_norm,
        small[0],
        small[1],
        by_row(grad_query),
        grad_keyval[0],
        by_column(grad_attn_out),
        small[2],
        small[3],
        by_row(grad_expand),
        by_column(grad_reduce),
    )


def solution(mesh):
    placed = (
        P(None, ("dp", "tensor"), None),
        P(None, ("dp", "tensor"), None),
        P(),
        P("dp"),
        P("dp"),
        P("dp", "tensor"),
        P("dp", None),
        P("tensor", "dp"),
        P("dp"),
        P("dp"),
        P("dp", "tensor"),
        P("tensor", "dp"),
    )
    return jax.shard_map(
        local,
        mesh=mesh,
        in_specs=placed,
        out_specs=(
            P(None, ("dp", "tensor"), None),
            P(None, ("dp", "tensor"), None),
            P(("dp", "tensor")),
            P(("dp", "tensor")),
            P("dp", "tensor"),
            P(("dp", "tensor"), None),
            P("tensor", "dp"),
            P(("dp", "tensor")),
            P(("dp", "tensor")),
            P("dp", "tensor"),
            P("tensor", "dp"),
        ),
        check_vma=False,
    )
```

time: 2180 us -> 767 us (0.35)
  waiting for transfers between devices: 1530 us -> 0 us
  Pallas kernels: 0 us -> 616 us
  matrix products: 327 us -> 96.7 us
  blocking collectives: 114 us -> 0 us
  local copies, waits for them, and re-layouts: 117 us -> 14.6 us
  other arithmetic: 54.4 us -> 29.6 us
    reduce_scatter x20 -> x0, waiting for transfers between devices: 965 us -> none  [the longest x3 224 us: local(): lax.psum_scatter(grad_kv_rows, ('dp', 'tensor'), scatter_dimension=0, til...]
    pallas_call x0 -> x10, Pallas kernels: none -> 616 us  [the longest x8 598 us: exchange(): pl.pallas_call(kernel, out_shape=[shape for shape, _ in outs], in_specs=[...]
    all_gather x20 -> x0, waiting for transfers between devices: 561 us -> none  [the longest x1 128 us: fetch(): lax.all_gather(w_reduce, 'dp', axis=1, tiled=True)]
    dot_general x213 -> x15, matrix products: 327 us -> 96.7 us  [the longest x5 35.8 us: dot(): return jnp.dot(a, b, preferred_element_type=F32)]
    all_gather x4 -> x0, blocking collectives: 73.6 us -> none  [the longest x1 22.2 us: fetch(): lax.all_gather(attn_shift, 'dp', axis=0, tiled=True)]
    squeeze x72 -> x3, local copies, waits for them, and re-layouts: 66.4 us -> 1.44 us  [the longest x1 1.35 us: local(): small[3]]
    unnamed x1 -> x0, blocking collectives: 40.2 us -> none
  transfers between devices with their start and end apart: 40 -> 0, of which waited for: 34 -> 0; matrix products, arithmetic and copies ran while one was open for 21% -> 0% of each run, Pallas kernels for 0% -> 0%
where the time goes in v1:
time: 767 us; the launch traced here: 758 us
  Pallas kernels  616 us (80%)
  matrix products  96.7 us (13%)
  other arithmetic  29.6 us (4%)
  local copies, waits for them, and re-layouts  14.6 us (2%)
    pallas_call x8, Pallas kernels, exchange(): pl.pallas_call(kernel, out_shape=[shape for shape, _ in outs], in_specs=[...  598 us
    dot_general x5, matrix products, dot(): return jnp.dot(a, b, preferred_element_type=F32)  35.8 us
    dot_general x5, matrix products, dot_bt(): lax.dot_general(a, b, (((1,), (1,)), ((), ())), preferred_element_type=F32)  32.4 us
    dot_general x5, matrix products, dot_at(): lax.dot_general(a, b, (((0,), (0,)), ((), ())), preferred_element_type=F32)  28.5 us

profile of v1, /device:TPU:0, one launch (start us, length us, event | category | flops | bytes accessed | tf_op | source)
XLA Modules:
  0.0 758.0 jit_solution(13373822289144153648)
XLA Ops:
  3.4 0.8 slice.54
  5.5 0.7 constant_dynamic-slice_fusion
  6.8 0.8 broadcast_in_dim.31.kd_ref
  7.9 79.3 %gather_attention.1 = (bf16[3,512,2048]{2,1,0:T(8,128)(2,1)}, bf16[2048,256]{1,0:T(8,128)(2,1)}, bf16[256,2048]{1,0:T(8,128)(2,1)}, bf16[2048,256]{1,0:T(8,128)(2,1)}, bf16[8,8,256]{2,1,0:T(8,128)(2,1)}) custom-call(bf16[3,64,2048]{2,1,0:T(8,128)(2,1)} %refs_0_.1, bf16[256,512]{1,0:T(8,128)(2,1)} %refs_1_.3, bf16[512,256]{1,0:T(8,128)(2,1)} %refs_2_.2, ...), custom_call_target="tpu_custom_call" | custom-call | tf_op jit(solution)/shard_map/gather_attention/pallas_call | solution.py:747
  87.3 0.9 convert_bitcast_fusion
  88.2 3.9 convert_reduce_fusion
  92.1 1.8 fusion.2
  93.9 3.1 fusion.5
  97.0 2.9 convolution_convert_fusion.7
  100.0 1.9 convolution_convert_fusion.8
  101.8 26.7 %gather_keys.1.kv_ref = bf16[3,2048,256]{2,1,0:T(8,128)(2,1)} custom-call(bf16[3,512,256]{2,1,0:T(8,128)(2,1)} %bitcast.108), custom_call_target="tpu_custom_call" | custom-call | tf_op jit(solution)/shard_map/gather_keys/pallas_call | solution.py:747
  128.5 1.9 copy-done
  130.4 8.1 %attend_forward.1 = (bf16[3,512,256]{2,1,0:T(8,128)(2,1)S(1)}, f32[3,2,512,1]{3,2,1,0:T(8,128)S(1)}) custom-call(s32[12]{0:T(128)S(1)} %reshape.176.bounds_ref, bf16[3,512,256]{2,1,0:T(8,128)(2,1)S(1)} %bitcast.91, bf16[3,2048,256]{2,1,0:T(8,128)(2,1)S(1)} %copy-done, s32[3,512,1]{2,1,0:T(8,128)S(1)} %copy.37.qd_ref, s32[3,1,2048]{2,1,0:T(1,128)S(1)} %broadcast_in_dim.31.kd_ref), custom_call_target="tpu_custom_call" | custom-call | tf_op jit(solution)/shard_map/attend_forward/pallas_call | solution.py:816
  138.5 4.4 convolution_convert_fusion.1
  142.9 96.1 %scatter_branch.1 = (f32[3,64,2048]{2,1,0:T(8,128)}, bf16[3,512,2048]{2,1,0:T(8,128)(2,1)}, bf16[2048,1024]{1,0:T(8,128)(2,1)}) custom-call(bf16[3,512,2048]{2,1,0:T(8,128)(2,1)} %bitcast.97, bf16[3,64,2048]{2,1,0:T(8,128)(2,1)} %refs_1_.4, bf16[256,2048]{1,0:T(8,128)(2,1)} %refs_2_.3), custom_call_target="tpu_custom_call" | custom-call | tf_op jit(solution)/shard_map/scatter_branch/pallas_call | solution.py:747
  239.1 1.8 fusion.41
  241.2 1.3 add_convert_fusion.1.refs_0_
  242.4 88.1 %gather_normed_two.1 = (bf16[3,512,2048]{2,1,0:T(8,128)(2,1)}, bf16[1024,2048]{1,0:T(8,128)(2,1)}) custom-call(bf16[3,64,2048]{2,1,0:T(8,128)(2,1)} %add_convert_fusion.1.refs_0_, bf16[2048,256]{1,0:T(8,128)(2,1)} %refs_1_.5), custom_call_target="tpu_custom_call" | custom-call | tf_op jit(solution)/shard_map/gather_normed_two/pallas_call | solution.py:747
  330.5 12.0 %fusion.43 = f32[1536,1024]{1,0:T(8,128)} fusion(bf16[1536,2048]{1,0:T(8,128)(2,1)} %bitcast.122, bf16[1024,2048]{1,0:T(8,128)(2,1)} %get-tuple-element.44), kind=kOutput, calls=%fused_computation.100 | convolution fusion | flops 6442450944 | bytes 16777216 | tf_op jit(solution)/shard_map/dot_general | solution.py:950
  342.5 13.6 %fusion.12 = (bf16[1536,1024]{1,0:T(8,128)(2,1)S(1)}, f32[1536,1024]{1,0:T(8,128)}) fusion(f32[1536,1024]{1,0:T(8,128)} %fusion.43, bf16[1536,2048]{1,0:T(8,128)(2,1)S(1)} %bitcast.126, bf16[2048,1024]{1,0:T(8,128)(2,1)S(1)} %copy-done.26), kind=kOutput, calls=%fused_computation.20 | convolution fusion | flops 6473908224 | bytes 26214400 | tf_op jit(solution)/shard_map/dot_general | solution.py:947
  356.1 12.5 %convolution_convert_fusion.5.refs_1_ = bf16[1024,2048]{1,0:T(8,128)(2,1)} fusion(bf16[1536,2048]{1,0:T(8,128)(2,1)S(1)} %bitcast.125, f32[1536,1024]{1,0:T(8,128)} %get-tuple-element.89), kind=kOutput, calls=%fused_computation.23 | convolution fusion | flops 6458703872 | bytes 16777216 | tf_op jit(solution)/shard_map/dot_general | solution.py:953
  368.6 8.7 %convolution_convert_fusion.4.refs_2_ = bf16[2048,1024]{1,0:T(8,128)(2,1)} fusion(bf16[1536,2048]{1,0:T(8,128)(2,1)S(1)} %bitcast.127, bf16[1536,1024]{1,0:T(8,128)(2,1)S(1)} %get-tuple-element.88), kind=kOutput, calls=%fused_computation.22 | convolution fusion | flops 6444548096 | bytes 13631488 | tf_op jit(solution)/shard_map/dot_general | solution.py:953
  377.3 8.8 %convolution_convert_fusion.3 = bf16[1536,2048]{1,0:T(8,128)(2,1)} fusion(bf16[1536,1024]{1,0:T(8,128)(2,1)S(1)} %get-tuple-element.88, bf16[2048,1024]{1,0:T(8,128)(2,1)S(1)} %copy-done.26), kind=kOutput, calls=%fused_computation.13 | convolution fusion | flops 6445596672 | bytes 13631488 | tf_op jit(solution)/shard_map/dot_general | solution.py:950
  386.1 76.8 %scatter_normed_two.1 = (f32[3,64,2048]{2,1,0:T(8,128)}, bf16[2,1024,256]{2,1,0:T(8,128)(2,1)}) custom-call(bf16[3,512,2048]{2,1,0:T(8,128)(2,1)} %bitcast.102, bf16[1024,2048]{1,0:T(8,128)(2,1)} %convolution_convert_fusion.5.refs_1_), custom_call_target="tpu_custom_call" | custom-call | tf_op jit(solution)/shard_map/scatter_normed_two/pallas_call | solution.py:747
  462.9 2.1 multiply_reduce_fusion
  465.0 1.6 fusion.40
  466.8 2.9 fusion.28.refs_0_
  469.7 2.7 bitcast_convert_fusion
  472.4 13.1 %convolution_convert_fusion.2 = bf16[1536,2048]{1,0:T(8,128)(2,1)} fusion(bf16[1024,2048]{1,0:T(8,128)(2,1)S(1)} %copy-done.25, f32[1536,1024]{1,0:T(8,128)} %get-tuple-element.89), kind=kOutput, calls=%fused_computation.12 | convolution fusion | flops 6459752448 | bytes 16777216 | tf_op jit(solution)/shard_map/dot_general | solution.py:947
  485.5 101.8 %gather_branch.1 = (bf16[3,512,2048]{2,1,0:T(8,128)(2,1)}, f32[3,64,2048]{2,1,0:T(8,128)}, bf16[2,256,1024]{2,1,0:T(8,128)(2,1)}) custom-call(bf16[3,64,2048]{2,1,0:T(8,128)(2,1)} %fusion.28.refs_0_, bf16[3,512,2048]{2,1,0:T(8,128)(2,1)} %bitcast.106, bf16[2048,1024]{1,0:T(8,128)(2,1)} %convolution_convert_fusion.4.refs_2_), custom_call_target="tpu_custom_call" | custom-call | tf_op jit(solution)/shard_map/gather_branch/pallas_call | solution.py:747
  587.3 4.8 convolution_convert_fusion.6
  592.1 9.8 %attend_backward.1 = (bf16[3,512,256]{2,1,0:T(8,128)(2,1)S(1)}, bf16[3,2048,256]{2,1,0:T(8,128)(2,1)S(1)}) custom-call(s32[12]{0:T(128)S(1)} %reshape.176.bounds_ref, bf16[3,512,256]{2,1,0:T(8,128)(2,1)S(1)} %bitcast.92, bf16[3,2048,256]{2,1,0:T(8,128)(2,1)S(1)} %copy-done.1, bf16[3,512,256]{2,1,0:T(8,128)(2,1)S(1)} %get-tuple-element.40.o_ref, ...), custom_call_target="tpu_custom_call" | custom-call | tf_op jit(solution)/shard_map/attend_backward/pallas_call | solution.py:892
  602.1 2.9 fusion.14.refs_3_
  605.5 1.1 add_convert_fusion
  606.8 0.8 slice-done.3
  607.6 2.8 fusion.13.refs_2_
  610.5 1.6 maximum_convert_fusion
  612.0 4.4 convolution_convert_fusion
  616.5 108.6 %scatter_query.1 = (f32[3,64,2048]{2,1,0:T(8,128)}, f32[3,64,256]{2,1,0:T(8,128)}, bf16[2,256,256]{2,1,0:T(8,128)(2,1)}, bf16[2,256,256]{2,1,0:T(8,128)(2,1)}) custom-call(bf16[3,512,2048]{2,1,0:T(8,128)(2,1)} %bitcast.96, bf16[12,512,256]{2,1,0:T(8,128)(2,1)} %bitcast.93, bf16[256,2048]{1,0:T(8,128)(2,1)} %fusion.13.refs_2_, bf16[2048,256]{1,0:T(8,128)(2,1)} %fusion.14.refs_3_), custom_call_target="tpu_custom_call" | custom-call | tf_op jit(solution)/shard_map/scatter_query/pallas_call | solution.py:747
  725.1 2.4 fusion.25
  727.5 0.8 fusion.24
  728.3 1.9 add_add_fusion.2
  731.1 0.9 maximum_convert_fusion.1
  732.0 0.8 bitcast_convert_fusion.1
  732.8 1.6 fusion.15
  734.4 20.5 %scatter_small.1 = (f32[1,64,256]{2,1,0:T(8,128)}, f32[8,128]{1,0:T(8,128)}) custom-call(bf16[4,512,256]{2,1,0:T(8,128)(2,1)} %bitcast.107, f32[8,4,8,128]{3,2,1,0:T(8,128)} %pad.4.refs_1_), custom_call_target="tpu_custom_call" | custom-call | tf_op jit(solution)/shard_map/scatter_small/pallas_call | solution.py:747
  755.0 1.4 slice_bitcast_fusion.4
  756.3 1.5 copy.48
  (105 shorter events, 7.4 us)
Async XLA Ops:
  87.3 4.8 copy-start.5
  93.9 3.1 copy-start.19
  97.0 3.0 copy-start.11
  97.0 2.9 copy-start.14
  101.8 36.7 %copy-start.16 = (bf16[256,2048]{1,0:T(8,128)(2,1)S(1)}, bf16[256,2048]{1,0:T(8,128)(2,1)}, u32[]{:S(2)}) copy-start(bf16[256,2048]{1,0:T(8,128)(2,1)} %get-tuple-element.41) | copy-start | bytes 3145732
  128.5 1.9 copy-start
  138.5 4.4 copy-start.3
  142.9 96.1 %copy-start.8 = (bf16[3,64,2048]{2,1,0:T(8,128)(2,1)S(1)}, bf16[3,64,2048]{2,1,0:T(8,128)(2,1)}, u32[]{:S(2)}) copy-start(bf16[3,64,2048]{2,1,0:T(8,128)(2,1)} %refs_0_.1) | copy-start | bytes 2359300
  240.8 224.2 %copy-start.6 = (f32[3,64,2048]{2,1,0:T(8,128)}, f32[3,64,2048]{2,1,0:T(8,128)S(1)}, u32[]{:S(2)}) copy-start(f32[3,64,2048]{2,1,0:T(8,128)S(1)} %get-tuple-element.72) | copy-start | bytes 4718596
  330.5 12.0 %copy-start.24 = (bf16[3,512,2048]{2,1,0:T(8,128)(2,1)S(1)}, bf16[3,512,2048]{2,1,0:T(8,128)(2,1)}, u32[]{:S(2)}) copy-start(bf16[3,512,2048]{2,1,0:T(8,128)(2,1)} %get-tuple-element.45) | copy-start | bytes 18874372
  330.5 12.0 %copy-start.26 = (bf16[2048,1024]{1,0:T(8,128)(2,1)S(1)}, bf16[2048,1024]{1,0:T(8,128)(2,1)}, u32[]{:S(2)}) copy-start(bf16[2048,1024]{1,0:T(8,128)(2,1)} %get-tuple-element.46) | copy-start | bytes 12582916
  330.5 25.6 %slice-start.4 = ((s8[6291456]{0:T(1024)(128)(4,1)}), s8[4194304]{0:T(1024)(128)(4,1)S(1)}, s32[]{:S(2)}) async-start(s8[6291456]{0:T(1024)(128)(4,1)} %bitcast.123), calls=%async_computation.4 | async-start | bytes 8388608
  342.5 13.6 %slice-start.5 = ((s8[6291456]{0:T(1024)(128)(4,1)}), s8[2097152]{0:T(1024)(128)(4,1)S(1)}, s32[]{:S(2)}) async-start(s8[6291456]{0:T(1024)(128)(4,1)} %bitcast.123), calls=%async_computation.5 | async-start | bytes 4194304
  462.9 2.1 copy-start.12
  466.8 5.6 copy-start.25
  485.5 101.8 %copy-start.17 = (bf16[256,2048]{1,0:T(8,128)(2,1)S(1)}, bf16[256,2048]{1,0:T(8,128)(2,1)}, u32[]{:S(2)}) copy-start(bf16[256,2048]{1,0:T(8,128)(2,1)} %get-tuple-element.41) | copy-start | bytes 3145732
  485.5 116.5 %slice-start = ((s8[6291456]{0:T(1024)(128)(4,1)}), s8[2097152]{0:T(1024)(128)(4,1)S(1)}, s32[]{:S(2)}) async-start(s8[6291456]{0:T(1024)(128)(4,1)} %bitcast.100), calls=%async_computation | async-start | bytes 4194304
  587.3 4.8 copy-start.1
  587.3 4.8 copy-start.4
  587.3 14.7 %slice-start.1 = ((s8[6291456]{0:T(1024)(128)(4,1)}), s8[4194304]{0:T(1024)(128)(4,1)S(1)}, s32[]{:S(2)}) async-start(s8[6291456]{0:T(1024)(128)(4,1)} %bitcast.100), calls=%async_computation.1 | async-start | bytes 8388608
  602.0 3.0 copy-start.2
  602.0 4.8 slice-start.2
  602.0 2.9 copy-start.7
  602.1 3.4 copy-start.13
  602.1 5.5 slice-start.3
  607.6 2.8 copy-start.18
  610.4 1.6 copy-start.15
  616.5 108.6 %copy-start.20 = (bf16[2048,256]{1,0:T(8,128)(2,1)S(1)}, bf16[2048,256]{1,0:T(8,128)(2,1)}, u32[]{:S(2)}) copy-start(bf16[2048,256]{1,0:T(8,128)(2,1)} %get-tuple-element.39) | copy-start | bytes 3145732
  725.0 3.2 copy-start.9
  725.0 3.2 copy-start.10
  727.5 3.7 copy-start.22
  728.2 3.8 copy-start.21
  728.3 4.6 copy-start.23

commit v2 on v1

--- a/solution.py
+++ b/solution.py
@@ -11,6 +11,8 @@
 BLOCK = 256
 EPSILON = 1e-05
 NEG_FILL = -1e30
+GELU_A = math.sqrt(2.0 / math.pi)
+GELU_B = 0.044715
 MESH = pl.DeviceIdType.MESH
 ANY = pl.BlockSpec(memory_space=pl.ANY)
 BF16 = jnp.bfloat16
@@ -76,9 +78,9 @@
         return pltpu.make_async_copy(src, dst, self.local.at[at])
 
 
-def add_rows(dst, terms, rows=16):
-    lead, height, _ = dst.shape
-    rows = min(rows, height)
+def add_rows(dst, terms):
+    lead, height, width = dst.shape
+    rows = min(max(16, 32768 // width), height)
     steps = height // rows
 
     def body(step, carry):
@@ -95,8 +97,8 @@
 class FaceGather:
     moves = ("x", "y", "c")
 
-    def __init__(self, own, nz, ny):
-        self.ins = [own]
+    def __init__(self, own, nz, ny, hold_x=False):
+        self.ins, self.hold_x = [own], hold_x
         m, t, d = own.shape
         self.outs = [(jax.ShapeDtypeStruct((m, 4 * ny * t, d), own.dtype), ANY)]
         self.scratch = []
@@ -119,14 +121,20 @@
             sent[key] = net.remote((id(self), key), src, dst, device)
             sent[key].start()
 
-        send(("x", 0), mine[0], piece(0, 0, 0), net.device(1, 0))
+        if not self.hold_x:
+            send(("x", 0), mine[0], piece(0, 0, 0), net.device(1, 0))
         for dy in dys:
             send(("y", dy, 1), mine[1], piece(0, 0, 1), net.device(0, dy))
-        send(("x", 1), mine[1], piece(0, 0, 1), net.device(1, 0))
+        if not self.hold_x:
+            send(("x", 1), mine[1], piece(0, 0, 1), net.device(1, 0))
         for dy in dys:
             send(("y", dy, 0), mine[0], piece(0, 0, 0), net.device(0, dy))
         for h in (0, 1):
             send(("c", h), mine[h], piece(0, 0, h), net.device(0, 0, 1))
+        if self.hold_x:
+            yield
+            for h in (0, 1):
+                send(("x", h), mine[h], piece(0, 0, h), net.device(1, 0))
 
         def share(key, dx, dy, h):
             send(("c",) + key, piece(dx, dy, h), piece(dx, dy, h), net.device(0, 0, 1))
@@ -167,26 +175,27 @@
 class FaceScatter:
     moves = ("x", "y", "c")
 
-    def __init__(self, part, nz, ny, dtype=F32):
-        self.ins = [part]
+    def __init__(self, part, nz, ny, resident=False):
+        self.ins, self.resident = [part], resident
         m, rows, d = part.shape
         t = rows // (4 * ny)
-        self.outs = [(jax.ShapeDtypeStruct((m, t, d), dtype), pl.BlockSpec(memory_space=pltpu.VMEM))]
+        self.outs = [(jax.ShapeDtypeStruct((m, t, d), F32), pl.BlockSpec(memory_space=pltpu.VMEM))]
         half = t // 2
         self.half = half
         self.scratch = [
             pltpu.VMEM((2 * ny, m, t, d), BF16),
-            pltpu.VMEM((2 * ny, m, t, d), BF16),
-            pltpu.VMEM((ny, m, half, d), BF16),
-            pltpu.VMEM((ny, m, half, d), BF16),
+            pltpu.VMEM((ny - 1, m, half, d), BF16),
+            pltpu.VMEM((ny - 1, m, half, d), BF16),
             pltpu.VMEM((2, m, half, d), BF16),
-            pltpu.VMEM((2, ny, m, half, d), BF16),
+            pltpu.VMEM((2, ny - 1, m, half, d), BF16),
         ]
+        if not resident:
+            self.scratch.append(pltpu.VMEM((2 * ny, m, t, d), BF16))
         self.remotes, self.locals = 6 * ny + 4, 2 * ny
 
     def run(self, net, ins, outs, scratch):
         (part,), (out,), half = ins, outs, self.half
-        work, from_core, x_diag, y_diag, x_in, y_in = scratch
+        from_core, x_diag, y_diag, x_in, y_in = scratch[:5]
         ny = net.ny
         dys = range(1, ny)
         order = [(1, dy) for dy in dys] + [(1, 0)] + [(0, dy) for dy in dys] + [(0, 0)]
@@ -196,49 +205,56 @@
             sent[key] = net.remote((id(self), key), src, dst, device)
             sent[key].start()
 
-        def rows(dx, dy, dc):
-            return part.at[:, pl.ds(pl.multiple_of(net.rank(dx, dy, dc) * 2 * half, half), 2 * half), :]
+        def rows(dx, dy, dc, first=0, size=2 * half):
+            at = net.rank(dx, dy, dc) * 2 * half + first
+            return part.at[:, pl.ds(pl.multiple_of(at, half), size), :]
+
+        def work(dx, dy, first=0, size=2 * half):
+            if self.resident:
+                return rows(dx, dy, 0, first, size)
+            return scratch[5].at[dx * ny + dy, :, pl.ds(first, size), :]
 
         for dx, dy in order:
             at = dx * ny + dy
-            loads[at] = net.copy(rows(dx, dy, 0), work.at[at])
-            loads[at].start()
+            if not self.resident:
+                loads[at] = net.copy(rows(dx, dy, 0), work(dx, dy))
+                loads[at].start()
             send(("c", at), rows(dx, dy, 1), from_core.at[at], net.device(0, 0, 1))
         for dx, dy in order:
             at = dx * ny + dy
             yield
-            loads[at].wait()
+            if not self.resident:
+                loads[at].wait()
             sent["c", at].wait_recv()
-            add_rows(work.at[at], [work.at[at], from_core.at[at]])
-            top, low = work.at[at, :, pl.ds(0, half), :], work.at[at, :, pl.ds(half, half), :]
+            add_rows(work(dx, dy), [work(dx, dy), from_core.at[at]])
+            top, low = work(dx, dy, 0, half), work(dx, dy, half, half)
             if dx and dy:
-                send(("xd", dy), top, x_diag.at[dy], net.device(1, 0))
-                send(("yd", dy), low, y_diag.at[dy], net.device(0, dy))
+                send(("xd", dy), top, x_diag.at[dy - 1], net.device(1, 0))
+                send(("yd", dy), low, y_diag.at[dy - 1], net.device(0, dy))
             elif dx:
                 send(("x", 0), top, x_in.at[0], net.device(1, 0))
             elif dy:
-                send(("y", dy, 1), low, y_in.at[1, dy], net.device(0, dy))
+                send(("y", dy, 1), low, y_in.at[1, dy - 1], net.device(0, dy))
         for dy in dys:
             yield
             sent["xd", dy].wait_recv()
-            top = work.at[dy, :, pl.ds(0, half), :]
-            add_rows(top, [top, x_diag.at[dy]])
-            send(("y", dy, 0), top, y_in.at[0, dy], net.device(0, dy))
-        low = work.at[ny, :, pl.ds(half, half), :]
+            top = work(0, dy, 0, half)
+            add_rows(top, [top, x_diag.at[dy - 1]])
+            send(("y", dy, 0), top, y_in.at[0, dy - 1], net.device(0, dy))
+        low = work(1, 0, half, half)
         for dy in dys:
             yield
             sent["yd", dy].wait_recv()
-            add_rows(low, [low, y_diag.at[dy]])
+            add_rows(low, [low, y_diag.at[dy - 1]])
         send(("x", 1), low, x_in.at[1], net.device(1, 0))
         for h in (0, 1):
             yield
             sent["x", h].wait_recv()
             for dy in dys:
                 sent["y", dy, h].wait_recv()
-            side = pl.ds(h * half, half)
             add_rows(
-                out.at[:, side, :],
-                [work.at[0, :, side, :], x_in.at[h]] + [y_in.at[h, dy] for dy in dys],
+                out.at[:, pl.ds(h * half, half), :],
+                [work(0, 0, h * half, half), x_in.at[h]] + [y_in.at[h, dy - 1] for dy in dys],
             )
         for copy in sent.values():
             copy.wait_send()
@@ -247,15 +263,15 @@
 class LineGather:
     moves = ("x", "line", "c")
 
-    def __init__(self, shards, kinds, nz, ny):
-        self.ins, self.kinds = list(shards), list(kinds)
+    def __init__(self, shards, kinds, nz, ny, share=(0, 1)):
+        self.ins, self.kinds, self.share = list(shards), list(kinds), share
         self.outs, self.scratch = [], []
         for shard, kind in zip(shards, kinds):
             rows, columns = shard.shape
             if kind == "row":
-                shape = (rows * 2 * nz, columns // 2)
+                shape = (rows * 2 * nz, columns // 2 // share[1])
             elif kind == "col":
-                shape = (rows // 2, columns * 2 * nz)
+                shape = (rows // 2 // share[1], columns * 2 * nz)
             else:
                 shape = (rows * 2 * nz, columns)
             self.outs.append((jax.ShapeDtypeStruct(shape, shard.dtype), ANY))
@@ -271,20 +287,22 @@
             rows, columns = shard.shape
 
             if kind == "row":
-                half = columns // 2
-
-                def mine(dx, shard=shard, half=half):
-                    return shard.at[:, pl.ds(pl.multiple_of(net.flip(net.x, dx) * half, half), half)]
+                span = columns // 2 // self.share[1]
+
+                def mine(dx, shard=shard, span=span):
+                    first = (net.flip(net.x, dx) * self.share[1] + self.share[0]) * span
+                    return shard.at[:, pl.ds(pl.multiple_of(first, span), span)]
 
                 def block(line, dx, out=out, rows=rows):
                     first = (line * 2 + net.flip(net.x, dx)) * rows
                     return out.at[pl.ds(pl.multiple_of(first, rows), rows), :]
 
             elif kind == "col":
-                half = rows // 2
-
-                def mine(dx, shard=shard, half=half):
-                    return shard.at[pl.ds(pl.multiple_of(net.flip(net.x, dx) * half, half), half), :]
+                span = rows // 2 // self.share[1]
+
+                def mine(dx, shard=shard, span=span):
+                    first = (net.flip(net.x, dx) * self.share[1] + self.share[0]) * span
+                    return shard.at[pl.ds(pl.multiple_of(first, span), span), :]
 
                 def block(line, dx, out=out, columns=columns):
                     first = (line * 2 + net.flip(net.x, dx)) * columns
@@ -345,8 +363,10 @@
             else:
                 locals_.append(net.copy(mine(0), block(z, 0)))
             locals_[-1].start()
+        yield
+        for copy in locals_:
+            copy.wait()
         for at, kind, mine, block in weights:
-            yield
             swaps[at].wait_recv()
             for up in (True, False):
                 start(at, 1, 1, up, block)
@@ -372,21 +392,19 @@
             pl.when(fits)(copy.wait_send)
         for copy in swaps.values():
             copy.wait_send()
-        for copy in locals_:
-            copy.wait()
 
 
 class LineScatter:
     moves = ("x", "line")
 
-    def __init__(self, parts, kinds, nz, ny):
-        self.ins, self.kinds = list(parts), list(kinds)
+    def __init__(self, parts, kinds, nz, ny, resident=False):
+        self.ins, self.kinds, self.resident = list(parts), list(kinds), resident
         self.outs, self.scratch = [], []
         for part, kind in zip(parts, kinds):
             rows, columns = part.shape
             shape = (rows // (2 * nz), columns) if kind == "row" else (rows, columns // (2 * nz))
             self.outs.append((jax.ShapeDtypeStruct((2,) + shape, BF16), ANY))
-            for lead in (nz, nz, nz, 1):
+            for lead in (nz - 1, nz - 1, 1) + (() if resident else (nz,)):
                 self.scratch.append(pltpu.VMEM((lead, 2) + shape, BF16))
         count = len(self.ins)
         self.remotes = count * (1 + 4 * (nz - 1))
@@ -396,43 +414,53 @@
         nz, z = net.nz, net.z
         sent, loads, stores = [], {}, []
         grads = []
+        each = 3 if self.resident else 4
         for at, (part, out, kind) in enumerate(zip(ins, outs, self.kinds)):
-            work, down, up, mine = scratch[4 * at : 4 * at + 4]
-            _, _, rows, columns = work.shape
+            down, up, mine = scratch[each * at : each * at + 3]
+            _, _, rows, columns = mine.shape
 
             def block(line, dx, part=part, kind=kind, rows=rows, columns=columns):
                 size = rows if kind == "row" else columns
                 first = pl.ds(pl.multiple_of((line * 2 + net.flip(net.x, dx)) * size, size), size)
                 return part.at[first, :] if kind == "row" else part.at[:, first]
 
+            if self.resident:
+                work = block
+            else:
+
+                def work(line, dx, at=at):
+                    return scratch[each * at + 3].at[line, dx]
+
+                order = []
+                for k in range(nz):
+                    order += [k, nz - 1 - k]
+                for line in dict.fromkeys(order):
+                    for dx in (1, 0):
+                        loads[at, line, dx] = net.copy(block(line, dx), work(line, dx))
+                        loads[at, line, dx].start()
             grads.append((at, out, work, down, up, mine))
-            order = []
-            for k in range(nz):
-                order += [k, nz - 1 - k]
-            for line in dict.fromkeys(order):
-                for dx in (1, 0):
-                    loads[at, line, dx] = net.copy(block(line, dx), work.at[line, dx])
-                    loads[at, line, dx].start()
+
+        def inbox(slots, line, dx, toward):
+            return slots.at[line if toward < 0 else line - 1, dx]
 
         for k in range(nz - 1):
             for dx in (1, 0):
                 for at, out, work, down, up, mine in grads:
                     yield
                     for line, slots, toward in ((k, down, -1), (nz - 1 - k, up, 1)):
-                        here, inbox = work.at[line, dx], slots.at[line, dx]
-                        copy = net.remote(
-                            (id(self), at, line, dx, toward), here, inbox, net.device(z=z + toward)
-                        )
+                        here, slot = work(line, dx), inbox(slots, line, dx, toward)
+                        copy = net.remote((id(self), at, line, dx, toward), here, slot, net.device(z=z + toward))
                         first = z == (nz - 1 if toward < 0 else 0)
                         sends = z > line if toward < 0 else z < line
 
-                        def step(copy=copy, here=here, inbox=inbox, first=first, load=loads[at, line, dx]):
-                            load.wait()
+                        def step(copy=copy, here=here, slot=slot, first=first, load=loads.get((at, line, dx))):
+                            if load is not None:
+                                load.wait()
 
                             @pl.when(jnp.logical_not(first))
                             def _():
                                 copy.wait_recv()
-                                add_rows(_lead(here), [_lead(here), _lead(inbox)])
+                                add_rows(_lead(here), [_lead(here), _lead(slot)])
 
                             copy.start()
 
@@ -447,18 +475,15 @@
 
                     @pl.when(z == line)
                     def _(line=line, at=at, total=total, work=work, down=down, up=up):
-                        loads[at, line, dx].wait()
-                        terms = [_lead(work.at[line, dx])]
-                        if line < nz - 1:
-                            net.remote(
-                                (id(self), at, line, dx, -1), total, down.at[line, dx], net.device(z=z - 1)
-                            ).wait_recv()
-                            terms.append(_lead(down.at[line, dx]))
-                        if line > 0:
-                            net.remote(
-                                (id(self), at, line, dx, 1), total, up.at[line, dx], net.device(z=z + 1)
-                            ).wait_recv()
-                            terms.append(_lead(up.at[line, dx]))
+                        if not self.resident:
+                            loads[at, line, dx].wait()
+                        terms = [_lead(work(line, dx))]
+                        for slots, toward in ((down, -1), (up, 1)):
+                            if (line < nz - 1) if toward < 0 else (line > 0):
+                                slot = inbox(slots, line, dx, toward)
+                                key = (id(self), at, line, dx, toward)
+                                net.remote(key, total, slot, net.device(z=z + toward)).wait_recv()
+                                terms.append(_lead(slot))
                         add_rows(_lead(total), terms)
 
                 if dx:
@@ -686,15 +711,12 @@
         out[...] = jnp.sum(line_in[...], axis=0)
 
 
-def exchange(plans, nz, ny, collective_id, name):
+def launch(body, ins, in_specs, outs, scratch, plans, nz, ny, collective_id, name, extra_locals=0, vmem=56):
     moves = set()
     for plan in plans:
         moves |= set(plan.moves)
     remotes = sum(plan.remotes for plan in plans)
-    locals_ = max(1, sum(plan.locals for plan in plans))
-    ins = [array for plan in plans for array in plan.ins]
-    outs = [out for plan in plans for out in plan.outs]
-    scratch = [entry for plan in plans for entry in plan.scratch]
+    locals_ = max(1, extra_locals + sum(plan.locals for plan in plans))
 
     def kernel(*refs):
         in_refs, refs = refs[: len(ins)], refs[len(ins) :]
@@ -728,6 +750,34 @@
         for device in peers.values():
             pl.semaphore_signal(barrier, inc=1, device_id=device, device_id_type=MESH)
         pl.semaphore_wait(barrier, len(peers))
+        body(net, in_refs, out_refs, scratch_refs)
+
+    return list(
+        pl.pallas_call(
+            kernel,
+            out_shape=[shape for shape, _ in outs],
+            in_specs=in_specs,
+            out_specs=[spec for _, spec in outs],
+            scratch_shapes=list(scratch)
+            + [
+                pltpu.SemaphoreType.DMA((remotes,)),
+                pltpu.SemaphoreType.DMA((remotes,)),
+                pltpu.SemaphoreType.DMA((locals_,)),
+            ],
+            compiler_params=pltpu.CompilerParams(
+                collective_id=collective_id, has_side_effects=True, vmem_limit_bytes=vmem << 20
+            ),
+            name=name,
+        )(*ins)
+    )
+
+
+def exchange(plans, nz, ny, collective_id, name):
+    ins = [array for plan in plans for array in plan.ins]
+    outs = [out for plan in plans for out in plan.outs]
+    scratch = [entry for plan in plans for entry in plan.scratch]
+
+    def body(net, in_refs, out_refs, scratch_refs):
         running = []
         for plan in plans:
             mine = []
@@ -744,28 +794,303 @@
                 except StopIteration:
                     running.remove(steps)
 
-    results = pl.pallas_call(
-        kernel,
-        out_shape=[shape for shape, _ in outs],
-        in_specs=[ANY] * len(ins),
-        out_specs=[spec for _, spec in outs],
-        scratch_shapes=scratch
-        + [
-            pltpu.SemaphoreType.DMA((remotes,)),
-            pltpu.SemaphoreType.DMA((remotes,)),
-            pltpu.SemaphoreType.DMA((locals_,)),
-        ],
-        compiler_params=pltpu.CompilerParams(
-            collective_id=collective_id, has_side_effects=True, vmem_limit_bytes=56 << 20
-        ),
-        name=name,
-    )(*ins)
-    results = list(results)
+    results = launch(body, ins, [ANY] * len(ins), outs, scratch, plans, nz, ny, collective_id, name)
     grouped = []
     for plan in plans:
         grouped.append(results[: len(plan.outs)])
         results = results[len(plan.outs) :]
     return grouped
+
+
+def drive(steps, actions):
+    actions = list(actions)
+    for _ in steps:
+        if actions:
+            action = actions.pop(0)
+            if action is not None:
+                action()
+    for action in actions:
+        if action is not None:
+            action()
+
+
+def loop(count, body):
+    def step(at, carry):
+        body(at)
+        return carry
+
+    lax.fori_loop(0, count, step, 0)
+
+
+def mlp_block(mixed, wo, inputs, cotangent, cot_face, norms, wexp_first, w_expand, w_reduce, nz, ny, collective_id):
+    micro_count, own_rows, width = inputs.shape
+    face_rows = cot_face.shape[1]
+    tokens = micro_count * face_rows
+    attn = mixed.shape[1]
+    units = w_expand.shape[1] // 2
+    half = units // 2
+    tile = min(512, half)
+    wide = 512
+    part = jax.ShapeDtypeStruct((micro_count, face_rows, width), BF16)
+    part_red = jax.ShapeDtypeStruct((units, width), BF16)
+    own = (micro_count, own_rows, width)
+    scatter_a, scatter_b = (FaceScatter(part, nz, ny, resident=True) for _ in range(2))
+    gather = FaceGather(jax.ShapeDtypeStruct(own, BF16), nz, ny)
+    line_e = LineGather([w_expand], ["row"], nz, ny, share=(1, 2))
+    line_r = LineGather([w_reduce], ["col"], nz, ny)
+    line_s = LineScatter([part_red], ["col"], nz, ny, resident=True)
+    plans = [scatter_a, scatter_b, gather, line_e, line_r, line_s]
+    vmem = pl.BlockSpec(memory_space=pltpu.VMEM)
+    outs = [
+        (jax.ShapeDtypeStruct(own, F32), ANY),
+        (jax.ShapeDtypeStruct(own, F32), ANY),
+        (jax.ShapeDtypeStruct(own, BF16), ANY),
+        (jax.ShapeDtypeStruct((2, 16, width), F32), vmem),
+        (jax.ShapeDtypeStruct((width, half), BF16), ANY),
+        (jax.ShapeDtypeStruct((width, half), BF16), ANY),
+        (part, ANY),
+    ] + line_s.outs
+    scratch = [
+        pltpu.VMEM((micro_count, face_rows, width), BF16),
+        pltpu.VMEM(own, F32),
+        pltpu.VMEM(own, F32),
+        pltpu.VMEM(own, BF16),
+        pltpu.VMEM(own, BF16),
+        pltpu.VMEM(own, BF16),
+        pltpu.VMEM((micro_count, face_rows, width), BF16),
+        pltpu.VMEM((micro_count, face_rows, width), BF16),
+        pltpu.VMEM((width, half), BF16),
+        pltpu.VMEM((width, half), BF16),
+        pltpu.VMEM((units, width), BF16),
+        pltpu.VMEM((tokens, units), BF16),
+        pltpu.VMEM((tokens, units), BF16),
+        pltpu.VMEM((units, width), BF16),
+        pltpu.VMEM((tokens, attn), BF16),
+        pltpu.VMEM((attn, width), BF16),
+    ]
+    shared = len(scratch)
+    scratch += scatter_a.scratch + line_s.scratch
+
+    def body(net, ins, outs, scratch):
+        mixed_in, wo_in, own_in, cot_in, face_in, norms, first_in, expand_in, reduce_in = ins
+        middle_out, grad_out, low_out, norm_out, expand_a, expand_b, reduced_out, reduce_out = outs
+        p, branch, middle, own, cot_own, n_own, n_face, cot, we0, we1, wr, active, slope, pr, mixed, wo = scratch[:shared]
+        we = (we0, we1)
+        slots = list(scratch[shared : shared + len(scatter_a.scratch)])
+        line_slots = list(scratch[shared + len(scatter_a.scratch) :])
+
+        loads = [
+            net.copy(*pair)
+            for pair in (
+                (mixed_in, mixed),
+                (wo_in, wo),
+                (own_in, own),
+                (cot_in, cot_own),
+                (first_in, we0),
+                (face_in, cot),
+            )
+        ]
+        e = line_e.run(net, [expand_in], [we1], [])
+        r = line_r.run(net, [reduce_in], [wr], [])
+        queue = []
+
+        def tick(count=1):
+            def act():
+                for _ in range(count):
+                    if queue:
+                        next(queue.pop(0), None)
+
+            return act
+
+        next(e)
+        for load in loads:
+            load.start()
+        queue += [e, r, e, e, r, e, e, r, r, e, e, r, r, r, r]
+        loads[0].wait()
+        loads[1].wait()
+
+        def branch_tile(at):
+            m, n = lax.div(at, width // wide), lax.rem(at, width // wide)
+            columns = pl.ds(pl.multiple_of(n * wide, wide), wide)
+            rows = pl.ds(pl.multiple_of(m * face_rows, face_rows), face_rows)
+            p[m, :, columns] = jnp.dot(mixed[rows, :], wo[:, columns], preferred_element_type=F32).astype(BF16)
+
+        loop(micro_count * (width // wide), branch_tile)
+        tick(2)()
+        drive(
+            scatter_a.run(net, [p], [branch], slots),
+            [None, None, None, None, tick(2), None, tick(1), None],
+        )
+        loads[2].wait()
+        row_steps = own_rows // 16
+
+        def own_rows_at(at):
+            return lax.div(at, row_steps), pl.ds(pl.multiple_of(lax.rem(at, row_steps) * 16, 16), 16)
+
+        def norm_rows(at):
+            m, rows = own_rows_at(at)
+            values = own[m, rows, :].astype(F32) + branch[m, rows, :]
+            middle[m, rows, :] = values
+            centered = values - jnp.mean(values, axis=-1, keepdims=True)
+            spread = lax.rsqrt(jnp.mean(centered * centered, axis=-1, keepdims=True) + EPSILON)
+            n_own[m, rows, :] = (centered * spread * norms[0:1, :] + norms[1:2, :]).astype(BF16)
+
+        loop(micro_count * row_steps, norm_rows)
+        keep_middle = net.copy(middle, middle_out)
+        keep_middle.start()
+        drive(
+            gather.run(net, [n_own], [n_face], []),
+            [tick(2), tick(1), tick(1), tick(2), None, None, None],
+        )
+        loads[4].wait()
+
+        def hidden_tile(h):
+            def tile_at(at):
+                m, n = lax.div(at, half // tile), lax.rem(at, half // tile)
+                rows = pl.ds(pl.multiple_of(m * face_rows, face_rows), face_rows)
+                columns = pl.ds(pl.multiple_of(n * tile, tile), tile)
+                into = pl.ds(pl.multiple_of(h * half + n * tile, tile), tile)
+                hidden = jnp.dot(n_face[m], we[h][:, columns], preferred_element_type=F32)
+                square = hidden * hidden
+                bend = jnp.tanh(GELU_A * hidden * (1.0 + GELU_B * square))
+                active[rows, into] = (0.5 * hidden * (1.0 + bend)).astype(BF16)
+                slope[rows, into] = (
+                    0.5 * (1.0 + bend)
+                    + (0.5 * GELU_A) * hidden * (1.0 - bend * bend) * (1.0 + (3.0 * GELU_B) * square)
+                ).astype(BF16)
+
+            return tile_at
+
+        across = (((0,), (0,)), ((), ()))
+        along = (((1,), (1,)), ((), ()))
+        loop(micro_count * (half // tile), hidden_tile(0))
+        tick(1)()
+        loop(micro_count * (half // tile), hidden_tile(1))
+        tick(1)()
+        loads[5].wait()
+
+        def reduce_tile(first):
+            def tile_at(at):
+                f, n = lax.div(at, width // wide), lax.rem(at, width // wide)
+                columns = pl.ds(pl.multiple_of(n * wide, wide), wide)
+                rows = pl.ds(pl.multiple_of(first + f * tile, tile), tile)
+                pr[rows, columns] = lax.dot_general(
+                    active[:, rows],
+                    cot[:, :, columns].reshape(tokens, wide),
+                    across,
+                    preferred_element_type=F32,
+                ).astype(BF16)
+
+            return tile_at
+
+        loop((half // tile) * (width // wide), reduce_tile(0))
+        tick(1)()
+        loop((half // tile) * (width // wide), reduce_tile(half))
+        s = line_s.run(net, [pr], [reduce_out], line_slots)
+        tick(9)()
+        queue.extend([s] * 40)
+        tick(1)()
+
+        def slope_tile(at):
+            m, n = lax.div(at, units // tile), lax.rem(at, units // tile)
+            rows = pl.ds(pl.multiple_of(m * face_rows, face_rows), face_rows)
+            columns = pl.ds(pl.multiple_of(n * tile, tile), tile)
+            grad = lax.dot_general(cot[m], wr[columns, :], along, preferred_element_type=F32)
+            slope[rows, columns] = (grad * slope[rows, columns].astype(F32)).astype(BF16)
+
+        def normed_tile(at):
+            m, n = lax.div(at, width // wide), lax.rem(at, width // wide)
+            rows = pl.ds(pl.multiple_of(m * face_rows, face_rows), face_rows)
+            columns = pl.ds(pl.multiple_of(n * wide, wide), wide)
+            grad = lax.dot_general(slope[rows, :half], we0[columns, :], along, preferred_element_type=F32)
+            grad = grad + lax.dot_general(slope[rows, half:], we1[columns, :], along, preferred_element_type=F32)
+            p[m, :, columns] = grad.astype(BF16)
+
+        loop(micro_count * (units // tile), slope_tile)
+        tick(1)()
+        loop(micro_count * (width // wide), normed_tile)
+        tick(1)()
+        for steps in (e, r):
+            for _ in steps:
+                pass
+        stores = []
+
+        def reduced_tiles():
+            def tile_at(at):
+                m, n = lax.div(at, width // wide), lax.rem(at, width // wide)
+                rows = pl.ds(pl.multiple_of(m * face_rows, face_rows), face_rows)
+                columns = pl.ds(pl.multiple_of(n * wide, wide), wide)
+                cot[m, :, columns] = jnp.dot(active[rows, :], wr[:, columns], preferred_element_type=F32).astype(BF16)
+
+            loop(micro_count * (width // wide), tile_at)
+            stores.append(net.copy(cot, reduced_out))
+            stores[-1].start()
+
+        def expand_tiles():
+            for h in (0, 1):
+
+                def tile_at(at, h=h):
+                    k, n = lax.div(at, half // tile), lax.rem(at, half // tile)
+                    rows = pl.ds(pl.multiple_of(k * wide, wide), wide)
+                    columns = pl.ds(pl.multiple_of(n * tile, tile), tile)
+                    grads = pl.ds(pl.multiple_of(h * half + n * tile, tile), tile)
+                    we[h][rows, columns] = lax.dot_general(
+                        n_face[:, :, rows].reshape(tokens, wide),
+                        slope[:, grads],
+                        across,
+                        preferred_element_type=F32,
+                    ).astype(BF16)
+
+                loop((width // wide) * (half // tile), tile_at)
+                stores.append(net.copy(we[h], (expand_a, expand_b)[h]))
+                stores[-1].start()
+
+        def do(*actions):
+            def act():
+                for action in actions:
+                    action()
+
+            return act
+
+        drive(
+            scatter_b.run(net, [p], [branch], slots),
+            [None, None, None, None, expand_tiles, tick(1), do(tick(1), reduced_tiles, tick(1)), None],
+        )
+        loads[3].wait()
+        keep_middle.wait()
+        norm_out[...] = jnp.zeros_like(norm_out)
+
+        def back_rows(at):
+            m, rows = own_rows_at(at)
+            values = middle[m, rows, :]
+            centered = values - jnp.mean(values, axis=-1, keepdims=True)
+            spread = lax.rsqrt(jnp.mean(centered * centered, axis=-1, keepdims=True) + EPSILON)
+            unit = centered * spread
+            grad = branch[m, rows, :]
+            norm_out[0] += grad * unit
+            norm_out[1] += grad
+            turned = grad * norms[0:1, :]
+            inner = jnp.mean(turned * unit, axis=-1, keepdims=True)
+            total = cot_own[m, rows, :].astype(F32) + spread * (
+                turned - jnp.mean(turned, axis=-1, keepdims=True) - unit * inner
+            )
+            middle[m, rows, :] = total
+            n_own[m, rows, :] = total.astype(BF16)
+
+        loop(micro_count * row_steps, back_rows)
+        for pair in ((middle, grad_out), (n_own, low_out)):
+            stores.append(net.copy(*pair))
+            stores[-1].start()
+        for _ in s:
+            pass
+        for store in stores:
+            store.wait()
+
+    ins = [mixed, wo, inputs, cotangent, cot_face, norms, wexp_first, w_expand, w_reduce]
+    specs = [ANY] * 5 + [vmem] + [ANY] * 3
+    return launch(
+        body, ins, specs, outs, scratch, plans, nz, ny, collective_id, "mlp_block", extra_locals=12, vmem=62
+    )
 
 
 def masked_scores(queries, keys, query_doc, key_doc, scale):
@@ -954,22 +1279,30 @@
 
     norms = jnp.stack([attn_gain, attn_shift, mlp_gain, mlp_shift])
     norms = jnp.concatenate([norms, jnp.zeros((4, norms.shape[1]), BF16)])
-    (face_in,), (wq, wo, wkv), (norms,) = swap(
+    (wq, wo, wkv), (norms,), (face_in,) = swap(
         [
-            FaceGather(inputs, *on),
             LineGather([w_query, w_attn_out, w_keyval], ["row", "col", "both"], *on),
             PlaneGather(norms, *on),
+            FaceGather(inputs, *on, hold_x=True),
         ],
         collective_id=1,
         name="gather_attention",
     )
     norms = norms[:, :4].transpose(1, 0, 2).reshape(4, width).astype(F32)
-    gain_one, shift_one, gain_two, shift_two = norms[0], norms[1], norms[2], norms[3]
+    gain_one, shift_one = norms[0], norms[1]
 
     normed = layer_norm(face_in.astype(F32), gain_one, shift_one).astype(BF16).reshape(tokens, width)
     queries = dot(normed, wq).astype(BF16).reshape(micro_count, face_rows, heads * head_dim)
     keys_face = dot(normed, wkv).astype(BF16).reshape(micro_count, face_rows, 2 * head_dim)
-    ((keys_vals,),) = swap([KeysGather(keys_face, *on)], collective_id=2, name="gather_keys")
+    (keys_vals,), (wexp_first,), (cot_face,) = swap(
+        [
+            KeysGather(keys_face, *on),
+            LineGather([w_expand], ["row"], *on, share=(0, 2)),
+            FaceGather(cotangent, *on, hold_x=True),
+        ],
+        collective_id=2,
+        name="gather_keys",
+    )
 
     query_doc = lax.dynamic_slice_in_dim(doc_ids, z * face_rows, face_rows, axis=1)
     blocks = face_rows // BLOCK
@@ -982,41 +1315,16 @@
     mixed, log_total = attend_forward(queries, keys_vals, *docs)
     mixed_flat = mixed.reshape(tokens, heads * head_dim)
 
-    branch = dot(mixed_flat, wo).astype(BF16).reshape(micro_count, face_rows, width)
-    (branch,), (cot_face,), (wexp,) = swap(
-        [FaceScatter(branch, *on), FaceGather(cotangent, *on), LineGather([w_expand], ["row"], *on)],
-        collective_id=3,
-        name="scatter_branch",
+    own_in = inputs.astype(F32)
+    middle, grad_middle, low_middle, grad_norm_two, part_expand_a, part_expand_b, reduced, grad_reduce = mlp_block(
+        mixed_flat, wo, inputs, cotangent, cot_face, norms[2:], wexp_first, w_expand, w_reduce, *on, collective_id=3
     )
-    own_in = inputs.astype(F32)
-    middle = own_in + branch
-    normed_two_full, norm_pull_two = jax.vjp(layer_norm, middle, gain_two, shift_two)
-    (normed_two,), (wred,) = swap(
-        [FaceGather(normed_two_full.astype(BF16), *on), LineGather([w_reduce], ["col"], *on)],
-        collective_id=4,
-        name="gather_normed_two",
-    )
-    normed_two = normed_two.reshape(tokens, width)
-    cot_flat = cot_face.reshape(tokens, width)
-    gelu_value, gelu_pull = jax.vjp(gelu_tanh, dot(normed_two, wexp))
-    active = gelu_value.astype(BF16)
-    part_reduce = dot_at(active, cot_flat).astype(BF16)
-    grad_hidden = gelu_pull(dot_bt(cot_flat, wred))[0].astype(BF16)
-    grad_normed_two = dot_bt(grad_hidden, wexp).astype(BF16).reshape(micro_count, face_rows, width)
-    part_expand = dot_at(normed_two, grad_hidden).astype(BF16)
-    reduced = dot(active, wred).astype(BF16).reshape(micro_count, face_rows, width)
-    (grad_normed_two,), (grad_reduce,) = swap(
-        [FaceScatter(grad_normed_two, *on), LineScatter([part_reduce], ["col"], *on)],
-        collective_id=5,
-        name="scatter_normed_two",
-    )
-    grad_mid_norm, grad_gain_two, grad_shift_two = norm_pull_two(grad_normed_two)
-    grad_middle = cotangent.astype(F32) + grad_mid_norm
-    (grad_branch,), (reduced,), (grad_expand,) = swap(
+    grad_gain_two, grad_shift_two = jnp.sum(grad_norm_two, axis=1)
+    (grad_branch,), (reduced,), (grad_expand_a, grad_expand_b) = swap(
         [
-            FaceGather(grad_middle.astype(BF16), *on),
+            FaceGather(low_middle, *on),
             FaceScatter(reduced, *on),
-            LineScatter([part_expand], ["row"], *on),
+            LineScatter([part_expand_a, part_expand_b], ["row", "row"], *on),
         ],
         collective_id=6,
         name="gather_branch",
@@ -1070,7 +1378,7 @@
         by_column(grad_attn_out),
         small[2],
         small[3],
-        by_row(grad_expand),
+        by_row(jnp.concatenate([grad_expand_a, grad_expand_b], axis=2)),
         by_column(grad_reduce),
     )
 

time: 767 us -> 667 us (0.87)
  matrix products: 96.7 us -> 21.8 us
  Pallas kernels: 616 us -> 601 us
  other arithmetic: 29.6 us -> 16.7 us
    dot_general x5 -> x2, matrix products: 35.8 us -> 6.1 us  [dot(): return jnp.dot(a, b, preferred_element_type=F32)]
    dot_general x5 -> x3, matrix products: 32.4 us -> 8.48 us  [dot_bt(): lax.dot_general(a, b, (((1,), (1,)), ((), ())), preferred_element_type=F32)]
    dot_general x5 -> x3, matrix products: 28.5 us -> 7.24 us  [dot_at(): lax.dot_general(a, b, (((0,), (0,)), ((), ())), preferred_element_type=F32)]
    pallas_call x8 -> x6, Pallas kernels: 598 us -> 583 us  [launch(): pl.pallas_call(kernel, out_shape=[shape for shape, _ in outs], in_specs=i...]
where the time goes in v2:
time: 667 us; the launch traced here: 659 us
  Pallas kernels  601 us (90%)
  matrix products  21.8 us (3%)
  local copies, waits for them, and re-layouts  18.1 us (3%)
  other arithmetic  16.7 us (3%)
    pallas_call x6, Pallas kernels, launch(): pl.pallas_call(kernel, out_shape=[shape for shape, _ in outs], in_specs=i...  583 us

profile of v2, /device:TPU:0, one launch (start us, length us, event | category | flops | bytes accessed | tf_op | source)
XLA Modules:
  0.0 659.3 jit_solution(4836708613940586365)
XLA Ops:
  0.7 0.7 fusion.44
  1.4 0.3 copy.36.qd_ref
  1.7 0.7 constant_dynamic-slice_fusion
  2.5 0.8 slice.53
  3.3 0.2 fusion.29
  3.9 0.7 stack.32
  4.6 0.7 stack.33
  5.2 0.7 stack.34
  5.9 0.7 stack.35
  6.5 0.6 concatenate.13.refs_3_
  7.2 63.4 %gather_attention.1 = (bf16[2048,256]{1,0:T(8,128)(2,1)}, bf16[256,2048]{1,0:T(8,128)(2,1)}, bf16[2048,256]{1,0:T(8,128)(2,1)}, bf16[8,8,256]{2,1,0:T(8,128)(2,1)}, bf16[3,512,2048]{2,1,0:T(8,128)(2,1)}) custom-call(bf16[256,512]{1,0:T(8,128)(2,1)} %refs_0_.1, bf16[512,256]{1,0:T(8,128)(2,1)} %refs_1_.2, bf16[256,256]{1,0:T(8,128)(2,1)} %refs_2_.3, ...), custom_call_target="tpu_custom_call" | custom-call | tf_op jit(solution)/shard_map/gather_attention/pallas_call | solution.py:756
  70.6 3.8 convert_reduce_fusion
  74.4 0.8 copy-done.7
  75.2 1.8 fusion.2
  77.0 2.8 fusion.5
  79.8 2.9 convolution_convert_fusion.2
  82.8 66.7 %gather_keys.1 = (bf16[3,2048,256]{2,1,0:T(8,128)(2,1)}, bf16[2048,512]{1,0:T(8,128)(2,1)}, bf16[3,512,2048]{2,1,0:T(8,128)(2,1)}) custom-call(bf16[3,512,256]{2,1,0:T(8,128)(2,1)} %bitcast.87, bf16[256,2048]{1,0:T(8,128)(2,1)} %refs_7_.1, bf16[3,64,2048]{2,1,0:T(8,128)(2,1)} %refs_3_.1), custom_call_target="tpu_custom_call" | custom-call | tf_op jit(solution)/shard_map/gather_keys/pallas_call | solution.py:756
  149.5 3.2 convolution_convert_fusion.3
  152.7 8.1 %attend_forward.1 = (bf16[3,512,256]{2,1,0:T(8,128)(2,1)S(1)}, f32[3,2,512,1]{3,2,1,0:T(8,128)S(1)}) custom-call(s32[12]{0:T(128)S(1)} %reshape.121.bounds_ref, bf16[3,512,256]{2,1,0:T(8,128)(2,1)S(1)} %bitcast.73, bf16[3,2048,256]{2,1,0:T(8,128)(2,1)S(1)} %copy-done, s32[3,512,1]{2,1,0:T(8,128)S(1)} %copy.36.qd_ref, s32[3,1,2048]{2,1,0:T(1,128)S(1)} %broadcast_in_dim.23.kd_ref), custom_call_target="tpu_custom_call" | custom-call | tf_op jit(solution)/shard_map/attend_forward/pallas_call | solution.py:1141
  160.9 0.9 copy-done.2
  161.8 1.1 copy-done.5
  162.9 0.6 slice.70
  163.5 204.4 %mlp_block.1 = (f32[3,64,2048]{2,1,0:T(8,128)}, f32[3,64,2048]{2,1,0:T(8,128)}, bf16[3,64,2048]{2,1,0:T(8,128)(2,1)}, f32[2,16,2048]{2,1,0:T(8,128)}, bf16[2048,...) custom-call(bf16[1536,256]{1,0:T(8,128)(2,1)} %bitcast.72, ...), custom_call_target="tpu_custom_call" | custom-call | tf_op jit(solution)/shard_map/mlp_block/pallas_call | solution.py:756
  367.9 115.9 %gather_branch.1 = (bf16[3,512,2048]{2,1,0:T(8,128)(2,1)}, f32[3,64,2048]{2,1,0:T(8,128)}, bf16[2,256,512]{2,1,0:T(8,128)(2,1)}, bf16[2,256,512]{2,1,0:T(8,128)(2,1)}) custom-call(bf16[3,64,2048]{2,1,0:T(8,128)(2,1)} %get-tuple-element.51.refs_0_, bf16[3,512,2048]{2,1,0:T(8,128)(2,1)} %get-tuple-element.52.refs_1_, ...), custom_call_target="tpu_custom_call" | custom-call | tf_op jit(solution)/shard_map/gather_branch/pallas_call | solution.py:756
  483.8 1.2 constant_dynamic-update-slice_fusion.1
  485.0 1.3 constant_dynamic-update-slice_fusion
  486.4 1.6 maximum_convert_fusion
  487.9 0.8 copy-done.10
  488.8 1.8 convolution_convert_fusion.1
  490.6 0.2 copy-done.1
  491.0 0.5 copy-done.6
  491.5 9.6 %attend_backward.1 = (bf16[3,512,256]{2,1,0:T(8,128)(2,1)S(1)}, bf16[3,2048,256]{2,1,0:T(8,128)(2,1)S(1)}) custom-call(s32[12]{0:T(128)S(1)} %reshape.121.bounds_ref, bf16[3,512,256]{2,1,0:T(8,128)(2,1)S(1)} %bitcast.74, bf16[3,2048,256]{2,1,0:T(8,128)(2,1)S(1)} %copy-done.1, bf16[3,512,256]{2,1,0:T(8,128)(2,1)S(1)} %copy-done.3, ...), custom_call_target="tpu_custom_call" | custom-call | tf_op jit(solution)/shard_map/attend_backward/pallas_call | solution.py:1217
  501.2 2.9 fusion.7.refs_3_
  504.1 2.8 fusion.6.refs_2_
  506.9 4.5 convolution_convert_fusion
  511.4 110.6 %scatter_query.1 = (f32[3,64,2048]{2,1,0:T(8,128)}, f32[3,64,256]{2,1,0:T(8,128)}, bf16[2,256,256]{2,1,0:T(8,128)(2,1)}, bf16[2,256,256]{2,1,0:T(8,128)(2,1)}) custom-call(bf16[3,512,2048]{2,1,0:T(8,128)(2,1)} %bitcast.78, bf16[12,512,256]{2,1,0:T(8,128)(2,1)} %bitcast.75, bf16[256,2048]{1,0:T(8,128)(2,1)} %fusion.6.refs_2_, bf16[2048,256]{1,0:T(8,128)(2,1)} %fusion.7.refs_3_), custom_call_target="tpu_custom_call" | custom-call | tf_op jit(solution)/shard_map/scatter_query/pallas_call | solution.py:756
  622.0 1.1 slice_bitcast_fusion.3
  623.2 0.9 maximum_convert_fusion.1
  624.2 2.1 fusion.18
  626.4 0.8 fusion.17
  627.6 0.7 pad.4.refs_1_
  628.3 1.6 fusion.8
  629.9 22.4 %scatter_small.1 = (f32[1,64,256]{2,1,0:T(8,128)}, f32[8,128]{1,0:T(8,128)}) custom-call(bf16[4,512,256]{2,1,0:T(8,128)(2,1)} %bitcast.86, f32[8,4,8,128]{3,2,1,0:T(8,128)} %pad.4.refs_1_), custom_call_target="tpu_custom_call" | custom-call | tf_op jit(solution)/shard_map/scatter_small/pallas_call | solution.py:756
  652.3 1.4 slice_bitcast_fusion.4
  653.7 2.2 add_add_fusion.1
  655.8 0.8 bitcast_convert_fusion.1
  656.7 1.5 bitcast_convert_fusion
  658.2 0.6 copy.47
  (80 shorter events, 1.5 us)
Async XLA Ops:
  70.6 4.6 copy-start.7
  75.2 1.8 copy-start.24
  77.0 2.8 copy-start.16
  79.8 69.7 %copy-start.9 = (bf16[3,512,2048]{2,1,0:T(8,128)(2,1)}, bf16[3,512,2048]{2,1,0:T(8,128)(2,1)S(1)}, u32[]{:S(2)}) copy-start(bf16[3,512,2048]{2,1,0:T(8,128)(2,1)S(1)} %fusion.5) | copy-start | bytes 18874372
  149.5 3.2 copy-start.22
  149.5 3.2 copy-start
  160.9 0.9 copy-start.2
  161.8 1.1 copy-start.5
  483.8 4.1 copy-start.18
  485.0 3.7 copy-start.10
  486.4 14.8 %slice-start = ((s8[6291456]{0:T(1024)(128)(4,1)}), s8[4194304]{0:T(1024)(128)(4,1)S(1)}, s32[]{:S(2)}) async-start(s8[6291456]{0:T(1024)(128)(4,1)} %bitcast.81), calls=%async_computation | async-start | bytes 8388608
  488.8 2.0 copy-start.1
  488.8 2.2 copy-start.3
  488.8 2.7 copy-start.6
  488.8 12.4 %slice-start.1 = ((s8[6291456]{0:T(1024)(128)(4,1)}), s8[2097152]{0:T(1024)(128)(4,1)S(1)}, s32[]{:S(2)}) async-start(s8[6291456]{0:T(1024)(128)(4,1)} %bitcast.81), calls=%async_computation.1 | async-start | bytes 4194304
  491.5 12.6 %slice-start.2 = ((s8[6291456]{0:T(1024)(128)(4,1)}), s8[4194304]{0:T(1024)(128)(4,1)S(1)}, s32[]{:S(2)}) async-start(s8[6291456]{0:T(1024)(128)(4,1)} %bitcast.84), calls=%async_computation.2 | async-start | bytes 8388608
  501.2 2.9 copy-start.4
  501.2 2.9 slice-start.3
  504.1 2.8 copy-start.15
  622.0 2.0 copy-start.8
  622.0 2.2 copy-start.17
  622.0 2.2 copy-start.21
  626.4 1.0 copy-start.20
  628.3 25.3 %copy-start.11 = (f32[3,64,2048]{2,1,0:T(8,128)S(1)}, f32[3,64,2048]{2,1,0:T(8,128)}, u32[]{:S(2)}) copy-start(f32[3,64,2048]{2,1,0:T(8,128)} %get-tuple-element.50) | copy-start | bytes 4718596
  628.3 25.3 %copy-start.12 = (f32[3,64,2048]{2,1,0:T(8,128)S(1)}, f32[3,64,2048]{2,1,0:T(8,128)}, u32[]{:S(2)}) copy-start(f32[3,64,2048]{2,1,0:T(8,128)} %get-tuple-element.56) | copy-start | bytes 4718596
  628.3 25.3 %copy-start.13 = (f32[3,64,2048]{2,1,0:T(8,128)S(1)}, f32[3,64,2048]{2,1,0:T(8,128)}, u32[]{:S(2)}) copy-start(f32[3,64,2048]{2,1,0:T(8,128)} %get-tuple-element.55) | copy-start | bytes 4718596
  653.6 2.2 copy-start.19
  653.6 3.0 copy-start.14
  656.7 1.6 copy-start.23

commit v3 on v2

--- a/solution.py
+++ b/solution.py
@@ -13,8 +13,12 @@
 NEG_FILL = -1e30
 GELU_A = math.sqrt(2.0 / math.pi)
 GELU_B = 0.044715
+LOG2_E = 1.0 / math.log(2.0)
+K1_ORDER = (0, 2, 1, 2, 0, 2, 3, 0, 0, 0, 0, 0, 2, 0, 0, 2, 0, 1, 0, 0, 2, 2, 2, 0, 0, 0, 0, 0, 0, 2)
+K2_ORDER = (0, 2, 2, 1, 0, 1, 1, 2, 2, 2, 0, 2, 0, 1, 2)
 MESH = pl.DeviceIdType.MESH
 ANY = pl.BlockSpec(memory_space=pl.ANY)
+IN_VMEM = pl.BlockSpec(memory_space=pltpu.VMEM)
 BF16 = jnp.bfloat16
 F32 = jnp.float32
 
@@ -72,10 +76,16 @@
             device_id_type=MESH,
         )
 
+    def take_locals(self, count):
+        first = self.used[1]
+        self.used[1] += count
+        return first
+
+    def copy_at(self, at, src, dst):
+        return pltpu.make_async_copy(src, dst, self.local.at[at])
+
     def copy(self, src, dst):
-        at = self.used[1]
-        self.used[1] += 1
-        return pltpu.make_async_copy(src, dst, self.local.at[at])
+        return self.copy_at(self.take_locals(1), src, dst)
 
 
 def add_rows(dst, terms):
@@ -96,6 +106,7 @@
 
 class FaceGather:
     moves = ("x", "y", "c")
+    in_spec = IN_VMEM
 
     def __init__(self, own, nz, ny, hold_x=False):
         self.ins, self.hold_x = [own], hold_x
@@ -139,23 +150,30 @@
         def share(key, dx, dy, h):
             send(("c",) + key, piece(dx, dy, h), piece(dx, dy, h), net.device(0, 0, 1))
 
-        yield
-        sent["x", 0].wait_recv()
-        for dy in dys:
-            send(("xy", dy), piece(1, 0, 0), piece(1, 0, 0), net.device(0, dy))
-        share(("x", 0), 1, 0, 0)
-        for dy in dys:
-            yield
-            sent["y", dy, 1].wait_recv()
-            send(("yx", dy), piece(0, -dy % net.ny, 1), piece(0, -dy % net.ny, 1), net.device(1, 0))
-            share(("y", dy, 1), 0, -dy % net.ny, 1)
-        yield
-        sent["x", 1].wait_recv()
-        share(("x", 1), 1, 0, 1)
-        for dy in dys:
-            yield
-            sent["y", dy, 0].wait_recv()
-            share(("y", dy, 0), 0, -dy % net.ny, 0)
+        def from_x(h):
+            sent["x", h].wait_recv()
+            if not h:
+                for dy in dys:
+                    send(("xy", dy), piece(1, 0, 0), piece(1, 0, 0), net.device(0, dy))
+            share(("x", h), 1, 0, h)
+
+        def from_y(dy, h):
+            sent["y", dy, h].wait_recv()
+            if h:
+                send(("yx", dy), piece(0, -dy % net.ny, 1), piece(0, -dy % net.ny, 1), net.device(1, 0))
+            share(("y", dy, h), 0, -dy % net.ny, h)
+
+        arrivals = []
+        for first in (True, False):
+            on_x = [functools.partial(from_x, 0 if first else 1)]
+            on_y = [functools.partial(from_y, dy, 1 if first else 0) for dy in dys]
+            arrivals.append(on_x + on_y)
+        if self.hold_x:
+            arrivals = [arrivals[0][1:], arrivals[1][1:], arrivals[0][:1], arrivals[1][:1]]
+        for group in arrivals:
+            for arrive in group:
+                yield
+                arrive()
         for dy in dys:
             yield
             sent["xy", dy].wait_recv()
@@ -262,9 +280,10 @@
 
 class LineGather:
     moves = ("x", "line", "c")
-
-    def __init__(self, shards, kinds, nz, ny, share=(0, 1)):
-        self.ins, self.kinds, self.share = list(shards), list(kinds), share
+    in_spec = IN_VMEM
+
+    def __init__(self, shards, kinds, nz, ny, share=(0, 1), given=()):
+        self.ins, self.kinds, self.share = list(shards) + list(given), list(kinds), share
         self.outs, self.scratch = [], []
         for shard, kind in zip(shards, kinds):
             rows, columns = shard.shape
@@ -275,14 +294,15 @@
             else:
                 shape = (rows * 2 * nz, columns)
             self.outs.append((jax.ShapeDtypeStruct(shape, shard.dtype), ANY))
-        count = len(self.ins)
+        count = len(self.kinds)
         self.remotes = count * (1 + 4 * (nz - 1)) + kinds.count("both") * (1 + 4 * (nz - 1))
-        self.locals = count
+        self.locals = 2 * count
 
     def run(self, net, ins, outs, scratch):
         nz, z = net.nz, net.z
         sent, locals_, shared = [], [], []
         weights = []
+        given = ins[len(self.kinds) :]
         for at, (shard, out, kind) in enumerate(zip(ins, outs, self.kinds)):
             rows, columns = shard.shape
 
@@ -351,8 +371,9 @@
 
         swaps = {}
         for at, kind, mine, block in weights:
-            swaps[at] = net.remote((id(self), at, "x"), mine(1), block(z, 0), net.device(1, 0))
-            swaps[at].start()
+            if not given:
+                swaps[at] = net.remote((id(self), at, "x"), mine(1), block(z, 0), net.device(1, 0))
+                swaps[at].start()
             for up in (True, False):
                 start(at, 0, 1, up, block, mine(0))
         for at, kind, mine, block in weights:
@@ -363,10 +384,19 @@
             else:
                 locals_.append(net.copy(mine(0), block(z, 0)))
             locals_[-1].start()
+        for (at, kind, mine, block), other in zip(weights, given):
+            span = pl.ds(self.share[0] * other.shape[kind == "row"] // self.share[1], other.shape[kind == "row"] // self.share[1])
+            other = other.at[:, span] if kind == "row" else other.at[span, :]
+            locals_.append(net.copy(other, block(z, 1)))
+            locals_[-1].start()
+            for up in (True, False):
+                start(at, 1, 1, up, block, other)
         yield
         for copy in locals_:
             copy.wait()
         for at, kind, mine, block in weights:
+            if given:
+                continue
             swaps[at].wait_recv()
             for up in (True, False):
                 start(at, 1, 1, up, block)
@@ -394,6 +424,31 @@
             copy.wait_send()
 
 
+class HalfSwap:
+    moves = ("x",)
+
+    def __init__(self, shards, kinds, nz, ny):
+        self.ins, self.kinds = list(shards), list(kinds)
+        self.outs, self.scratch = [], []
+        for shard, kind in zip(shards, kinds):
+            rows, columns = shard.shape
+            shape = (rows, columns // 2) if kind == "row" else (rows // 2, columns)
+            self.outs.append((jax.ShapeDtypeStruct(shape, shard.dtype), ANY))
+        self.remotes, self.locals = len(self.ins), 0
+
+    def run(self, net, ins, outs, scratch):
+        copies = []
+        for at, (shard, out, kind) in enumerate(zip(ins, outs, self.kinds)):
+            span = out.shape[kind == "row"]
+            there = pl.ds(pl.multiple_of((1 - net.x) * span, span), span)
+            src = shard.at[:, there] if kind == "row" else shard.at[there, :]
+            copies.append(net.remote((id(self), at), src, out, net.device(1, 0)))
+            copies[-1].start()
+        yield
+        for copy in copies:
+            copy.wait()
+
+
 class LineScatter:
     moves = ("x", "line")
 
@@ -407,13 +462,12 @@
             for lead in (nz - 1, nz - 1, 1) + (() if resident else (nz,)):
                 self.scratch.append(pltpu.VMEM((lead, 2) + shape, BF16))
         count = len(self.ins)
-        self.remotes = count * (1 + 4 * (nz - 1))
+        self.remotes = count * (1 + 4 * nz)
         self.locals = count * (2 * nz + 1)
 
     def run(self, net, ins, outs, scratch):
         nz, z = net.nz, net.z
-        sent, loads, stores = [], {}, []
-        grads = []
+        loads, grads = {}, []
         each = 3 if self.resident else 4
         for at, (part, out, kind) in enumerate(zip(ins, outs, self.kinds)):
             down, up, mine = scratch[each * at : each * at + 3]
@@ -443,55 +497,88 @@
         def inbox(slots, line, dx, toward):
             return slots.at[line if toward < 0 else line - 1, dx]
 
-        for k in range(nz - 1):
-            for dx in (1, 0):
-                for at, out, work, down, up, mine in grads:
-                    yield
-                    for line, slots, toward in ((k, down, -1), (nz - 1 - k, up, 1)):
-                        here, slot = work(line, dx), inbox(slots, line, dx, toward)
-                        copy = net.remote((id(self), at, line, dx, toward), here, slot, net.device(z=z + toward))
-                        first = z == (nz - 1 if toward < 0 else 0)
-                        sends = z > line if toward < 0 else z < line
-
-                        def step(copy=copy, here=here, slot=slot, first=first, load=loads.get((at, line, dx))):
-                            if load is not None:
-                                load.wait()
-
-                            @pl.when(jnp.logical_not(first))
-                            def _():
-                                copy.wait_recv()
-                                add_rows(_lead(here), [_lead(here), _lead(slot)])
-
-                            copy.start()
-
-                        pl.when(sends)(step)
-                        sent.append((copy, sends))
-        swaps = []
-        for dx in (1, 0):
-            for at, out, work, down, up, mine in grads:
+        pieces = [(grad, dx) for dx in (1, 0) for grad in grads]
+        each_line = len(pieces)
+
+        for at, *_ in grads:
+            net.slot((id(self), at, "x"))
+            for dx in (0, 1):
+                for line in range(nz):
+                    for toward in (-1, 1):
+                        net.slot((id(self), at, line, dx, toward))
+
+        def chain(grad, dx, line, toward):
+            at, out, work, down, up, mine = grad
+            slot = inbox(down if toward < 0 else up, line, dx, toward)
+            copy = net.remote((id(self), at, line, dx, toward), work(line, dx), slot, net.device(z=z + toward))
+            return copy, slot
+
+        def forward(place, grad, dx, line, toward):
+            at, out, work, down, up, mine = grad
+            copy, slot = chain(grad, dx, line, toward)
+            if not self.resident:
+                loads[at, line, dx].wait()
+            if place != (nz - 1 if toward < 0 else 0):
+                copy.wait_recv()
+                add_rows(_lead(work(line, dx)), [_lead(work(line, dx)), _lead(slot)])
+            copy.start()
+
+        def finish(place, grad, dx):
+            at, out, work, down, up, mine = grad
+            if not self.resident:
+                loads[at, place, dx].wait()
+            terms = [_lead(work(place, dx))]
+            for toward in (-1, 1):
+                if (place < nz - 1) if toward < 0 else (place > 0):
+                    copy, slot = chain(grad, dx, place, toward)
+                    copy.wait_recv()
+                    terms.append(_lead(slot))
+            total = mine.at[0, dx]
+            add_rows(_lead(total), terms)
+            if dx:
+                net.remote((id(self), at, "x"), total, out.at[net.x], net.device(1, 0)).start()
+            else:
+                net.copy_at(self.first_local + at, total, out.at[net.x]).start()
+
+        plan = {}
+        for place in range(nz):
+            waits_up, waits_down = place, nz - 1 - place
+            todo = []
+            for toward, waits, lines in (
+                (1, waits_up, range(nz - 1, place, -1)),
+                (-1, waits_down, range(place)),
+            ):
+                order = [(line, piece) for line in lines for piece in pieces]
+                for j, (line, (grad, dx)) in enumerate(order):
+                    todo.append((waits + j if waits else 0, waits, (forward, grad, dx, line, toward)))
+            for q, (grad, dx) in enumerate(pieces):
+                times = []
+                if waits_up:
+                    times.append(waits_up + each_line * (nz - 1 - place) + q)
+                if waits_down:
+                    times.append(waits_down + each_line * place + q)
+                todo.append((max(times), nz, (finish, grad, dx)))
+            for time, waits, item in sorted(todo, key=lambda entry: entry[:2]):
+                plan.setdefault(time, {}).setdefault(place, []).append(item)
+        self.first_local = net.take_locals(len(grads))
+        for time in range(max(plan) + 1):
+            if time:
                 yield
-                total = mine.at[0, dx]
-                for line in range(nz):
-
-                    @pl.when(z == line)
-                    def _(line=line, at=at, total=total, work=work, down=down, up=up):
-                        if not self.resident:
-                            loads[at, line, dx].wait()
-                        terms = [_lead(work(line, dx))]
-                        for slots, toward in ((down, -1), (up, 1)):
-                            if (line < nz - 1) if toward < 0 else (line > 0):
-                                slot = inbox(slots, line, dx, toward)
-                                key = (id(self), at, line, dx, toward)
-                                net.remote(key, total, slot, net.device(z=z + toward)).wait_recv()
-                                terms.append(_lead(slot))
-                        add_rows(_lead(total), terms)
-
-                if dx:
-                    swaps.append(net.remote((id(self), at, "x"), total, out.at[net.x], net.device(1, 0)))
-                    swaps[-1].start()
-                else:
-                    stores.append(net.copy(total, out.at[net.x]))
-                    stores[-1].start()
+            for place, items in sorted(plan.get(time, {}).items()):
+
+                def act(place=place, items=items):
+                    for item in items:
+                        item[0](place, *item[1:])
+
+                pl.when(z == place)(act)
+        sent = [
+            (chain(grad, dx, line, toward)[0], (z > line) if toward < 0 else (z < line))
+            for grad, dx in pieces
+            for toward, lines in ((-1, range(nz - 1)), (1, range(1, nz)))
+            for line in lines
+        ]
+        swaps = [net.remote((id(self), at, "x"), mine.at[0, 1], out.at[net.x], net.device(1, 0)) for at, out, _, _, _, mine in grads]
+        stores = [net.copy_at(self.first_local + at, mine.at[0, 0], out.at[net.x]) for at, out, _, _, _, mine in grads]
         yield
         for copy, sends in sent:
             pl.when(sends)(copy.wait_send)
@@ -518,6 +605,7 @@
 
 class KeysGather:
     moves = ("x", "line", "c")
+    in_spec = IN_VMEM
 
     def __init__(self, face, nz, ny):
         m, rows, width = face.shape
@@ -634,6 +722,7 @@
 
 class PlaneGather:
     moves = ("plane",)
+    in_spec = IN_VMEM
 
     def __init__(self, own, nz, ny):
         self.ins = [own]
@@ -772,7 +861,7 @@
     )
 
 
-def exchange(plans, nz, ny, collective_id, name):
+def exchange(plans, nz, ny, collective_id, name, order=()):
     ins = [array for plan in plans for array in plan.ins]
     outs = [out for plan in plans for out in plan.outs]
     scratch = [entry for plan in plans for entry in plan.scratch]
@@ -787,6 +876,8 @@
             out_refs = out_refs[len(plan.outs) :]
             scratch_refs = scratch_refs[len(plan.scratch) :]
             running.append(plan.run(net, *mine))
+        for at in order:
+            next(running[at], None)
         while running:
             for steps in list(running):
                 try:
@@ -794,7 +885,8 @@
                 except StopIteration:
                     running.remove(steps)
 
-    results = launch(body, ins, [ANY] * len(ins), outs, scratch, plans, nz, ny, collective_id, name)
+    specs = [getattr(plan, "in_spec", ANY) for plan in plans for _ in plan.ins]
+    results = launch(body, ins, specs, outs, scratch, plans, nz, ny, collective_id, name)
     grouped = []
     for plan in plans:
         grouped.append(results[: len(plan.outs)])
@@ -827,7 +919,7 @@
     face_rows = cot_face.shape[1]
     tokens = micro_count * face_rows
     attn = mixed.shape[1]
-    units = w_expand.shape[1] // 2
+    units = w_expand[0].shape[1] // 2
     half = units // 2
     tile = min(512, half)
     wide = 512
@@ -836,8 +928,8 @@
     own = (micro_count, own_rows, width)
     scatter_a, scatter_b = (FaceScatter(part, nz, ny, resident=True) for _ in range(2))
     gather = FaceGather(jax.ShapeDtypeStruct(own, BF16), nz, ny)
-    line_e = LineGather([w_expand], ["row"], nz, ny, share=(1, 2))
-    line_r = LineGather([w_reduce], ["col"], nz, ny)
+    line_e = LineGather(w_expand[:1], ["row"], nz, ny, share=(1, 2), given=w_expand[1:])
+    line_r = LineGather(w_reduce[:1], ["col"], nz, ny, given=w_reduce[1:])
     line_s = LineScatter([part_red], ["col"], nz, ny, resident=True)
     plans = [scatter_a, scatter_b, gather, line_e, line_r, line_s]
     vmem = pl.BlockSpec(memory_space=pltpu.VMEM)
@@ -872,7 +964,7 @@
     scratch += scatter_a.scratch + line_s.scratch
 
     def body(net, ins, outs, scratch):
-        mixed_in, wo_in, own_in, cot_in, face_in, norms, first_in, expand_in, reduce_in = ins
+        mixed_in, wo_in, own_in, cot_in, face_in, norms, first_in, *weights_in = ins
         middle_out, grad_out, low_out, norm_out, expand_a, expand_b, reduced_out, reduce_out = outs
         p, branch, middle, own, cot_own, n_own, n_face, cot, we0, we1, wr, active, slope, pr, mixed, wo = scratch[:shared]
         we = (we0, we1)
@@ -890,8 +982,8 @@
                 (face_in, cot),
             )
         ]
-        e = line_e.run(net, [expand_in], [we1], [])
-        r = line_r.run(net, [reduce_in], [wr], [])
+        e = line_e.run(net, weights_in[:2], [we1], [])
+        r = line_r.run(net, weights_in[2:], [wr], [])
         queue = []
 
         def tick(count=1):
@@ -903,9 +995,10 @@
             return act
 
         next(e)
+        next(r)
         for load in loads:
             load.start()
-        queue += [e, r, e, e, r, e, e, r, r, e, e, r, r, r, r]
+        queue += [e, e, e, r, e, e, r, r, e, e, r, r, r, r]
         loads[0].wait()
         loads[1].wait()
 
@@ -916,7 +1009,7 @@
             p[m, :, columns] = jnp.dot(mixed[rows, :], wo[:, columns], preferred_element_type=F32).astype(BF16)
 
         loop(micro_count * (width // wide), branch_tile)
-        tick(2)()
+        tick(1)()
         drive(
             scatter_a.run(net, [p], [branch], slots),
             [None, None, None, None, tick(2), None, tick(1), None],
@@ -987,9 +1080,9 @@
         tick(1)()
         loop((half // tile) * (width // wide), reduce_tile(half))
         s = line_s.run(net, [pr], [reduce_out], line_slots)
+        next(s)
         tick(9)()
         queue.extend([s] * 40)
-        tick(1)()
 
         def slope_tile(at):
             m, n = lax.div(at, units // tile), lax.rem(at, units // tile)
@@ -1015,35 +1108,38 @@
                 pass
         stores = []
 
-        def reduced_tiles():
-            def tile_at(at):
-                m, n = lax.div(at, width // wide), lax.rem(at, width // wide)
-                rows = pl.ds(pl.multiple_of(m * face_rows, face_rows), face_rows)
+        def reduced_tiles(m):
+            def tile_at(n):
+                rows = pl.ds(m * face_rows, face_rows)
                 columns = pl.ds(pl.multiple_of(n * wide, wide), wide)
                 cot[m, :, columns] = jnp.dot(active[rows, :], wr[:, columns], preferred_element_type=F32).astype(BF16)
 
-            loop(micro_count * (width // wide), tile_at)
-            stores.append(net.copy(cot, reduced_out))
-            stores[-1].start()
-
-        def expand_tiles():
-            for h in (0, 1):
-
-                def tile_at(at, h=h):
-                    k, n = lax.div(at, half // tile), lax.rem(at, half // tile)
-                    rows = pl.ds(pl.multiple_of(k * wide, wide), wide)
-                    columns = pl.ds(pl.multiple_of(n * tile, tile), tile)
-                    grads = pl.ds(pl.multiple_of(h * half + n * tile, tile), tile)
-                    we[h][rows, columns] = lax.dot_general(
-                        n_face[:, :, rows].reshape(tokens, wide),
-                        slope[:, grads],
-                        across,
-                        preferred_element_type=F32,
-                    ).astype(BF16)
-
+            def act():
+                loop(width // wide, tile_at)
+                stores.append(net.copy(cot.at[m], reduced_out.at[m]))
+                stores[-1].start()
+
+            return act
+
+        def expand_tiles(h):
+            def tile_at(at):
+                k, n = lax.div(at, half // tile), lax.rem(at, half // tile)
+                rows = pl.ds(pl.multiple_of(k * wide, wide), wide)
+                columns = pl.ds(pl.multiple_of(n * tile, tile), tile)
+                grads = pl.ds(pl.multiple_of(h * half + n * tile, tile), tile)
+                we[h][rows, columns] = lax.dot_general(
+                    n_face[:, :, rows].reshape(tokens, wide),
+                    slope[:, grads],
+                    across,
+                    preferred_element_type=F32,
+                ).astype(BF16)
+
+            def act():
                 loop((width // wide) * (half // tile), tile_at)
                 stores.append(net.copy(we[h], (expand_a, expand_b)[h]))
                 stores[-1].start()
+
+            return act
 
         def do(*actions):
             def act():
@@ -1054,7 +1150,16 @@
 
         drive(
             scatter_b.run(net, [p], [branch], slots),
-            [None, None, None, None, expand_tiles, tick(1), do(tick(1), reduced_tiles, tick(1)), None],
+            [
+                None,
+                None,
+                None,
+                None,
+                do(tick(1), expand_tiles(0)),
+                do(expand_tiles(1), tick(1)),
+                do(*[reduced_tiles(m) for m in range(micro_count)], tick(1)),
+                None,
+            ],
         )
         loads[3].wait()
         keep_middle.wait()
@@ -1086,41 +1191,47 @@
         for store in stores:
             store.wait()
 
-    ins = [mixed, wo, inputs, cotangent, cot_face, norms, wexp_first, w_expand, w_reduce]
-    specs = [ANY] * 5 + [vmem] + [ANY] * 3
+    ins = [mixed, wo, inputs, cotangent, cot_face, norms, wexp_first, *w_expand, *w_reduce]
+    specs = [ANY] * 5 + [vmem] + [ANY] * (len(ins) - 6)
     return launch(
         body, ins, specs, outs, scratch, plans, nz, ny, collective_id, "mlp_block", extra_locals=12, vmem=62
     )
 
 
-def masked_scores(queries, keys, query_doc, key_doc, scale):
-    raw = lax.dot_general(queries, keys, (((1,), (1,)), ((), ())), preferred_element_type=F32) * scale
-    return jnp.where(query_doc == key_doc, raw, NEG_FILL)
+def stack_heads(ref, heads, head_dim):
+    return jnp.concatenate([ref[0, :, h * head_dim : (h + 1) * head_dim] for h in range(heads)], axis=0)
+
+
+def masked_scores(queries, keys, query_doc, key_doc, head_dim):
+    raw = lax.dot_general(keys, queries, (((1,), (1,)), ((), ())), preferred_element_type=F32)
+    key_doc = jnp.concatenate([key_doc] * (raw.shape[1] // key_doc.shape[1]), axis=1)
+    return jnp.where(query_doc == key_doc, raw * (LOG2_E / math.sqrt(head_dim)), NEG_FILL)
 
 
 def attend_forward(queries, keys_vals, query_doc, key_doc, bounds, heads, head_dim):
     micro_count, rows, _ = queries.shape
     blocks = rows // BLOCK
-    scale = 1.0 / math.sqrt(head_dim)
     tall = heads * BLOCK
 
     def kernel(bounds_ref, q_ref, kv_ref, qd_ref, kd_ref, out_ref, log_ref):
         at = pl.program_id(0) * blocks + pl.program_id(1)
         low, high = bounds_ref[2 * at], bounds_ref[2 * at + 1]
-        queries = jnp.concatenate([q_ref[0, :, h * head_dim : (h + 1) * head_dim] for h in range(heads)], axis=0)
-        doc = jnp.concatenate([qd_ref[0]] * heads, axis=0)
+        queries = stack_heads(q_ref, heads, head_dim)
+        doc = jnp.concatenate([qd_ref[0, 0]] * heads, axis=1)
 
         def body(block, carry):
             top, total, mixed = carry
             first = pl.multiple_of(block * BLOCK, BLOCK)
             keys = kv_ref[0, pl.ds(first, BLOCK), :head_dim]
             values = kv_ref[0, pl.ds(first, BLOCK), head_dim:]
-            scores = masked_scores(queries, keys, doc, kd_ref[0, :, pl.ds(first, BLOCK)], scale)
-            new_top = jnp.maximum(top, jnp.max(scores, axis=-1, keepdims=True))
-            weights = jnp.where(scores == NEG_FILL, 0.0, jnp.exp(scores - new_top))
-            fade = jnp.exp(top - new_top)
-            total = total * fade + jnp.sum(weights, axis=-1, keepdims=True)
-            mixed = mixed * fade + jnp.dot(weights.astype(BF16), values, preferred_element_type=F32)
+            scores = masked_scores(queries, keys, doc, kd_ref[0, pl.ds(first, BLOCK), :], head_dim)
+            new_top = jnp.maximum(top, jnp.max(scores, axis=0, keepdims=True))
+            weights = jnp.exp2(scores - new_top)
+            fade = jnp.exp2(top - new_top)
+            total = total * fade + jnp.sum(weights, axis=0, keepdims=True)
+            mixed = mixed * fade + lax.dot_general(
+                values, weights.astype(BF16), (((0,), (0,)), ((), ())), preferred_element_type=F32
+            )
             return new_top, total, mixed
 
         top, total, mixed = lax.fori_loop(
@@ -1128,21 +1239,21 @@
             high,
             body,
             (
-                jnp.full((tall, 1), NEG_FILL, F32),
-                jnp.zeros((tall, 1), F32),
-                jnp.zeros((tall, head_dim), F32),
+                jnp.full((1, tall), NEG_FILL, F32),
+                jnp.zeros((1, tall), F32),
+                jnp.zeros((head_dim, tall), F32),
             ),
         )
-        mixed = (mixed / total).astype(BF16)
+        mixed = jnp.transpose(mixed / total).astype(BF16)
         for h in range(heads):
             out_ref[0, :, h * head_dim : (h + 1) * head_dim] = mixed[h * BLOCK : (h + 1) * BLOCK]
-        log_ref[0, 0] = top + jnp.log(total)
+        log_ref[0, 0] = top + jnp.log2(total)
 
     return pl.pallas_call(
         kernel,
         out_shape=[
             jax.ShapeDtypeStruct(queries.shape, BF16),
-            jax.ShapeDtypeStruct((micro_count, blocks, tall, 1), F32),
+            jax.ShapeDtypeStruct((micro_count, blocks, 1, tall), F32),
         ],
         grid_spec=pltpu.PrefetchScalarGridSpec(
             num_scalar_prefetch=1,
@@ -1150,12 +1261,12 @@
             in_specs=[
                 pl.BlockSpec((1, BLOCK, heads * head_dim), lambda m, b, _: (m, b, 0)),
                 pl.BlockSpec((1,) + keys_vals.shape[1:], lambda m, b, _: (m, 0, 0)),
-                pl.BlockSpec((1, BLOCK, 1), lambda m, b, _: (m, b, 0)),
-                pl.BlockSpec((1, 1, keys_vals.shape[1]), lambda m, b, _: (m, 0, 0)),
+                pl.BlockSpec((1, 1, 1, BLOCK), lambda m, b, _: (m, b, 0, 0)),
+                pl.BlockSpec((1,) + key_doc.shape[1:], lambda m, b, _: (m, 0, 0)),
             ],
             out_specs=[
                 pl.BlockSpec((1, BLOCK, heads * head_dim), lambda m, b, _: (m, b, 0)),
-                pl.BlockSpec((1, 1, tall, 1), lambda m, b, _: (m, b, 0, 0)),
+                pl.BlockSpec((1, 1, 1, tall), lambda m, b, _: (m, b, 0, 0)),
             ],
         ),
         compiler_params=pltpu.CompilerParams(vmem_limit_bytes=40 << 20),
@@ -1174,37 +1285,34 @@
         at = pl.program_id(0) * blocks + pl.program_id(1)
         low, high = bounds_ref[2 * at], bounds_ref[2 * at + 1]
 
-        def stack(ref):
-            return jnp.concatenate([ref[0, :, h * head_dim : (h + 1) * head_dim] for h in range(heads)], axis=0)
-
         @pl.when(pl.program_id(1) == 0)
         def _():
             acc_ref[...] = jnp.zeros_like(acc_ref)
 
-        queries, grad = stack(q_ref), stack(do_ref)
-        delta = jnp.sum(grad.astype(F32) * stack(o_ref).astype(F32), axis=-1, keepdims=True)
-        doc = jnp.concatenate([qd_ref[0]] * heads, axis=0)
+        queries, grad = stack_heads(q_ref, heads, head_dim), stack_heads(do_ref, heads, head_dim)
+        products = grad.astype(F32) * stack_heads(o_ref, heads, head_dim).astype(F32)
+        delta = jnp.sum(jnp.transpose(products), axis=0, keepdims=True)
+        doc = jnp.concatenate([qd_ref[0, 0]] * heads, axis=1)
         log_total = log_ref[0, 0]
 
         def body(block, grad_queries):
             first = pl.multiple_of(block * BLOCK, BLOCK)
             keys = kv_ref[0, pl.ds(first, BLOCK), :head_dim]
             values = kv_ref[0, pl.ds(first, BLOCK), head_dim:]
-            scores = masked_scores(queries, keys, doc, kd_ref[0, :, pl.ds(first, BLOCK)], scale)
-            probs = jnp.where(scores == NEG_FILL, 0.0, jnp.exp(scores - log_total))
-            grad_probs = lax.dot_general(grad, values, (((1,), (1,)), ((), ())), preferred_element_type=F32)
+            scores = masked_scores(queries, keys, doc, kd_ref[0, pl.ds(first, BLOCK), :], head_dim)
+            probs = jnp.exp2(scores - log_total)
+            grad_probs = lax.dot_general(values, grad, (((1,), (1,)), ((), ())), preferred_element_type=F32)
             grad_scores = (probs * (grad_probs - delta)).astype(BF16)
-            across = (((0,), (0,)), ((), ()))
             acc_ref[pl.ds(first, BLOCK), :head_dim] += (
-                lax.dot_general(grad_scores, queries, across, preferred_element_type=F32) * scale
+                jnp.dot(grad_scores, queries, preferred_element_type=F32) * scale
             )
-            acc_ref[pl.ds(first, BLOCK), head_dim:] += lax.dot_general(
-                probs.astype(BF16), grad, across, preferred_element_type=F32
+            acc_ref[pl.ds(first, BLOCK), head_dim:] += jnp.dot(probs.astype(BF16), grad, preferred_element_type=F32)
+            return grad_queries + lax.dot_general(
+                keys, grad_scores, (((0,), (0,)), ((), ())), preferred_element_type=F32
             )
-            return grad_queries + jnp.dot(grad_scores, keys, preferred_element_type=F32)
-
-        grad_queries = lax.fori_loop(low, high, body, jnp.zeros((tall, head_dim), F32))
-        grad_queries = (grad_queries * scale).astype(BF16)
+
+        grad_queries = lax.fori_loop(low, high, body, jnp.zeros((head_dim, tall), F32))
+        grad_queries = jnp.transpose(grad_queries * scale).astype(BF16)
         for h in range(heads):
             gq_ref[0, :, h * head_dim : (h + 1) * head_dim] = grad_queries[h * BLOCK : (h + 1) * BLOCK]
 
@@ -1228,9 +1336,9 @@
                 row,
                 wide,
                 wide,
-                pl.BlockSpec((1, 1, tall, 1), lambda m, b, _: (m, b, 0, 0)),
-                pl.BlockSpec((1, BLOCK, 1), lambda m, b, _: (m, b, 0)),
-                pl.BlockSpec((1, 1, seq_len), lambda m, b, _: (m, 0, 0)),
+                pl.BlockSpec((1, 1, 1, tall), lambda m, b, _: (m, b, 0, 0)),
+                pl.BlockSpec((1, 1, 1, BLOCK), lambda m, b, _: (m, b, 0, 0)),
+                pl.BlockSpec((1,) + key_doc.shape[1:], lambda m, b, _: (m, 0, 0)),
             ],
             out_specs=[wide, row],
             scratch_shapes=[pltpu.VMEM((seq_len, 2 * head_dim), F32)],
@@ -1279,14 +1387,16 @@
 
     norms = jnp.stack([attn_gain, attn_shift, mlp_gain, mlp_shift])
     norms = jnp.concatenate([norms, jnp.zeros((4, norms.shape[1]), BF16)])
-    (wq, wo, wkv), (norms,), (face_in,) = swap(
+    (wq, wo, wkv), (norms,), (face_in,), (expand_given,) = swap(
         [
             LineGather([w_query, w_attn_out, w_keyval], ["row", "col", "both"], *on),
             PlaneGather(norms, *on),
             FaceGather(inputs, *on, hold_x=True),
+            HalfSwap([w_expand], ["row"], *on),
         ],
         collective_id=1,
         name="gather_attention",
+        order=K1_ORDER,
     )
     norms = norms[:, :4].transpose(1, 0, 2).reshape(4, width).astype(F32)
     gain_one, shift_one = norms[0], norms[1]
@@ -1297,11 +1407,12 @@
     (keys_vals,), (wexp_first,), (cot_face,) = swap(
         [
             KeysGather(keys_face, *on),
-            LineGather([w_expand], ["row"], *on, share=(0, 2)),
+            LineGather([w_expand], ["row"], *on, share=(0, 2), given=[expand_given]),
             FaceGather(cotangent, *on, hold_x=True),
         ],
         collective_id=2,
         name="gather_keys",
+        order=K2_ORDER,
     )
 
     query_doc = lax.dynamic_slice_in_dim(doc_ids, z * face_rows, face_rows, axis=1)
@@ -1311,13 +1422,19 @@
     lows = jnp.sum((last_doc[:, None, :] < first_doc[:, :, None]).astype(jnp.int32), axis=-1)
     highs = jnp.broadcast_to(z * blocks + jnp.arange(blocks, dtype=jnp.int32) + 1, lows.shape)
     bounds = jnp.stack([lows, highs], axis=-1).reshape(-1)
-    docs = (query_doc[:, :, None], doc_ids[:, None, :], bounds, heads, head_dim)
+    docs = (
+        query_doc.reshape(micro_count, blocks, 1, BLOCK),
+        jnp.broadcast_to(doc_ids[:, :, None], doc_ids.shape + (128,)),
+        bounds,
+        heads,
+        head_dim,
+    )
     mixed, log_total = attend_forward(queries, keys_vals, *docs)
     mixed_flat = mixed.reshape(tokens, heads * head_dim)
 
     own_in = inputs.astype(F32)
     middle, grad_middle, low_middle, grad_norm_two, part_expand_a, part_expand_b, reduced, grad_reduce = mlp_block(
-        mixed_flat, wo, inputs, cotangent, cot_face, norms[2:], wexp_first, w_expand, w_reduce, *on, collective_id=3
+        mixed_flat, wo, inputs, cotangent, cot_face, norms[2:], wexp_first, (w_expand, expand_given), (w_reduce,), *on, collective_id=3
     )
     grad_gain_two, grad_shift_two = jnp.sum(grad_norm_two, axis=1)
     (grad_branch,), (reduced,), (grad_expand_a, grad_expand_b) = swap(

time: 667 us -> 530 us (0.79)
  Pallas kernels: 601 us -> 468 us
    pallas_call x6, Pallas kernels: 583 us -> 454 us  [launch(): pl.pallas_call(kernel, out_shape=[shape for shape, _ in outs], in_specs=i...]
where the time goes in v3:
time: 530 us; the launch traced here: 525 us
  Pallas kernels  468 us (88%)
  matrix products  20.6 us (4%)
  local copies, waits for them, and re-layouts  17.6 us (3%)
  other arithmetic  17 us (3%)
    pallas_call x6, Pallas kernels, launch(): pl.pallas_call(kernel, out_shape=[shape for shape, _ in outs], in_specs=i...  454 us

profile of v3, /device:TPU:0, one launch (start us, length us, event | category | flops | bytes accessed | tf_op | source)
XLA Modules:
  0.0 524.9 jit_solution(12146645505075624144)
XLA Ops:
  0.7 0.7 constant_dynamic-slice_fusion
  1.5 0.8 slice.53
  2.3 0.2 fusion.29
  2.9 0.7 stack.32
  3.6 0.7 stack.33
  4.2 0.7 stack.34
  4.9 0.7 stack.35
  5.6 0.6 concatenate.13.refs_3_
  6.2 55.0 %gather_attention.1 = (bf16[2048,256]{1,0:T(8,128)(2,1)}, bf16[256,2048]{1,0:T(8,128)(2,1)}, bf16[2048,256]{1,0:T(8,128)(2,1)}, bf16[8,8,256]{2,1,0:T(8,128)(2,1...) custom-call(bf16[256,512]{1,0:T(8,128)(2,1)} %refs_0_.1, bf16[512,256]{1,0:T(8,128)(2,1)} %refs_1_.2, ...), custom_call_target="tpu_custom_call" | custom-call | tf_op jit(solution)/shard_map/gather_attention/pallas_call | solution.py:845
  61.2 3.8 convert_reduce_fusion
  65.0 0.8 copy-done.7
  65.8 1.8 fusion.2
  67.6 3.1 fusion.5
  70.8 2.9 convolution_convert_fusion.2
  73.7 45.1 %gather_keys.1 = (bf16[3,2048,256]{2,1,0:T(8,128)(2,1)}, bf16[2048,512]{1,0:T(8,128)(2,1)}, bf16[3,512,2048]{2,1,0:T(8,128)(2,1)}) custom-call(bf16[3,512,256]{2,1,0:T(8,128)(2,1)} %bitcast.85, bf16[256,2048]{1,0:T(8,128)(2,1)} %refs_7_.1, bf16[256,1024]{1,0:T(8,128)(2,1)} %get-tuple-element.46.refs_2_.refs_8_, bf16[3,64,2048]{2,1,0:T(8,128)(2,1)} %refs_3_.3), custom_call_target="tpu_custom_call" | custom-call | tf_op jit(solution)/shard_map/gather_keys/pallas_call | solution.py:845
  118.9 1.8 convolution_convert_fusion.3
  120.7 0.9 broadcast_in_dim.9.kd_ref
  121.6 1.0 copy-done.2
  122.6 6.0 %attend_forward.1 = (bf16[3,512,256]{2,1,0:T(8,128)(2,1)S(1)}, f32[3,2,1,512]{3,2,1,0:T(1,128)S(1)}) custom-call(s32[12]{0:T(128)S(1)} %reshape.125.bounds_ref, bf16[3,512,256]{2,1,0:T(8,128)(2,1)S(1)} %bitcast.72, bf16[3,2048,256]{2,1,0:T(8,128)(2,1)S(1)} %copy-done.2, s32[3,2,1,256]{3,2,1,0:T(1,128)S(1)} %reshape.129.qd_ref, ...), custom_call_target="tpu_custom_call" | custom-call | tf_op jit(solution)/shard_map/attend_forward/pallas_call | solution.py:1252
  128.6 0.9 copy-done.4
  129.5 0.6 slice.70
  130.1 180.5 %mlp_block.1 = (f32[3,64,2048]{2,1,0:T(8,128)}, f32[3,64,2048]{2,1,0:T(8,128)}, bf16[3,64,2048]{2,1,0:T(8,128)(2,1)}, f32[2,16,2048]{2,1,0:T(8,128)}, bf16[2048,...) custom-call(bf16[1536,256]{1,0:T(8,128)(2,1)} %bitcast.70, ...), custom_call_target="tpu_custom_call" | custom-call | tf_op jit(solution)/shard_map/mlp_block/pallas_call | solution.py:845
  310.6 78.7 %gather_branch.1 = (bf16[3,512,2048]{2,1,0:T(8,128)(2,1)}, f32[3,64,2048]{2,1,0:T(8,128)}, bf16[2,256,512]{2,1,0:T(8,128)(2,1)}, bf16[2,256,512]{2,1,0:T(8,128)(2,1)}) custom-call(bf16[3,64,2048]{2,1,0:T(8,128)(2,1)} %get-tuple-element.53.refs_0_, bf16[3,512,2048]{2,1,0:T(8,128)(2,1)} %get-tuple-element.54.refs_1_, ...), custom_call_target="tpu_custom_call" | custom-call | tf_op jit(solution)/shard_map/gather_branch/pallas_call | solution.py:845
  389.3 1.3 constant_dynamic-update-slice_fusion.1
  390.6 1.4 constant_dynamic-update-slice_fusion
  392.1 1.6 maximum_convert_fusion
  393.6 2.0 convolution_convert_fusion.1
  395.6 0.2 copy-done.1
  395.8 0.9 copy-done.3
  396.8 0.1 copy-done.5
  396.9 8.2 %attend_backward.1 = (bf16[3,512,256]{2,1,0:T(8,128)(2,1)S(1)}, bf16[3,2048,256]{2,1,0:T(8,128)(2,1)S(1)}) custom-call(s32[12]{0:T(128)S(1)} %reshape.125.bounds_ref, bf16[3,512,256]{2,1,0:T(8,128)(2,1)S(1)} %bitcast.73, bf16[3,2048,256]{2,1,0:T(8,128)(2,1)S(1)} %copy-done.3, bf16[3,512,256]{2,1,0:T(8,128)(2,1)S(1)} %copy-done.5, ...), custom_call_target="tpu_custom_call" | custom-call | tf_op jit(solution)/shard_map/attend_backward/pallas_call | solution.py:1325
  405.2 2.9 fusion.7.refs_3_
  408.1 2.8 fusion.6.refs_2_
  410.9 4.5 convolution_convert_fusion
  415.4 69.9 %scatter_query.1 = (f32[3,64,2048]{2,1,0:T(8,128)}, f32[3,64,256]{2,1,0:T(8,128)}, bf16[2,256,256]{2,1,0:T(8,128)(2,1)}, bf16[2,256,256]{2,1,0:T(8,128)(2,1)}) custom-call(bf16[3,512,2048]{2,1,0:T(8,128)(2,1)} %bitcast.76, bf16[12,512,256]{2,1,0:T(8,128)(2,1)} %bitcast.71, bf16[256,2048]{1,0:T(8,128)(2,1)} %fusion.6.refs_2_, bf16[2048,256]{1,0:T(8,128)(2,1)} %fusion.7.refs_3_), custom_call_target="tpu_custom_call" | custom-call | tf_op jit(solution)/shard_map/scatter_query/pallas_call | solution.py:845
  485.3 1.1 slice_bitcast_fusion.3
  486.5 0.9 maximum_convert_fusion.1
  487.3 0.2 convert_reduce_fusion.1
  487.5 2.1 fusion.18
  489.7 0.8 fusion.17
  490.9 0.7 pad.4.refs_1_
  491.6 1.6 fusion.8
  493.2 24.9 %scatter_small.1 = (f32[1,64,256]{2,1,0:T(8,128)}, f32[8,128]{1,0:T(8,128)}) custom-call(bf16[4,512,256]{2,1,0:T(8,128)(2,1)} %bitcast.84, f32[8,4,8,128]{3,2,1,0:T(8,128)} %pad.4.refs_1_), custom_call_target="tpu_custom_call" | custom-call | tf_op jit(solution)/shard_map/scatter_small/pallas_call | solution.py:845
  518.1 1.3 slice_bitcast_fusion.4
  519.5 2.2 add_add_fusion.1
  521.6 0.8 bitcast_convert_fusion.1
  522.5 1.5 bitcast_convert_fusion
  524.0 0.6 copy.43
  (81 shorter events, 1.2 us)
Async XLA Ops:
  61.2 4.6 copy-start.7
  65.8 1.8 copy-start.25
  67.6 3.1 copy-start.17
  70.8 48.1 %copy-start.9 = (bf16[3,512,2048]{2,1,0:T(8,128)(2,1)}, bf16[3,512,2048]{2,1,0:T(8,128)(2,1)S(1)}, u32[]{:S(2)}) copy-start(bf16[3,512,2048]{2,1,0:T(8,128)(2,1)S(1)} %fusion.5) | copy-start | bytes 18874372
  73.7 45.1 %copy-start.15 = (bf16[2048,256]{1,0:T(8,128)(2,1)S(1)}, bf16[2048,256]{1,0:T(8,128)(2,1)}, u32[]{:S(2)}) copy-start(bf16[2048,256]{1,0:T(8,128)(2,1)} %get-tuple-element.44) | copy-start | bytes 3145732
  118.9 1.8 copy-start.24
  120.7 1.9 copy-start.2
  122.6 6.0 %copy-start = (s32[3,2048,128]{2,1,0:T(8,128)}, s32[3,2048,128]{2,1,0:T(8,128)S(1)}, u32[]{:S(2)}) copy-start(s32[3,2048,128]{2,1,0:T(8,128)S(1)} %broadcast_in_dim.9.kd_ref) | copy-start | bytes 9437188
  128.6 0.9 copy-start.4
  310.6 83.0 %copy-start.19 = (bf16[256,2048]{1,0:T(8,128)(2,1)S(1)}, bf16[256,2048]{1,0:T(8,128)(2,1)}, u32[]{:S(2)}) copy-start(bf16[256,2048]{1,0:T(8,128)(2,1)} %get-tuple-element.49.refs_1_) | copy-start | bytes 3145732
  389.3 4.3 copy-start.10
  392.0 13.2 %slice-start = ((s8[6291456]{0:T(1024)(128)(4,1)}), s8[4194304]{0:T(1024)(128)(4,1)S(1)}, s32[]{:S(2)}) async-start(s8[6291456]{0:T(1024)(128)(4,1)} %bitcast.79), calls=%async_computation | async-start | bytes 8388608
  393.6 2.2 copy-start.1
  393.6 3.1 copy-start.3
  393.6 3.3 copy-start.5
  393.6 11.5 %slice-start.1 = ((s8[6291456]{0:T(1024)(128)(4,1)}), s8[2097152]{0:T(1024)(128)(4,1)S(1)}, s32[]{:S(2)}) async-start(s8[6291456]{0:T(1024)(128)(4,1)} %bitcast.79), calls=%async_computation.1 | async-start | bytes 4194304
  396.9 11.2 %slice-start.2 = ((s8[6291456]{0:T(1024)(128)(4,1)}), s8[4194304]{0:T(1024)(128)(4,1)S(1)}, s32[]{:S(2)}) async-start(s8[6291456]{0:T(1024)(128)(4,1)} %bitcast.82), calls=%async_computation.2 | async-start | bytes 8388608
  405.1 2.9 copy-start.6
  405.2 2.9 slice-start.3
  408.1 2.8 copy-start.16
  485.3 2.0 copy-start.8
  485.3 2.2 copy-start.18
  485.3 2.2 copy-start.22
  489.7 1.0 copy-start.21
  491.6 27.9 %copy-start.11 = (f32[3,64,2048]{2,1,0:T(8,128)S(1)}, f32[3,64,2048]{2,1,0:T(8,128)}, u32[]{:S(2)}) copy-start(f32[3,64,2048]{2,1,0:T(8,128)} %get-tuple-element.52) | copy-start | bytes 4718596
  491.6 27.9 %copy-start.12 = (f32[3,64,2048]{2,1,0:T(8,128)S(1)}, f32[3,64,2048]{2,1,0:T(8,128)}, u32[]{:S(2)}) copy-start(f32[3,64,2048]{2,1,0:T(8,128)} %get-tuple-element.58) | copy-start | bytes 4718596
  491.6 27.9 %copy-start.13 = (f32[3,64,2048]{2,1,0:T(8,128)S(1)}, f32[3,64,2048]{2,1,0:T(8,128)}, u32[]{:S(2)}) copy-start(f32[3,64,2048]{2,1,0:T(8,128)} %get-tuple-element.57) | copy-start | bytes 4718596
  519.5 2.2 copy-start.20
  519.5 3.0 copy-start.14
  522.5 1.6 copy-start.23

commit v4 on v3

--- a/solution.py
+++ b/solution.py
@@ -14,6 +14,8 @@
 GELU_A = math.sqrt(2.0 / math.pi)
 GELU_B = 0.044715
 LOG2_E = 1.0 / math.log(2.0)
+MLP_ORDER = ("mmmmmeeemmmeerrmmmrmmmrmmmrmmmmsmsmmxxmm", "mmsxxsxsmm",)
+BACK_ORDER = ("mrmerrmrrmmmemmemmrreemwwwqwqqaewrawrqaa", "eaqwqwaaw",)
 K1_ORDER = (0, 2, 1, 2, 0, 2, 3, 0, 0, 0, 0, 0, 2, 0, 0, 2, 0, 1, 0, 0, 2, 2, 2, 0, 0, 0, 0, 0, 0, 2)
 K2_ORDER = (0, 2, 2, 1, 0, 1, 1, 2, 2, 2, 0, 2, 0, 1, 2)
 MESH = pl.DeviceIdType.MESH
@@ -497,7 +499,7 @@
         def inbox(slots, line, dx, toward):
             return slots.at[line if toward < 0 else line - 1, dx]
 
-        pieces = [(grad, dx) for dx in (1, 0) for grad in grads]
+        pieces = (1, 0)
         each_line = len(pieces)
 
         for at, *_ in grads:
@@ -548,16 +550,18 @@
                 (1, waits_up, range(nz - 1, place, -1)),
                 (-1, waits_down, range(place)),
             ):
-                order = [(line, piece) for line in lines for piece in pieces]
-                for j, (line, (grad, dx)) in enumerate(order):
-                    todo.append((waits + j if waits else 0, waits, (forward, grad, dx, line, toward)))
-            for q, (grad, dx) in enumerate(pieces):
+                order = [(line, dx) for line in lines for dx in pieces]
+                for j, (line, dx) in enumerate(order):
+                    for grad in grads:
+                        todo.append((waits + j if waits else 0, waits, (forward, grad, dx, line, toward)))
+            for q, dx in enumerate(pieces):
                 times = []
                 if waits_up:
                     times.append(waits_up + each_line * (nz - 1 - place) + q)
                 if waits_down:
                     times.append(waits_down + each_line * place + q)
-                todo.append((max(times), nz, (finish, grad, dx)))
+                for grad in grads:
+                    todo.append((max(times), nz, (finish, grad, dx)))
             for time, waits, item in sorted(todo, key=lambda entry: entry[:2]):
                 plan.setdefault(time, {}).setdefault(place, []).append(item)
         self.first_local = net.take_locals(len(grads))
@@ -573,7 +577,8 @@
                 pl.when(z == place)(act)
         sent = [
             (chain(grad, dx, line, toward)[0], (z > line) if toward < 0 else (z < line))
-            for grad, dx in pieces
+            for grad in grads
+            for dx in pieces
             for toward, lines in ((-1, range(nz - 1)), (1, range(1, nz)))
             for line in lines
         ]
@@ -679,9 +684,10 @@
 class WholeScatter(FaceScatter):
     moves = ("x", "y", "c", "z")
 
-    def __init__(self, part, nz, ny):
+    def __init__(self, part, nz, ny, resident=False):
         m, _, rows, d = part.shape
-        super().__init__(part.reshape(m * nz, rows, d), nz, ny)
+        merged = jax.ShapeDtypeStruct((m * nz, rows, d), part.dtype) if resident else part.reshape(m * nz, rows, d)
+        super().__init__(merged, nz, ny, resident)
         t = rows // (4 * ny)
         self.m, self.nz = m, nz
         self.outs = [(jax.ShapeDtypeStruct((m, t, d), F32), pl.BlockSpec(memory_space=pltpu.VMEM))]
@@ -718,6 +724,70 @@
         for copy in copies:
             copy.wait()
         add_rows(outs[0], [inbox.at[far] for far in range(nz)])
+
+
+class QuickScatter:
+    moves = ("c", "same", "z")
+
+    def __init__(self, part, nz, ny):
+        _, rows, d = part.shape
+        t = rows // (4 * ny)
+        self.ins, self.t = [part], t
+        self.outs = [(jax.ShapeDtypeStruct((t, d), F32), pl.BlockSpec(memory_space=pltpu.VMEM))]
+        self.scratch = [
+            pltpu.VMEM((2 * ny, nz, t, d), BF16),
+            pltpu.VMEM((2 * ny, nz, t, d), BF16),
+            pltpu.VMEM((2 * ny, nz, t, d), BF16),
+            pltpu.VMEM((nz, t, d), BF16),
+            pltpu.VMEM((nz, 1, t, d), BF16),
+        ]
+        self.remotes, self.locals = 4 * ny + nz, 2 * ny + 1
+
+    def run(self, net, ins, outs, scratch):
+        (part,), (out,), t = ins, outs, self.t
+        work, from_core, inbox, face, line_in = scratch
+        ny, nz = net.ny, net.nz
+        order = [(dx, dy) for dx in (1, 0) for dy in reversed(range(ny))]
+        cores, loads, copies = {}, {}, {}
+
+        def rows(dx, dy, dc):
+            return part.at[:, pl.ds(pl.multiple_of(net.rank(dx, dy, dc) * t, t), t), :]
+
+        for dx, dy in order:
+            at = dx * ny + dy
+            loads[at] = net.copy(rows(dx, dy, 0), work.at[at])
+            loads[at].start()
+            cores[at] = net.remote((id(self), "c", at), rows(dx, dy, 1), from_core.at[at], net.device(0, 0, 1))
+            cores[at].start()
+        for dx, dy in order:
+            at = dx * ny + dy
+            yield
+            loads[at].wait()
+            cores[at].wait_recv()
+            add_rows(work.at[at], [work.at[at], from_core.at[at]])
+            if at:
+                copies[at] = net.remote((id(self), at), work.at[at], inbox.at[at], net.device(dx, dy))
+                copies[at].start()
+        yield
+        for copy in copies.values():
+            copy.wait_recv()
+        add_rows(face, [work.at[0]] + [inbox.at[at] for at in copies])
+        lines = []
+        for far in range(1, nz):
+            line = lax.rem(net.z + far, nz)
+            lines.append(
+                net.remote((id(self), "z", far), face.at[pl.ds(line, 1)], line_in.at[far], net.device(z=line))
+            )
+            lines[-1].start()
+        own = net.copy(face.at[pl.ds(net.z, 1)], line_in.at[0])
+        own.start()
+        yield
+        own.wait()
+        for copy in lines:
+            copy.wait_recv()
+        add_rows(_lead(out), [line_in.at[far] for far in range(nz)])
+        for copy in list(cores.values()) + list(copies.values()) + lines:
+            copy.wait_send()
 
 
 class PlaneGather:
@@ -826,6 +896,8 @@
                                 kinds.add("y")
                             if dc and not dx and not dy:
                                 kinds.add("c")
+                            if not dc:
+                                kinds.add("same")
                         if far and not dx and not dy and not dc:
                             kinds.add("z")
                             if far in (1, nz - 1):
@@ -894,16 +966,21 @@
     return grouped
 
 
-def drive(steps, actions):
-    actions = list(actions)
-    for _ in steps:
-        if actions:
-            action = actions.pop(0)
-            if action is not None:
-                action()
-    for action in actions:
-        if action is not None:
-            action()
+class Weave:
+    def __init__(self):
+        self.plans = {}
+
+    def add(self, name, steps):
+        self.plans[name] = steps
+
+    def step(self, name):
+        steps = self.plans.get(name)
+        if steps is not None and next(steps, self) is self:
+            del self.plans[name]
+
+    def finish(self, name):
+        while name in self.plans:
+            self.step(name)
 
 
 def loop(count, body):
@@ -982,25 +1059,14 @@
                 (face_in, cot),
             )
         ]
-        e = line_e.run(net, weights_in[:2], [we1], [])
-        r = line_r.run(net, weights_in[2:], [wr], [])
-        queue = []
-
-        def tick(count=1):
-            def act():
-                for _ in range(count):
-                    if queue:
-                        next(queue.pop(0), None)
-
-            return act
-
-        next(e)
-        next(r)
+        weave = Weave()
+        stores = []
+        weave.add("e", line_e.run(net, weights_in[:2], [we1], []))
+        weave.step("e")
+        weave.add("r", line_r.run(net, weights_in[2:], [wr], []))
+        weave.step("r")
         for load in loads:
             load.start()
-        queue += [e, e, e, r, e, e, r, r, e, e, r, r, r, r]
-        loads[0].wait()
-        loads[1].wait()
 
         def branch_tile(at):
             m, n = lax.div(at, width // wide), lax.rem(at, width // wide)
@@ -1008,13 +1074,6 @@
             rows = pl.ds(pl.multiple_of(m * face_rows, face_rows), face_rows)
             p[m, :, columns] = jnp.dot(mixed[rows, :], wo[:, columns], preferred_element_type=F32).astype(BF16)
 
-        loop(micro_count * (width // wide), branch_tile)
-        tick(1)()
-        drive(
-            scatter_a.run(net, [p], [branch], slots),
-            [None, None, None, None, tick(2), None, tick(1), None],
-        )
-        loads[2].wait()
         row_steps = own_rows // 16
 
         def own_rows_at(at):
@@ -1027,15 +1086,6 @@
             centered = values - jnp.mean(values, axis=-1, keepdims=True)
             spread = lax.rsqrt(jnp.mean(centered * centered, axis=-1, keepdims=True) + EPSILON)
             n_own[m, rows, :] = (centered * spread * norms[0:1, :] + norms[1:2, :]).astype(BF16)
-
-        loop(micro_count * row_steps, norm_rows)
-        keep_middle = net.copy(middle, middle_out)
-        keep_middle.start()
-        drive(
-            gather.run(net, [n_own], [n_face], []),
-            [tick(2), tick(1), tick(1), tick(2), None, None, None],
-        )
-        loads[4].wait()
 
         def hidden_tile(h):
             def tile_at(at):
@@ -1056,12 +1106,6 @@
 
         across = (((0,), (0,)), ((), ()))
         along = (((1,), (1,)), ((), ()))
-        loop(micro_count * (half // tile), hidden_tile(0))
-        tick(1)()
-        loop(micro_count * (half // tile), hidden_tile(1))
-        tick(1)()
-        loads[5].wait()
-
         def reduce_tile(first):
             def tile_at(at):
                 f, n = lax.div(at, width // wide), lax.rem(at, width // wide)
@@ -1076,14 +1120,6 @@
 
             return tile_at
 
-        loop((half // tile) * (width // wide), reduce_tile(0))
-        tick(1)()
-        loop((half // tile) * (width // wide), reduce_tile(half))
-        s = line_s.run(net, [pr], [reduce_out], line_slots)
-        next(s)
-        tick(9)()
-        queue.extend([s] * 40)
-
         def slope_tile(at):
             m, n = lax.div(at, units // tile), lax.rem(at, units // tile)
             rows = pl.ds(pl.multiple_of(m * face_rows, face_rows), face_rows)
@@ -1098,15 +1134,6 @@
             grad = lax.dot_general(slope[rows, :half], we0[columns, :], along, preferred_element_type=F32)
             grad = grad + lax.dot_general(slope[rows, half:], we1[columns, :], along, preferred_element_type=F32)
             p[m, :, columns] = grad.astype(BF16)
-
-        loop(micro_count * (units // tile), slope_tile)
-        tick(1)()
-        loop(micro_count * (width // wide), normed_tile)
-        tick(1)()
-        for steps in (e, r):
-            for _ in steps:
-                pass
-        stores = []
 
         def reduced_tiles(m):
             def tile_at(n):
@@ -1140,30 +1167,6 @@
                 stores[-1].start()
 
             return act
-
-        def do(*actions):
-            def act():
-                for action in actions:
-                    action()
-
-            return act
-
-        drive(
-            scatter_b.run(net, [p], [branch], slots),
-            [
-                None,
-                None,
-                None,
-                None,
-                do(tick(1), expand_tiles(0)),
-                do(expand_tiles(1), tick(1)),
-                do(*[reduced_tiles(m) for m in range(micro_count)], tick(1)),
-                None,
-            ],
-        )
-        loads[3].wait()
-        keep_middle.wait()
-        norm_out[...] = jnp.zeros_like(norm_out)
 
         def back_rows(at):
             m, rows = own_rows_at(at)
@@ -1182,12 +1185,57 @@
             middle[m, rows, :] = total
             n_own[m, rows, :] = total.astype(BF16)
 
-        loop(micro_count * row_steps, back_rows)
-        for pair in ((middle, grad_out), (n_own, low_out)):
-            stores.append(net.copy(*pair))
-            stores[-1].start()
-        for _ in s:
-            pass
+        def later():
+            for h in (0, 1):
+                expand_tiles(h)()
+                yield
+            for m in range(micro_count):
+                reduced_tiles(m)()
+                yield
+
+        def main():
+            loads[0].wait()
+            loads[1].wait()
+            loop(micro_count * (width // wide), branch_tile)
+            yield
+            yield from scatter_a.run(net, [p], [branch], slots)
+            loads[2].wait()
+            loop(micro_count * row_steps, norm_rows)
+            keep_middle = net.copy(middle, middle_out)
+            keep_middle.start()
+            yield from gather.run(net, [n_own], [n_face], [])
+            loads[4].wait()
+            loop(micro_count * (half // tile), hidden_tile(0))
+            yield
+            weave.finish("e")
+            loop(micro_count * (half // tile), hidden_tile(1))
+            yield
+            loads[5].wait()
+            loop((half // tile) * (width // wide), reduce_tile(0))
+            yield
+            loop((half // tile) * (width // wide), reduce_tile(half))
+            weave.add("s", line_s.run(net, [pr], [reduce_out], line_slots))
+            weave.step("s")
+            yield
+            weave.finish("r")
+            loop(micro_count * (units // tile), slope_tile)
+            yield
+            loop(micro_count * (width // wide), normed_tile)
+            weave.add("x", later())
+            yield from scatter_b.run(net, [p], [branch], slots)
+            loads[3].wait()
+            keep_middle.wait()
+            norm_out[...] = jnp.zeros_like(norm_out)
+            loop(micro_count * row_steps, back_rows)
+            for pair in ((middle, grad_out), (n_own, low_out)):
+                stores.append(net.copy(*pair))
+                stores[-1].start()
+
+        weave.add("m", main())
+        for name in "".join(MLP_ORDER):
+            weave.step(name)
+        for name in "mxsre":
+            weave.finish(name)
         for store in stores:
             store.wait()
 
@@ -1346,6 +1394,186 @@
         compiler_params=pltpu.CompilerParams(vmem_limit_bytes=40 << 20),
         name="attend_backward",
     )(bounds, queries, keys_vals, mixed, grad_mixed, log_total, query_doc, key_doc)
+
+
+def back_block(low, reduced, parts, mixed, wo, wq, normed, queries, keys_vals, logs, limits, nz, ny, collective_id, head_dim):
+    micro_count, own_rows, width = low.shape
+    face_rows, attn = queries.shape[1:]
+    seq_len = keys_vals.shape[1]
+    tokens = micro_count * face_rows
+    blocks = face_rows // BLOCK
+    heads = attn // head_dim
+    tall = heads * BLOCK
+    scale = 1.0 / math.sqrt(head_dim)
+    wide = 512
+    half = parts[0].shape[1]
+    part = jax.ShapeDtypeStruct((micro_count, face_rows, width), BF16)
+    gather = FaceGather(low, nz, ny)
+    scatter_r = FaceScatter(reduced, nz, ny)
+    scatter_q = FaceScatter(part, nz, ny, resident=True)
+    whole = WholeScatter(jax.ShapeDtypeStruct((micro_count, nz, face_rows, 2 * head_dim), BF16), nz, ny, resident=True)
+    line_e = LineScatter(parts, ["row", "row"], nz, ny, resident=True)
+    attn_parts = [jax.ShapeDtypeStruct((attn, width), BF16), jax.ShapeDtypeStruct((width, attn), BF16)]
+    line_a = LineScatter(attn_parts, ["col", "row"], nz, ny, resident=True)
+    plans = [gather, scatter_r, scatter_q, whole, line_e, line_a]
+    groups = [scatter_r, scatter_q, whole, line_e, line_a]
+    outs = scatter_r.outs + scatter_q.outs + whole.outs + line_e.outs + line_a.outs
+    normed = normed.reshape(micro_count, face_rows, width)
+    given = [mixed, wo, wq, queries, keys_vals, logs, limits, *parts]
+    scratch = [pltpu.VMEM(entry.shape, entry.dtype) for entry in given] + [
+        pltpu.VMEM(part.shape, BF16),
+        pltpu.VMEM(queries.shape, BF16),
+        pltpu.VMEM(queries.shape, BF16),
+        pltpu.VMEM((seq_len, 2 * head_dim), F32),
+        pltpu.VMEM((micro_count * nz, face_rows, 2 * head_dim), BF16),
+        pltpu.VMEM((attn, width), BF16),
+        pltpu.VMEM((width, attn), BF16),
+        pltpu.VMEM((2, micro_count, face_rows, wide), BF16),
+    ]
+    shared = len(scratch)
+    for plan in groups:
+        scratch = scratch + plan.scratch
+
+    def body(net, ins, outs, scratch):
+        low, reduced_in, normed_in, *given_in = ins
+        reduced_out, from_out, keys_out, *line_outs = outs
+        mixed, wo, wq, queries, keys_vals, logs, limits, *expand = scratch[: len(given)]
+        face, grad_mixed, grad_queries, acc, grad_keys, part_out, part_query, normed = scratch[len(given) : shared]
+        slots, first = {}, shared
+        for name, plan in zip("rqwea", groups):
+            slots[name] = list(scratch[first : first + len(plan.scratch)])
+            first += len(plan.scratch)
+        loads = [net.copy(*pair) for pair in zip(given_in, scratch)]
+        order = [len(given) - 2, len(given) - 1] + list(range(len(given) - 2))
+        weave = Weave()
+        along = (((1,), (1,)), ((), ()))
+        across = (((0,), (0,)), ((), ()))
+
+        def mix_tile(m):
+            grad_mixed[m] = lax.dot_general(face[m], wo[...], along, preferred_element_type=F32).astype(BF16)
+
+        def attn_out_tile(n):
+            columns = pl.ds(pl.multiple_of(n * wide, wide), wide)
+            part_out[:, columns] = lax.dot_general(
+                mixed[...].reshape(tokens, attn),
+                face[:, :, columns].reshape(tokens, wide),
+                across,
+                preferred_element_type=F32,
+            ).astype(BF16)
+
+        def attn_tile(m):
+            def tile_at(b):
+                rows = pl.ds(pl.multiple_of(b * BLOCK, BLOCK), BLOCK)
+
+                def stack(ref):
+                    return jnp.concatenate(
+                        [ref[m, rows, h * head_dim : (h + 1) * head_dim] for h in range(heads)], axis=0
+                    )
+
+                query, grad = stack(queries), stack(grad_mixed)
+                products = grad.astype(F32) * stack(mixed).astype(F32)
+                delta = jnp.sum(jnp.transpose(products), axis=0, keepdims=True)
+                starts = jnp.concatenate([limits[m, b, 0:1, :]] * heads, axis=1)
+                ends = jnp.concatenate([limits[m, b, 1:2, :]] * heads, axis=1)
+                log_total = logs[m, b]
+                place = lax.broadcasted_iota(jnp.int32, (BLOCK, tall), 0)
+
+                def body(block, grad_query):
+                    first = pl.multiple_of(block * BLOCK, BLOCK)
+                    keys = keys_vals[m, pl.ds(first, BLOCK), :head_dim]
+                    values = keys_vals[m, pl.ds(first, BLOCK), head_dim:]
+                    raw = lax.dot_general(keys, query, along, preferred_element_type=F32)
+                    allowed = (place >= starts - first) & (place < ends - first)
+                    probs = jnp.where(allowed, jnp.exp2(raw * (LOG2_E * scale) - log_total), 0.0)
+                    grad_probs = lax.dot_general(values, grad, along, preferred_element_type=F32)
+                    grad_scores = (probs * (grad_probs - delta)).astype(BF16)
+                    acc[pl.ds(first, BLOCK), :head_dim] += (
+                        jnp.dot(grad_scores, query, preferred_element_type=F32) * scale
+                    )
+                    acc[pl.ds(first, BLOCK), head_dim:] += jnp.dot(
+                        probs.astype(BF16), grad, preferred_element_type=F32
+                    )
+                    return grad_query + lax.dot_general(keys, grad_scores, across, preferred_element_type=F32)
+
+                grad_query = lax.fori_loop(
+                    0, net.z * blocks + b + 1, body, jnp.zeros((head_dim, tall), F32)
+                )
+                grad_query = jnp.transpose(grad_query * scale).astype(BF16)
+                for h in range(heads):
+                    grad_queries[m, rows, h * head_dim : (h + 1) * head_dim] = grad_query[h * BLOCK : (h + 1) * BLOCK]
+
+            return tile_at
+
+        def from_tile(at):
+            m, n = lax.div(at, width // wide), lax.rem(at, width // wide)
+            columns = pl.ds(pl.multiple_of(n * wide, wide), wide)
+            face[m, :, columns] = lax.dot_general(
+                grad_queries[m], wq[columns, :], along, preferred_element_type=F32
+            ).astype(BF16)
+
+        columns_in = [
+            net.copy(normed_in.at[:, :, pl.ds(n * wide, wide)], normed.at[n % 2]) for n in range(width // wide)
+        ]
+
+        def query_tile(n):
+            columns_in[n].wait()
+
+            def tile_at(_):
+                part_query[n * wide : (n + 1) * wide, :] = lax.dot_general(
+                    normed[n % 2].reshape(tokens, wide),
+                    grad_queries[...].reshape(tokens, attn),
+                    across,
+                    preferred_element_type=F32,
+                ).astype(BF16)
+
+            loop(1, tile_at)
+            if n + 2 < width // wide:
+                columns_in[n + 2].start()
+
+        def main():
+            yield from gather.run(net, [low], [face], [])
+            for at in order[2:]:
+                loads[at].wait()
+            loop(micro_count, mix_tile)
+            yield
+            for m in range(micro_count):
+                acc[...] = jnp.zeros_like(acc)
+                loop(blocks, attn_tile(m))
+                for k in range(nz):
+                    grad_keys[m * nz + k] = acc[k * face_rows : (k + 1) * face_rows, :].astype(BF16)
+                yield
+            loop(width // wide, attn_out_tile)
+            weave.add("w", whole.run(net, [grad_keys], [keys_out], slots["w"]))
+            weave.step("w")
+            loop(micro_count * (width // wide), from_tile)
+            weave.add("q", scatter_q.run(net, [face], [from_out], slots["q"]))
+            weave.step("q")
+            for n in range(width // wide):
+                query_tile(n)
+            weave.add("a", line_a.run(net, [part_out, part_query], line_outs[2:], slots["a"]))
+            weave.step("a")
+
+        weave.add("m", main())
+        weave.step("m")
+        for at in order:
+            loads[at].start()
+        for copy in columns_in[:2]:
+            copy.start()
+        for at in order[:2]:
+            loads[at].wait()
+        weave.add("e", line_e.run(net, expand, line_outs[:2], slots["e"]))
+        weave.step("e")
+        weave.add("r", scatter_r.run(net, [reduced_in], [reduced_out], slots["r"]))
+        for name in "".join(BACK_ORDER):
+            weave.step(name)
+        for name in "mwqrea":
+            weave.finish(name)
+
+    ins = [low, reduced, normed, *given]
+    specs = [IN_VMEM] + [ANY] * (len(ins) - 1)
+    return launch(
+        body, ins, specs, outs, scratch, plans, nz, ny, collective_id, "back_block", extra_locals=len(given) + width // wide, vmem=62
+    )
 
 
 def local(
@@ -1437,32 +1665,27 @@
         mixed_flat, wo, inputs, cotangent, cot_face, norms[2:], wexp_first, (w_expand, expand_given), (w_reduce,), *on, collective_id=3
     )
     grad_gain_two, grad_shift_two = jnp.sum(grad_norm_two, axis=1)
-    (grad_branch,), (reduced,), (grad_expand_a, grad_expand_b) = swap(
-        [
-            FaceGather(low_middle, *on),
-            FaceScatter(reduced, *on),
-            LineScatter([part_expand_a, part_expand_b], ["row", "row"], *on),
-        ],
+    same = doc_ids[:, None, :]
+    starts = jnp.sum((same < query_doc[:, :, None]).astype(jnp.int32), axis=-1)
+    ends = jnp.sum((same <= query_doc[:, :, None]).astype(jnp.int32), axis=-1)
+    limits = jnp.stack([starts, ends], axis=1).reshape(micro_count, 2, blocks, BLOCK).transpose(0, 2, 1, 3)
+    reduced, from_query, grad_keys, grad_expand_a, grad_expand_b, grad_attn_out, grad_query = back_block(
+        low_middle,
+        reduced,
+        [part_expand_a, part_expand_b],
+        mixed,
+        wo,
+        wq,
+        normed,
+        queries,
+        keys_vals,
+        log_total,
+        limits,
+        *on,
         collective_id=6,
-        name="gather_branch",
+        head_dim=head_dim,
     )
     outputs = (middle + reduced).astype(BF16)
-    grad_branch = grad_branch.reshape(tokens, width)
-    part_attn_out = dot_at(mixed_flat, grad_branch).astype(BF16)
-    grad_mixed = dot_bt(grad_branch, wo).astype(BF16).reshape(mixed.shape)
-    grad_queries, grad_keys = attend_backward(queries, keys_vals, mixed, grad_mixed, log_total, *docs)
-    grad_queries = grad_queries.reshape(tokens, heads * head_dim)
-    part_query = dot_at(normed, grad_queries).astype(BF16)
-    from_query = dot_bt(grad_queries, wq).astype(BF16).reshape(micro_count, face_rows, width)
-    (from_query,), (grad_keys,), (grad_attn_out, grad_query) = swap(
-        [
-            FaceScatter(from_query, *on),
-            WholeScatter(grad_keys.reshape(micro_count, nz, face_rows, 2 * head_dim), *on),
-            LineScatter([part_attn_out, part_query], ["col", "row"], *on),
-        ],
-        collective_id=7,
-        name="scatter_query",
-    )
     grad_keys = grad_keys.astype(BF16).reshape(micro_count * own_rows, 2 * head_dim)
     normed_own, norm_pull_one = jax.vjp(layer_norm, own_in, gain_one, shift_one)
     grad_normed = from_query + dot_bt(grad_keys, wkv).reshape(from_query.shape)
@@ -1473,7 +1696,7 @@
     small = small.reshape(4, nz, ranks, own_width).transpose(2, 1, 0, 3)
     small = jnp.pad(small, ((0, 0), (0, 0), (0, 4), (0, 128 - own_width)))
     (grad_keyval,), (small,) = swap(
-        [WholeScatter(part_keyval.reshape(1, nz, width // nz, 2 * head_dim), *on), SmallScatter(small, *on)],
+        [QuickScatter(part_keyval.reshape(nz, width // nz, 2 * head_dim), *on), SmallScatter(small, *on)],
         collective_id=8,
         name="scatter_small",
     )
@@ -1491,7 +1714,7 @@
         small[0],
         small[1],
         by_row(grad_query),
-        grad_keyval[0],
+        grad_keyval,
         by_column(grad_attn_out),
         small[2],
         small[3],

time: 530 us -> 485 us (0.915)
  Pallas kernels: 468 us -> 434 us
  matrix products: 20.6 us -> 9.87 us
    pallas_call x6 -> x5, Pallas kernels: 454 us -> 428 us  [launch(): pl.pallas_call(kernel, out_shape=[shape for shape, _ in outs], in_specs=i...]
    pallas_call x1 -> x0, Pallas kernels: 8.23 us -> none  [attend_backward(): pl.pallas_call(kernel, out_shape=[jax.ShapeDtypeStruct(queries.shape, BF1...]
    dot_general x3 -> x1, matrix products: 8.59 us -> 0.77 us  [dot_bt(): lax.dot_general(a, b, (((1,), (1,)), ((), ())), preferred_element_type=F32)]
    dot_general x3 -> x1, matrix products: 7.24 us -> 1.59 us  [dot_at(): lax.dot_general(a, b, (((0,), (0,)), ((), ())), preferred_element_type=F32)]
where the time goes in v4:
time: 485 us; the launch traced here: 482 us
  Pallas kernels  434 us (89%)
  other arithmetic  20.2 us (4%)
  local copies, waits for them, and re-layouts  16.2 us (3%)
  matrix products  9.87 us (2%)
    pallas_call x5, Pallas kernels, launch(): pl.pallas_call(kernel, out_shape=[shape for shape, _ in outs], in_specs=i...  428 us

profile of v4, /device:TPU:0, one launch (start us, length us, event | category | flops | bytes accessed | tf_op | source)
XLA Modules:
  0.0 482.1 jit_solution(872008998601581137)
XLA Ops:
  0.7 0.7 constant_dynamic-slice_fusion
  1.4 0.1 slice.54
  1.5 0.8 slice.53
  2.3 0.2 fusion.27
  2.5 0.1 copy.28
  2.7 0.1 copy.29
  2.8 0.1 reshape.123.bounds_ref
  2.9 0.7 stack.41
  3.6 0.7 stack.42
  4.2 0.7 stack.43
  4.9 0.7 stack.44
  5.6 0.6 concatenate.14.refs_3_
  6.2 55.0 %gather_attention.1 = (bf16[2048,256]{1,0:T(8,128)(2,1)}, bf16[256,2048]{1,0:T(8,128)(2,1)}, bf16[2048,256]{1,0:T(8,128)(2,1)}, bf16[8,8,256]{2,1,0:T(8,128)(2,1...) custom-call(bf16[256,512]{1,0:T(8,128)(2,1)} %refs_0_.1, bf16[512,256]{1,0:T(8,128)(2,1)} %refs_1_.2, ...), custom_call_target="tpu_custom_call" | custom-call | tf_op jit(solution)/shard_map/gather_attention/pallas_call | solution.py:917
  61.2 3.8 convert_reduce_fusion
  65.0 0.8 copy-done.4
  65.8 1.8 fusion.2
  67.6 2.8 fusion.5.refs_2_
  70.4 2.9 convolution_convert_fusion
  73.4 45.1 %gather_keys.1 = (bf16[3,2048,256]{2,1,0:T(8,128)(2,1)}, bf16[2048,512]{1,0:T(8,128)(2,1)}, bf16[3,512,2048]{2,1,0:T(8,128)(2,1)}) custom-call(bf16[3,512,256]{2,1,0:T(8,128)(2,1)} %bitcast.56, bf16[256,2048]{1,0:T(8,128)(2,1)} %refs_7_.1, bf16[256,1024]{1,0:T(8,128)(2,1)} %get-tuple-element.43.refs_2_.refs_8_, bf16[3,64,2048]{2,1,0:T(8,128)(2,1)} %refs_3_.3), custom_call_target="tpu_custom_call" | custom-call | tf_op jit(solution)/shard_map/gather_keys/pallas_call | solution.py:917
  118.5 4.6 convolution_convert_fusion.1
  123.1 0.9 broadcast_in_dim.9.kd_ref
  124.0 1.3 copy-done
  125.3 6.0 %attend_forward.1 = (bf16[3,512,256]{2,1,0:T(8,128)(2,1)S(1)}, f32[3,2,1,512]{3,2,1,0:T(1,128)S(1)}) custom-call(s32[12]{0:T(128)S(1)} %reshape.123.bounds_ref, bf16[3,512,256]{2,1,0:T(8,128)(2,1)S(1)} %bitcast.51, bf16[3,2048,256]{2,1,0:T(8,128)(2,1)S(1)} %copy-done, s32[3,2,1,256]{3,2,1,0:T(1,128)S(1)} %reshape.127.qd_ref, ...), custom_call_target="tpu_custom_call" | custom-call | tf_op jit(solution)/shard_map/attend_forward/pallas_call | solution.py:1300
  131.3 0.9 copy-done.1
  132.2 0.6 copy-done.3
  132.8 0.6 slice.70
  133.4 176.7 %mlp_block.1 = (f32[3,64,2048]{2,1,0:T(8,128)}, f32[3,64,2048]{2,1,0:T(8,128)}, bf16[3,64,2048]{2,1,0:T(8,128)(2,1)}, f32[2,16,2048]{2,1,0:T(8,128)}, bf16[2048,...) custom-call(bf16[1536,256]{1,0:T(8,128)(2,1)} %bitcast.50, ...), custom_call_target="tpu_custom_call" | custom-call | tf_op jit(solution)/shard_map/mlp_block/pallas_call | solution.py:917
  310.1 2.9 convert_reduce_fusion.2
  313.1 0.6 add_bitcast_fusion.refs_9_
  313.7 129.4 %back_block.1 = (f32[3,64,2048]{2,1,0:T(8,128)}, f32[3,64,2048]{2,1,0:T(8,128)}, f32[3,64,256]{2,1,0:T(8,128)}, bf16[2,256,512]{2,1,0:T(8,128)(2,1)}, bf16[2,256...) custom-call(bf16[3,64,2048]{2,1,0:T(8,128)(2,1)} %get-tuple-element.50.refs_0_, ...), custom_call_target="tpu_custom_call" | custom-call | tf_op jit(solution)/shard_map/back_block/pallas_call | solution.py:917
  443.1 1.1 constant_dynamic-update-slice_fusion.1
  444.2 1.1 constant_dynamic-update-slice_fusion
  445.3 0.1 slice_bitcast_fusion.1
  445.4 1.6 maximum_convert_fusion
  447.0 0.9 maximum_convert_fusion.1
  447.9 0.2 convert_reduce_fusion.3
  448.1 0.6 copy-done.10
  448.7 0.8 fusion.16
  449.5 0.8 fusion.15
  450.5 0.1 stack.50
  450.7 0.7 pad.4.refs_1_
  451.3 1.6 fusion.6
  452.9 22.1 %scatter_small.1 = (f32[64,256]{1,0:T(8,128)}, f32[8,128]{1,0:T(8,128)}) custom-call(bf16[4,512,256]{2,1,0:T(8,128)(2,1)} %bitcast.55, f32[8,4,8,128]{3,2,1,0:T(8,128)} %pad.4.refs_1_), custom_call_target="tpu_custom_call" | custom-call | tf_op jit(solution)/shard_map/scatter_small/pallas_call | solution.py:917
  475.0 1.3 slice_bitcast_fusion.4
  476.4 2.1 add_add_fusion.1
  478.6 0.8 bitcast_convert_fusion.1
  479.4 1.5 bitcast_convert_fusion
  481.0 0.6 copy.35
  (61 shorter events, 0.6 us)
Async XLA Ops:
  61.2 4.6 copy-start.4
  65.8 1.8 copy-start.21
  67.6 2.8 copy-start.13
  70.4 3.0 copy-start.6
  73.4 45.1 %copy-start.12 = (bf16[2048,256]{1,0:T(8,128)(2,1)S(1)}, bf16[2048,256]{1,0:T(8,128)(2,1)}, u32[]{:S(2)}) copy-start(bf16[2048,256]{1,0:T(8,128)(2,1)} %get-tuple-element.41.refs_5_) | copy-start | bytes 3145732
  118.5 4.6 copy-start.20
  123.1 0.9 copy-start.2
  123.1 2.2 copy-start
  131.3 0.9 copy-start.1
  132.2 0.6 copy-start.3
  445.4 1.6 copy-start.17
  445.4 2.5 copy-start.5
  445.4 2.7 copy-start.14
  447.0 1.7 copy-start.10
  447.0 1.7 copy-start.18
  449.4 1.0 copy-start.16
  451.3 25.1 %copy-start.7 = (f32[3,64,2048]{2,1,0:T(8,128)S(1)}, f32[3,64,2048]{2,1,0:T(8,128)}, u32[]{:S(2)}) copy-start(f32[3,64,2048]{2,1,0:T(8,128)} %get-tuple-element.49) | copy-start | bytes 4718596
  451.3 25.1 %copy-start.8 = (f32[3,64,2048]{2,1,0:T(8,128)S(1)}, f32[3,64,2048]{2,1,0:T(8,128)}, u32[]{:S(2)}) copy-start(f32[3,64,2048]{2,1,0:T(8,128)} %get-tuple-element.56) | copy-start | bytes 4718596
  451.3 25.1 %copy-start.9 = (f32[3,64,2048]{2,1,0:T(8,128)S(1)}, f32[3,64,2048]{2,1,0:T(8,128)}, u32[]{:S(2)}) copy-start(f32[3,64,2048]{2,1,0:T(8,128)} %get-tuple-element.55) | copy-start | bytes 4718596
  476.4 2.2 copy-start.15
  476.4 3.0 copy-start.11
  479.4 1.6 copy-start.19

commit v5 on v4

--- a/solution.py
+++ b/solution.py
@@ -14,12 +14,12 @@
 GELU_A = math.sqrt(2.0 / math.pi)
 GELU_B = 0.044715
 LOG2_E = 1.0 / math.log(2.0)
-MLP_ORDER = ("mmmmmeeemmmeerrmmmrmmmrmmmrmmmmsmsmmxxmm", "mmsxxsxsmm",)
-BACK_ORDER = ("mrmerrmrrmmmemmemmrreemwwwqwqqaewrawrqaa", "eaqwqwaaw",)
-K1_ORDER = (0, 2, 1, 2, 0, 2, 3, 0, 0, 0, 0, 0, 2, 0, 0, 2, 0, 1, 0, 0, 2, 2, 2, 0, 0, 0, 0, 0, 0, 2)
-K2_ORDER = (0, 2, 2, 1, 0, 1, 1, 2, 2, 2, 0, 2, 0, 1, 2)
+MLP_ORDER = ("mmmmmeeemmmeerrmmmrmmmrmmmrmmmmsmsmmxmmm", "msxxsxs",)
+BACK_ORDER = ("mrmerrmrrmmmemmemmrreemwwwqwqqaewrawrqaa", "eaqwqwaa",)
+FRONT_ORDER = ("omoaaaamaaaaamcoaammhaommaommokkmekcooeh", "kookcacemecmkecmcemcec",)
 MESH = pl.DeviceIdType.MESH
 ANY = pl.BlockSpec(memory_space=pl.ANY)
+READY = "ready"
 IN_VMEM = pl.BlockSpec(memory_space=pltpu.VMEM)
 BF16 = jnp.bfloat16
 F32 = jnp.float32
@@ -417,9 +417,15 @@
         yield
         for copy, fits in shared:
             if fits is None:
-                copy.wait()
+                copy.wait_recv()
             else:
-                pl.when(fits)(copy.wait)
+                pl.when(fits)(copy.wait_recv)
+        yield READY
+        for copy, fits in shared:
+            if fits is None:
+                copy.wait_send()
+            else:
+                pl.when(fits)(copy.wait_send)
         for copy, fits in sent:
             pl.when(fits)(copy.wait_send)
         for copy in swaps.values():
@@ -448,7 +454,10 @@
             copies[-1].start()
         yield
         for copy in copies:
-            copy.wait()
+            copy.wait_recv()
+        yield READY
+        for copy in copies:
+            copy.wait_send()
 
 
 class LineScatter:
@@ -676,9 +685,10 @@
         yield
         for copy, fits in shared:
             pl.when(fits)(copy.wait_recv)
+        keep.wait()
+        yield READY
         for copy, fits in sent:
             pl.when(fits)(copy.wait_send)
-        keep.wait()
 
 
 class WholeScatter(FaceScatter):
@@ -968,15 +978,23 @@
 
 class Weave:
     def __init__(self):
-        self.plans = {}
+        self.plans, self.ready = {}, set()
 
     def add(self, name, steps):
         self.plans[name] = steps
 
     def step(self, name):
         steps = self.plans.get(name)
-        if steps is not None and next(steps, self) is self:
-            del self.plans[name]
+        if steps is not None:
+            state = next(steps, self)
+            if state is self:
+                del self.plans[name]
+            elif state == READY:
+                self.ready.add(name)
+
+    def need(self, name):
+        while name in self.plans and name not in self.ready:
+            self.step(name)
 
     def finish(self, name):
         while name in self.plans:
@@ -1186,6 +1204,7 @@
             n_own[m, rows, :] = total.astype(BF16)
 
         def later():
+            weave.finish("e")
             for h in (0, 1):
                 expand_tiles(h)()
                 yield
@@ -1207,7 +1226,7 @@
             loads[4].wait()
             loop(micro_count * (half // tile), hidden_tile(0))
             yield
-            weave.finish("e")
+            weave.need("e")
             loop(micro_count * (half // tile), hidden_tile(1))
             yield
             loads[5].wait()
@@ -1217,7 +1236,7 @@
             weave.add("s", line_s.run(net, [pr], [reduce_out], line_slots))
             weave.step("s")
             yield
-            weave.finish("r")
+            weave.need("r")
             loop(micro_count * (units // tile), slope_tile)
             yield
             loop(micro_count * (width // wide), normed_tile)
@@ -1246,154 +1265,168 @@
     )
 
 
-def stack_heads(ref, heads, head_dim):
-    return jnp.concatenate([ref[0, :, h * head_dim : (h + 1) * head_dim] for h in range(heads)], axis=0)
-
-
-def masked_scores(queries, keys, query_doc, key_doc, head_dim):
-    raw = lax.dot_general(keys, queries, (((1,), (1,)), ((), ())), preferred_element_type=F32)
-    key_doc = jnp.concatenate([key_doc] * (raw.shape[1] // key_doc.shape[1]), axis=1)
-    return jnp.where(query_doc == key_doc, raw * (LOG2_E / math.sqrt(head_dim)), NEG_FILL)
-
-
-def attend_forward(queries, keys_vals, query_doc, key_doc, bounds, heads, head_dim):
-    micro_count, rows, _ = queries.shape
-    blocks = rows // BLOCK
+def front_block(inputs, cotangent, w_query, w_attn_out, w_keyval, w_expand, norms, limits, nz, ny, collective_id, head_dim):
+    micro_count, own_rows, width = inputs.shape
+    face_rows = own_rows * 4 * ny
+    attn = w_query.shape[1] // 2
+    seq_len = nz * face_rows
+    blocks = face_rows // BLOCK
+    heads = attn // head_dim
     tall = heads * BLOCK
-
-    def kernel(bounds_ref, q_ref, kv_ref, qd_ref, kd_ref, out_ref, log_ref):
-        at = pl.program_id(0) * blocks + pl.program_id(1)
-        low, high = bounds_ref[2 * at], bounds_ref[2 * at + 1]
-        queries = stack_heads(q_ref, heads, head_dim)
-        doc = jnp.concatenate([qd_ref[0, 0]] * heads, axis=1)
-
-        def body(block, carry):
-            top, total, mixed = carry
-            first = pl.multiple_of(block * BLOCK, BLOCK)
-            keys = kv_ref[0, pl.ds(first, BLOCK), :head_dim]
-            values = kv_ref[0, pl.ds(first, BLOCK), head_dim:]
-            scores = masked_scores(queries, keys, doc, kd_ref[0, pl.ds(first, BLOCK), :], head_dim)
-            new_top = jnp.maximum(top, jnp.max(scores, axis=0, keepdims=True))
-            weights = jnp.exp2(scores - new_top)
-            fade = jnp.exp2(top - new_top)
-            total = total * fade + jnp.sum(weights, axis=0, keepdims=True)
-            mixed = mixed * fade + lax.dot_general(
-                values, weights.astype(BF16), (((0,), (0,)), ((), ())), preferred_element_type=F32
+    own = jax.ShapeDtypeStruct(inputs.shape, BF16)
+    keys_face = jax.ShapeDtypeStruct((micro_count, face_rows, 2 * head_dim), BF16)
+    plane = PlaneGather(norms, nz, ny)
+    gather = FaceGather(own, nz, ny)
+    gather_c = FaceGather(cotangent, nz, ny, hold_x=True)
+    swap_e = HalfSwap([w_expand], ["row"], nz, ny)
+    line_a = LineGather([w_keyval, w_query], ["both", "row"], nz, ny)
+    line_o = LineGather([w_attn_out], ["col"], nz, ny)
+    given = jax.ShapeDtypeStruct((w_expand.shape[0], w_expand.shape[1] // 2), BF16)
+    line_e = LineGather([w_expand], ["row"], nz, ny, share=(0, 2), given=[given])
+    keys = KeysGather(keys_face, nz, ny)
+    plans = [plane, gather, gather_c, swap_e, line_a, line_o, line_e, keys]
+    kept = [
+        jax.ShapeDtypeStruct((micro_count, face_rows, width), BF16),
+        line_a.outs[0][0],
+        line_a.outs[1][0],
+        given,
+        jax.ShapeDtypeStruct((micro_count, face_rows, attn), BF16),
+        keys.outs[0][0],
+        jax.ShapeDtypeStruct((micro_count, face_rows, attn), BF16),
+        jax.ShapeDtypeStruct((micro_count, blocks, 1, tall), F32),
+    ]
+    outs = [(shape, ANY) for shape in kept] + [
+        (plane.outs[0][0], IN_VMEM),
+        gather_c.outs[0],
+        line_o.outs[0],
+        line_e.outs[0],
+    ]
+    scratch = [pltpu.VMEM(shape.shape, shape.dtype) for shape in kept] + [
+        pltpu.VMEM(inputs.shape, BF16),
+        pltpu.VMEM(keys_face.shape, BF16),
+    ]
+
+    def body(net, ins, outs, scratch):
+        inputs, cotangent, w_query, w_attn_out, w_keyval, w_expand, norms, limits = ins
+        norms_out, cot_out, wo_out, first_out = outs[len(kept) :]
+        normed, wkv, wq, given, queries, keys_vals, mixed, logs, n_own, keys_face = scratch
+        stores = [net.copy(*pair) for pair in zip(scratch, outs[: len(kept)])]
+        weave = Weave()
+        weave.add("p", plane.run(net, [norms], [norms_out], []))
+        weave.step("p")
+        weave.add("a", line_a.run(net, [w_keyval, w_query], [wkv, wq], []))
+        weave.step("a")
+        weave.add("h", swap_e.run(net, [w_expand], [given], []))
+        weave.add("o", line_o.run(net, [w_attn_out], [wo_out], []))
+        weave.add("c", gather_c.run(net, [cotangent], [cot_out], []))
+
+        def line_first():
+            weave.need("h")
+            yield from line_e.run(net, [w_expand, given], [first_out], [])
+
+        weave.add("e", line_first())
+        along = (((1,), (1,)), ((), ()))
+        across = (((0,), (0,)), ((), ()))
+        step = min(32, own_rows)
+
+        def own_norm(at):
+            m = lax.div(at, own_rows // step)
+            rows = pl.ds(pl.multiple_of(lax.rem(at, own_rows // step) * step, step), step)
+            gain, shift = (
+                jnp.concatenate([norms_out[d].astype(F32)[k : k + 1] for d in range(2 * nz)], axis=1) for k in (0, 1)
             )
-            return new_top, total, mixed
-
-        top, total, mixed = lax.fori_loop(
-            low,
-            high,
-            body,
-            (
-                jnp.full((1, tall), NEG_FILL, F32),
-                jnp.zeros((1, tall), F32),
-                jnp.zeros((head_dim, tall), F32),
-            ),
-        )
-        mixed = jnp.transpose(mixed / total).astype(BF16)
-        for h in range(heads):
-            out_ref[0, :, h * head_dim : (h + 1) * head_dim] = mixed[h * BLOCK : (h + 1) * BLOCK]
-        log_ref[0, 0] = top + jnp.log2(total)
-
-    return pl.pallas_call(
-        kernel,
-        out_shape=[
-            jax.ShapeDtypeStruct(queries.shape, BF16),
-            jax.ShapeDtypeStruct((micro_count, blocks, 1, tall), F32),
-        ],
-        grid_spec=pltpu.PrefetchScalarGridSpec(
-            num_scalar_prefetch=1,
-            grid=(micro_count, blocks),
-            in_specs=[
-                pl.BlockSpec((1, BLOCK, heads * head_dim), lambda m, b, _: (m, b, 0)),
-                pl.BlockSpec((1,) + keys_vals.shape[1:], lambda m, b, _: (m, 0, 0)),
-                pl.BlockSpec((1, 1, 1, BLOCK), lambda m, b, _: (m, b, 0, 0)),
-                pl.BlockSpec((1,) + key_doc.shape[1:], lambda m, b, _: (m, 0, 0)),
-            ],
-            out_specs=[
-                pl.BlockSpec((1, BLOCK, heads * head_dim), lambda m, b, _: (m, b, 0)),
-                pl.BlockSpec((1, 1, 1, tall), lambda m, b, _: (m, b, 0, 0)),
-            ],
-        ),
-        compiler_params=pltpu.CompilerParams(vmem_limit_bytes=40 << 20),
-        name="attend_forward",
-    )(bounds, queries, keys_vals, query_doc, key_doc)
-
-
-def attend_backward(queries, keys_vals, mixed, grad_mixed, log_total, query_doc, key_doc, bounds, heads, head_dim):
-    micro_count, rows, _ = queries.shape
-    blocks = rows // BLOCK
-    seq_len = keys_vals.shape[1]
-    scale = 1.0 / math.sqrt(head_dim)
-    tall = heads * BLOCK
-
-    def kernel(bounds_ref, q_ref, kv_ref, o_ref, do_ref, log_ref, qd_ref, kd_ref, gq_ref, gkv_ref, acc_ref):
-        at = pl.program_id(0) * blocks + pl.program_id(1)
-        low, high = bounds_ref[2 * at], bounds_ref[2 * at + 1]
-
-        @pl.when(pl.program_id(1) == 0)
-        def _():
-            acc_ref[...] = jnp.zeros_like(acc_ref)
-
-        queries, grad = stack_heads(q_ref, heads, head_dim), stack_heads(do_ref, heads, head_dim)
-        products = grad.astype(F32) * stack_heads(o_ref, heads, head_dim).astype(F32)
-        delta = jnp.sum(jnp.transpose(products), axis=0, keepdims=True)
-        doc = jnp.concatenate([qd_ref[0, 0]] * heads, axis=1)
-        log_total = log_ref[0, 0]
-
-        def body(block, grad_queries):
-            first = pl.multiple_of(block * BLOCK, BLOCK)
-            keys = kv_ref[0, pl.ds(first, BLOCK), :head_dim]
-            values = kv_ref[0, pl.ds(first, BLOCK), head_dim:]
-            scores = masked_scores(queries, keys, doc, kd_ref[0, pl.ds(first, BLOCK), :], head_dim)
-            probs = jnp.exp2(scores - log_total)
-            grad_probs = lax.dot_general(values, grad, (((1,), (1,)), ((), ())), preferred_element_type=F32)
-            grad_scores = (probs * (grad_probs - delta)).astype(BF16)
-            acc_ref[pl.ds(first, BLOCK), :head_dim] += (
-                jnp.dot(grad_scores, queries, preferred_element_type=F32) * scale
-            )
-            acc_ref[pl.ds(first, BLOCK), head_dim:] += jnp.dot(probs.astype(BF16), grad, preferred_element_type=F32)
-            return grad_queries + lax.dot_general(
-                keys, grad_scores, (((0,), (0,)), ((), ())), preferred_element_type=F32
-            )
-
-        grad_queries = lax.fori_loop(low, high, body, jnp.zeros((head_dim, tall), F32))
-        grad_queries = jnp.transpose(grad_queries * scale).astype(BF16)
-        for h in range(heads):
-            gq_ref[0, :, h * head_dim : (h + 1) * head_dim] = grad_queries[h * BLOCK : (h + 1) * BLOCK]
-
-        @pl.when(pl.program_id(1) == blocks - 1)
-        def _():
-            gkv_ref[0] = acc_ref[...].astype(BF16)
-
-    wide = pl.BlockSpec((1, BLOCK, heads * head_dim), lambda m, b, _: (m, b, 0))
-    row = pl.BlockSpec((1, seq_len, 2 * head_dim), lambda m, b, _: (m, 0, 0))
-    return pl.pallas_call(
-        kernel,
-        out_shape=[
-            jax.ShapeDtypeStruct(queries.shape, BF16),
-            jax.ShapeDtypeStruct(keys_vals.shape, BF16),
-        ],
-        grid_spec=pltpu.PrefetchScalarGridSpec(
-            num_scalar_prefetch=1,
-            grid=(micro_count, blocks),
-            in_specs=[
-                wide,
-                row,
-                wide,
-                wide,
-                pl.BlockSpec((1, 1, 1, tall), lambda m, b, _: (m, b, 0, 0)),
-                pl.BlockSpec((1, 1, 1, BLOCK), lambda m, b, _: (m, b, 0, 0)),
-                pl.BlockSpec((1,) + key_doc.shape[1:], lambda m, b, _: (m, 0, 0)),
-            ],
-            out_specs=[wide, row],
-            scratch_shapes=[pltpu.VMEM((seq_len, 2 * head_dim), F32)],
-        ),
-        compiler_params=pltpu.CompilerParams(vmem_limit_bytes=40 << 20),
-        name="attend_backward",
-    )(bounds, queries, keys_vals, mixed, grad_mixed, log_total, query_doc, key_doc)
+            values = inputs[m, rows, :].astype(F32)
+            centered = values - jnp.mean(values, axis=-1, keepdims=True)
+            spread = lax.rsqrt(jnp.mean(centered * centered, axis=-1, keepdims=True) + EPSILON)
+            n_own[m, rows, :] = (centered * spread * gain + shift).astype(BF16)
+
+        def keys_tile(m):
+            keys_face[m] = jnp.dot(normed[m], wkv[...], preferred_element_type=F32).astype(BF16)
+
+        def queries_tile(m):
+            queries[m] = jnp.dot(normed[m], wq[...], preferred_element_type=F32).astype(BF16)
+
+        def mixed_tile(m):
+            def tile_at(b):
+                rows = pl.ds(pl.multiple_of(b * BLOCK, BLOCK), BLOCK)
+                query = jnp.concatenate(
+                    [queries[m, rows, h * head_dim : (h + 1) * head_dim] for h in range(heads)], axis=0
+                )
+                starts = jnp.concatenate([limits[m, b, 0:1, :]] * heads, axis=1)
+                ends = jnp.concatenate([limits[m, b, 1:2, :]] * heads, axis=1)
+                place = lax.broadcasted_iota(jnp.int32, (BLOCK, tall), 0)
+
+                def body(block, carry):
+                    top, total, out = carry
+                    first = pl.multiple_of(block * BLOCK, BLOCK)
+                    keys = keys_vals[m, pl.ds(first, BLOCK), :head_dim]
+                    values = keys_vals[m, pl.ds(first, BLOCK), head_dim:]
+                    raw = lax.dot_general(keys, query, along, preferred_element_type=F32)
+                    allowed = (place >= starts - first) & (place < ends - first)
+                    scores = jnp.where(allowed, raw * (LOG2_E / math.sqrt(head_dim)), NEG_FILL)
+                    new_top = jnp.maximum(top, jnp.max(scores, axis=0, keepdims=True))
+                    weights = jnp.exp2(scores - new_top)
+                    fade = jnp.exp2(top - new_top)
+                    total = total * fade + jnp.sum(weights, axis=0, keepdims=True)
+                    out = out * fade + lax.dot_general(
+                        values, weights.astype(BF16), across, preferred_element_type=F32
+                    )
+                    return new_top, total, out
+
+                top, total, out = lax.fori_loop(
+                    0,
+                    net.z * blocks + b + 1,
+                    body,
+                    (
+                        jnp.full((1, tall), NEG_FILL, F32),
+                        jnp.zeros((1, tall), F32),
+                        jnp.zeros((head_dim, tall), F32),
+                    ),
+                )
+                out = jnp.transpose(out / total).astype(BF16)
+                for h in range(heads):
+                    mixed[m, rows, h * head_dim : (h + 1) * head_dim] = out[h * BLOCK : (h + 1) * BLOCK]
+                logs[m, b] = top + jnp.log2(total)
+
+            return tile_at
+
+        def main():
+            weave.finish("p")
+            loop(micro_count * (own_rows // step), own_norm)
+            yield from gather.run(net, [n_own], [normed], [])
+            stores[0].start()
+            yield
+            weave.need("a")
+            loop(micro_count, keys_tile)
+            weave.add("k", keys.run(net, [keys_face], [keys_vals], []))
+            weave.step("k")
+            yield
+            for at in (1, 2):
+                stores[at].start()
+            loop(micro_count, queries_tile)
+            stores[4].start()
+            yield
+            weave.need("k")
+            stores[5].start()
+            for m in range(micro_count):
+                loop(blocks, mixed_tile(m))
+                yield
+            for at in (6, 7):
+                stores[at].start()
+
+        weave.add("m", main())
+        for name in "".join(FRONT_ORDER):
+            weave.step(name)
+        for name in "mhcoeak":
+            weave.finish(name)
+        stores[3].start()
+        for store in stores:
+            store.wait()
+
+    ins = [inputs, cotangent, w_query, w_attn_out, w_keyval, w_expand, norms, limits]
+    return launch(
+        body, ins, [IN_VMEM] * len(ins), outs, scratch, plans, nz, ny, collective_id, "front_block", extra_locals=len(kept)
+    )
 
 
 def back_block(low, reduced, parts, mixed, wo, wq, normed, queries, keys_vals, logs, limits, nz, ny, collective_id, head_dim):
@@ -1576,6 +1609,94 @@
     )
 
 
+def end_block(inputs, grad_middle, from_query, grad_keys, wkv, norms, grad_norm_two, nz, ny, collective_id):
+    micro_count, own_rows, width = inputs.shape
+    rows_all = micro_count * own_rows
+    side = grad_keys.shape[-1]
+    ranks = 4 * ny
+    own_width = width // (nz * ranks)
+    step = min(32, own_rows)
+    part = jax.ShapeDtypeStruct((nz, width // nz, side), BF16)
+    small = jax.ShapeDtypeStruct((ranks, nz, 8, 128), F32)
+    quick, tiny = QuickScatter(part, nz, ny), SmallScatter(small, nz, ny)
+    plans = [quick, tiny]
+    outs = [(jax.ShapeDtypeStruct(inputs.shape, F32), IN_VMEM)] + quick.outs + tiny.outs
+    scratch = [
+        pltpu.VMEM((rows_all, width), BF16),
+        pltpu.VMEM((rows_all, side), BF16),
+        pltpu.VMEM(part.shape, BF16),
+        pltpu.VMEM(small.shape, F32),
+        pltpu.VMEM((2, step, width), F32),
+    ] + quick.scratch + tiny.scratch
+
+    def body(net, ins, outs, scratch):
+        inputs, grad_middle, from_query, grad_keys, wkv, norms, grad_norm_two = ins
+        grad_out, keyval_out, small_out = outs
+        n_own, low_keys, part, small, sums, *slots = scratch
+        weave = Weave()
+
+        def place(at):
+            m, first = lax.div(at, own_rows // step), lax.rem(at, own_rows // step) * step
+            rows = pl.ds(pl.multiple_of(first, step), step)
+            return m, rows, pl.ds(pl.multiple_of(at * step, step), step)
+
+        def unit_rows(m, rows):
+            values = inputs[m, rows, :].astype(F32)
+            centered = values - jnp.mean(values, axis=-1, keepdims=True)
+            spread = lax.rsqrt(jnp.mean(centered * centered, axis=-1, keepdims=True) + EPSILON)
+            return centered * spread, spread
+
+        def first_rows(at):
+            m, rows, flat = place(at)
+            unit, _ = unit_rows(m, rows)
+            n_own[flat, :] = (unit * norms[0:1, :] + norms[1:2, :]).astype(BF16)
+            low_keys[flat, :] = grad_keys[m, rows, :].astype(BF16)
+
+        def keyval_tile(k):
+            columns = pl.ds(pl.multiple_of(k * (width // nz), width // nz), width // nz)
+            part[k] = lax.dot_general(
+                n_own[:, columns], low_keys[...], (((0,), (0,)), ((), ())), preferred_element_type=F32
+            ).astype(BF16)
+
+        def last_rows(at):
+            m, rows, flat = place(at)
+            unit, spread = unit_rows(m, rows)
+            grad = from_query[m, rows, :] + lax.dot_general(
+                low_keys[flat, :], wkv[...], (((1,), (1,)), ((), ())), preferred_element_type=F32
+            )
+            sums[0] += grad * unit
+            sums[1] += grad
+            turned = grad * norms[0:1, :]
+            inner = jnp.mean(turned * unit, axis=-1, keepdims=True)
+            grad_out[m, rows, :] = grad_middle[m, rows, :] + spread * (
+                turned - jnp.mean(turned, axis=-1, keepdims=True) - unit * inner
+            )
+
+        count = rows_all // step
+        loop(count, first_rows)
+        loop(nz, keyval_tile)
+        weave.add("q", quick.run(net, [part], [keyval_out], slots[: len(quick.scratch)]))
+        for _ in range(2 * ny + 1):
+            weave.step("q")
+        sums[...] = jnp.zeros_like(sums)
+        loop(count, last_rows)
+        rows = [jnp.sum(sums[k], axis=0, keepdims=True) for k in (0, 1)]
+        rows += [jnp.sum(grad_norm_two[k], axis=0, keepdims=True) for k in (0, 1)]
+        rows = jnp.concatenate(rows + [jnp.zeros((4, width), F32)], axis=0)
+        for line in range(nz):
+            for rank in range(ranks):
+                first = (line * ranks + rank) * own_width // 128 * 128
+                small[rank, line] = rows[:, first : first + 128]
+        weave.add("s", tiny.run(net, [small], [small_out], slots[len(quick.scratch) :]))
+        for name in "sqsqs":
+            weave.step(name)
+        for name in "qs":
+            weave.finish(name)
+
+    ins = [inputs, grad_middle, from_query, grad_keys, wkv, norms, grad_norm_two]
+    return launch(body, ins, [IN_VMEM] * len(ins), outs, scratch, plans, nz, ny, collective_id, "end_block")
+
+
 def local(
     inputs,
     cotangent,
@@ -1601,74 +1722,34 @@
     head_dim = w_keyval.shape[1] // 2
     heads = w_query.shape[1] // (2 * head_dim)
     z = lax.axis_index("dp") // 2
-    swap = functools.partial(exchange, nz=nz, ny=ny)
     on = (nz, ny)
-
-    def dot(a, b):
-        return jnp.dot(a, b, preferred_element_type=F32)
-
-    def dot_bt(a, b):
-        return lax.dot_general(a, b, (((1,), (1,)), ((), ())), preferred_element_type=F32)
-
-    def dot_at(a, b):
-        return lax.dot_general(a, b, (((0,), (0,)), ((), ())), preferred_element_type=F32)
 
     norms = jnp.stack([attn_gain, attn_shift, mlp_gain, mlp_shift])
     norms = jnp.concatenate([norms, jnp.zeros((4, norms.shape[1]), BF16)])
-    (wq, wo, wkv), (norms,), (face_in,), (expand_given,) = swap(
-        [
-            LineGather([w_query, w_attn_out, w_keyval], ["row", "col", "both"], *on),
-            PlaneGather(norms, *on),
-            FaceGather(inputs, *on, hold_x=True),
-            HalfSwap([w_expand], ["row"], *on),
-        ],
-        collective_id=1,
-        name="gather_attention",
-        order=K1_ORDER,
-    )
-    norms = norms[:, :4].transpose(1, 0, 2).reshape(4, width).astype(F32)
-    gain_one, shift_one = norms[0], norms[1]
-
-    normed = layer_norm(face_in.astype(F32), gain_one, shift_one).astype(BF16).reshape(tokens, width)
-    queries = dot(normed, wq).astype(BF16).reshape(micro_count, face_rows, heads * head_dim)
-    keys_face = dot(normed, wkv).astype(BF16).reshape(micro_count, face_rows, 2 * head_dim)
-    (keys_vals,), (wexp_first,), (cot_face,) = swap(
-        [
-            KeysGather(keys_face, *on),
-            LineGather([w_expand], ["row"], *on, share=(0, 2), given=[expand_given]),
-            FaceGather(cotangent, *on, hold_x=True),
-        ],
-        collective_id=2,
-        name="gather_keys",
-        order=K2_ORDER,
-    )
-
     query_doc = lax.dynamic_slice_in_dim(doc_ids, z * face_rows, face_rows, axis=1)
     blocks = face_rows // BLOCK
-    last_doc = doc_ids[:, BLOCK - 1 :: BLOCK]
-    first_doc = query_doc[:, ::BLOCK]
-    lows = jnp.sum((last_doc[:, None, :] < first_doc[:, :, None]).astype(jnp.int32), axis=-1)
-    highs = jnp.broadcast_to(z * blocks + jnp.arange(blocks, dtype=jnp.int32) + 1, lows.shape)
-    bounds = jnp.stack([lows, highs], axis=-1).reshape(-1)
-    docs = (
-        query_doc.reshape(micro_count, blocks, 1, BLOCK),
-        jnp.broadcast_to(doc_ids[:, :, None], doc_ids.shape + (128,)),
-        bounds,
-        heads,
-        head_dim,
-    )
-    mixed, log_total = attend_forward(queries, keys_vals, *docs)
-    mixed_flat = mixed.reshape(tokens, heads * head_dim)
-
-    own_in = inputs.astype(F32)
-    middle, grad_middle, low_middle, grad_norm_two, part_expand_a, part_expand_b, reduced, grad_reduce = mlp_block(
-        mixed_flat, wo, inputs, cotangent, cot_face, norms[2:], wexp_first, (w_expand, expand_given), (w_reduce,), *on, collective_id=3
-    )
-    grad_gain_two, grad_shift_two = jnp.sum(grad_norm_two, axis=1)
     same = doc_ids[:, None, :]
     starts = jnp.sum((same < query_doc[:, :, None]).astype(jnp.int32), axis=-1)
     ends = jnp.sum((same <= query_doc[:, :, None]).astype(jnp.int32), axis=-1)
     limits = jnp.stack([starts, ends], axis=1).reshape(micro_count, 2, blocks, BLOCK).transpose(0, 2, 1, 3)
+    normed, wkv, wq, expand_given, queries, keys_vals, mixed, log_total, norms, cot_face, wo, wexp_first = front_block(
+        inputs,
+        cotangent,
+        w_query,
+        w_attn_out,
+        w_keyval,
+        w_expand,
+        norms,
+        limits,
+        *on,
+        collective_id=1,
+        head_dim=head_dim,
+    )
+    norms = norms[:, :4].transpose(1, 0, 2).reshape(4, width).astype(F32)
+    mixed_flat = mixed.reshape(tokens, heads * head_dim)
+    middle, grad_middle, low_middle, grad_norm_two, part_expand_a, part_expand_b, reduced, grad_reduce = mlp_block(
+        mixed_flat, wo, inputs, cotangent, cot_face, norms[2:], wexp_first, (w_expand, expand_given), (w_reduce,), *on, collective_id=3
+    )
     reduced, from_query, grad_keys, grad_expand_a, grad_expand_b, grad_attn_out, grad_query = back_block(
         low_middle,
         reduced,
@@ -1686,21 +1767,12 @@
         head_dim=head_dim,
     )
     outputs = (middle + reduced).astype(BF16)
-    grad_keys = grad_keys.astype(BF16).reshape(micro_count * own_rows, 2 * head_dim)
-    normed_own, norm_pull_one = jax.vjp(layer_norm, own_in, gain_one, shift_one)
-    grad_normed = from_query + dot_bt(grad_keys, wkv).reshape(from_query.shape)
-    grad_tok_norm, grad_gain_one, grad_shift_one = norm_pull_one(grad_normed)
-    part_keyval = dot_at(normed_own.astype(BF16).reshape(-1, width), grad_keys).astype(BF16)
+    grad_inputs, grad_keyval, small = end_block(
+        inputs, grad_middle, from_query, grad_keys, wkv, norms[:2], grad_norm_two, *on, collective_id=8
+    )
     own_width = width // (nz * ranks)
-    small = jnp.stack([grad_gain_one, grad_shift_one, grad_gain_two, grad_shift_two])
-    small = small.reshape(4, nz, ranks, own_width).transpose(2, 1, 0, 3)
-    small = jnp.pad(small, ((0, 0), (0, 0), (0, 4), (0, 128 - own_width)))
-    (grad_keyval,), (small,) = swap(
-        [QuickScatter(part_keyval.reshape(nz, width // nz, 2 * head_dim), *on), SmallScatter(small, *on)],
-        collective_id=8,
-        name="scatter_small",
-    )
-    small = small[:4, :own_width]
+    device = lax.axis_index("dp") * tensor_count + lax.axis_index("tensor")
+    small = lax.dynamic_slice_in_dim(small[:4], device * own_width % 128, own_width, axis=1)
 
     def by_row(halves):
         return jnp.concatenate([halves[0], halves[1]], axis=1).astype(F32)
@@ -1710,7 +1782,7 @@
 
     return (
         outputs,
-        grad_middle + grad_tok_norm,
+        grad_inputs,
         small[0],
         small[1],
         by_row(grad_query),

time: 485 us -> 448 us (0.924)
  matrix products: 9.87 us -> 0 us
  other arithmetic: 20.2 us -> 10.9 us
  local copies, waits for them, and re-layouts: 16.2 us -> 7.65 us
  Pallas kernels: 434 us -> 428 us
    dot_general x4 -> x0, matrix products: 9.87 us -> none  [the longest x2 7.52 us: dot(): return jnp.dot(a, b, preferred_element_type=F32)]
    reduce_sum x6 -> x0, other arithmetic: 6.83 us -> none  [the longest x2 4.02 us: layer_norm(): center = jnp.mean(values, axis=-1, keepdims=True)]
    pallas_call x1 -> x0, Pallas kernels: 5.99 us -> none  [attend_forward(): pl.pallas_call(kernel, out_shape=[jax.ShapeDtypeStruct(queries.shape, BF1...]
    pallas_call x5 -> x4, Pallas kernels: 428 us -> 428 us  [launch(): pl.pallas_call(kernel, out_shape=[shape for shape, _ in outs], in_specs=i...]
where the time goes in v5:
time: 448 us
  Pallas kernels  428 us (96%)
  other arithmetic  10.9 us (2%)
  local copies, waits for them, and re-layouts  7.65 us (2%)
    pallas_call x4, Pallas kernels, launch(): pl.pallas_call(kernel, out_shape=[shape for shape, _ in outs], in_specs=i...  428 us

profile of v5, /device:TPU:0, one launch (start us, length us, event | category | flops | bytes accessed | tf_op | source)
XLA Modules:
  0.0 447.6 jit_solution(14762024039213837151)
XLA Ops:
  0.7 0.7 stack.21
  1.3 0.7 stack.22
  2.0 0.7 stack.23
  2.7 0.7 stack.24
  3.3 0.6 concatenate.13.refs_6_
  3.9 0.7 constant_dynamic-slice_fusion.1
  4.6 3.6 convert_reduce_fusion.1
  8.3 0.6 add_bitcast_fusion.refs_7_.refs_9_
  8.9 99.8 %front_block.1 = (bf16[3,512,2048]{2,1,0:T(8,128)(2,1)}, bf16[2048,256]{1,0:T(8,128)(2,1)}, bf16[2048,256]{1,0:T(8,128)(2,1)}, bf16[256,1024]{1,0:T(8,128)(2,1)}...) custom-call(bf16[3,64,2048]{2,1,0:T(8,128)(2,1)} %refs_0_.3, ...), custom_call_target="tpu_custom_call" | custom-call | tf_op jit(solution)/shard_map/front_block/pallas_call | solution.py:927
  108.7 0.8 convert_bitcast_fusion
  109.5 0.6 fusion
  110.1 171.9 %mlp_block.1 = (f32[3,64,2048]{2,1,0:T(8,128)}, f32[3,64,2048]{2,1,0:T(8,128)}, bf16[3,64,2048]{2,1,0:T(8,128)(2,1)}, f32[2,16,2048]{2,1,0:T(8,128)}, bf16[2048,...) custom-call(bf16[1536,256]{1,0:T(8,128)(2,1)} %bitcast.29, ...), custom_call_target="tpu_custom_call" | custom-call | tf_op jit(solution)/shard_map/mlp_block/pallas_call | solution.py:927
  282.0 129.0 %back_block.1 = (f32[3,64,2048]{2,1,0:T(8,128)}, f32[3,64,2048]{2,1,0:T(8,128)}, f32[3,64,256]{2,1,0:T(8,128)}, bf16[2,256,512]{2,1,0:T(8,128)(2,1)}, bf16[2,256...) custom-call(bf16[3,64,2048]{2,1,0:T(8,128)(2,1)} %get-tuple-element.48.refs_0_, ...), custom_call_target="tpu_custom_call" | custom-call | tf_op jit(solution)/shard_map/back_block/pallas_call | solution.py:927
  411.0 0.0 copy-start.1
  411.0 0.0 copy-start.2
  411.0 27.6 %end_block.1 = (f32[3,64,2048]{2,1,0:T(8,128)}, f32[64,256]{1,0:T(8,128)}, f32[8,128]{1,0:T(8,128)}) custom-call(bf16[3,64,2048]{2,1,0:T(8,128)(2,1)} %refs_0_.3, f32[3,64,2048]{2,1,0:T(8,128)} %get-tuple-element.58.refs_1_, f32[3,64,2048]{2,1,0:T(8,128)} %get-tuple-element.59.refs_2_, f32[3,64,256]{2,1,0:T(8,128)} %get-tuple-element.60.refs_3_, ...), custom_call_target="tpu_custom_call" | custom-call | tf_op jit(solution)/shard_map/end_block/pallas_call | solution.py:927
  438.6 0.0 copy-start.9
  438.6 0.0 copy-start.7
  438.7 0.0 copy-done.1
  438.7 0.0 copy-done.2
  438.7 0.0 copy-start.6
  438.7 0.0 copy-start.5
  438.7 1.1 add_convert_fusion
  439.8 0.0 copy-start.4
  439.8 0.0 copy-done.9
  439.8 0.1 constant_dynamic-slice_fusion
  439.9 0.5 slice_bitcast_fusion.4
  440.4 0.0 copy-done.7
  440.4 0.9 maximum_convert_fusion.1
  441.3 0.0 copy-done.6
  441.3 0.8 bitcast_convert_fusion.1
  442.1 0.0 copy-done.5
  442.1 0.1 constant_dynamic-update-slice_fusion.1
  442.2 0.0 copy-done.4
  442.2 0.1 constant_dynamic-update-slice_fusion
  442.2 0.1 slice_bitcast_fusion.1
  442.3 0.0 copy-start.3
  442.3 1.6 maximum_convert_fusion
  443.9 0.0 copy-done.3
  443.9 0.0 copy-start
  443.9 1.5 bitcast_convert_fusion
  445.4 0.4 copy-done
  445.9 0.0 copy-start.8
  445.9 1.1 copy.26
  447.0 0.0 copy-done.8
  447.0 0.6 copy.27
  (5 shorter events, 0.1 us)
Async XLA Ops:
  411.0 27.6 %copy-start.1 = (f32[3,64,2048]{2,1,0:T(8,128)S(1)}, f32[3,64,2048]{2,1,0:T(8,128)}, u32[]{:S(2)}) copy-start(f32[3,64,2048]{2,1,0:T(8,128)} %get-tuple-element.47) | copy-start | bytes 4718596
  411.0 27.6 %copy-start.2 = (f32[3,64,2048]{2,1,0:T(8,128)S(1)}, f32[3,64,2048]{2,1,0:T(8,128)}, u32[]{:S(2)}) copy-start(f32[3,64,2048]{2,1,0:T(8,128)} %get-tuple-element.57) | copy-start | bytes 4718596
  438.6 1.1 copy-start.9
  438.6 1.7 copy-start.7
  438.7 2.6 copy-start.6
  438.7 3.4 copy-start.5
  439.8 2.4 copy-start.4
  442.3 1.6 copy-start.3
  443.9 2.0 copy-start
  445.9 1.1 copy-start.8

commit v6 on v5

--- a/solution.py
+++ b/solution.py
@@ -14,9 +14,9 @@
 GELU_A = math.sqrt(2.0 / math.pi)
 GELU_B = 0.044715
 LOG2_E = 1.0 / math.log(2.0)
-MLP_ORDER = ("mmmmmeeemmmeerrmmmrmmmrmmmrmmmmsmsmmxmmm", "msxxsxs",)
-BACK_ORDER = ("mrmerrmrrmmmemmemmrreemwwwqwqqaewrawrqaa", "eaqwqwaa",)
-FRONT_ORDER = ("omoaaaamaaaaamcoaammhaommaommokkmekcooeh", "kookcacemecmkecmcemcec",)
+MLP_ORDER = ("mmmmmmmrmrmemeemememermmmeeermmrmmmmsmmx", "rmsmmxmxsxss",)
+BACK_ORDER = ("rmmemrrmrmermmmremrmeemwwawqaqqwaqawrwqr", "qeaae",)
+FRONT_ORDER = ("omaoaaamaaamcoaammhaaommommokkmekecaceme", "ckceme",)
 MESH = pl.DeviceIdType.MESH
 ANY = pl.BlockSpec(memory_space=pl.ANY)
 READY = "ready"
@@ -463,13 +463,16 @@
 class LineScatter:
     moves = ("x", "line")
 
-    def __init__(self, parts, kinds, nz, ny, resident=False):
-        self.ins, self.kinds, self.resident = list(parts), list(kinds), resident
+    def __init__(self, parts, kinds, nz, ny, resident=False, joined=False):
+        self.ins, self.kinds, self.resident, self.joined = list(parts), list(kinds), resident, joined
         self.outs, self.scratch = [], []
         for part, kind in zip(parts, kinds):
             rows, columns = part.shape
             shape = (rows // (2 * nz), columns) if kind == "row" else (rows, columns // (2 * nz))
-            self.outs.append((jax.ShapeDtypeStruct((2,) + shape, BF16), ANY))
+            times = 2 * (len(parts) if joined else 1)
+            whole = (shape[0], shape[1] * times) if kind == "row" else (shape[0] * times, shape[1])
+            if not (joined and self.outs):
+                self.outs.append((jax.ShapeDtypeStruct(whole, BF16), ANY))
             for lead in (nz - 1, nz - 1, 1) + (() if resident else (nz,)):
                 self.scratch.append(pltpu.VMEM((lead, 2) + shape, BF16))
         count = len(self.ins)
@@ -480,6 +483,16 @@
         nz, z = net.nz, net.z
         loads, grads = {}, []
         each = 3 if self.resident else 4
+        outs = list(outs) * len(ins) if self.joined else outs
+
+        def spot(at, out):
+            rows, columns = scratch[each * at + 2].shape[2:]
+            kind = self.kinds[at]
+            size = columns if kind == "row" else rows
+            first = (net.x * len(ins) + at) * size if self.joined else net.x * size
+            span = pl.ds(pl.multiple_of(first, size), size)
+            return out.at[:, span] if kind == "row" else out.at[span, :]
+
         for at, (part, out, kind) in enumerate(zip(ins, outs, self.kinds)):
             down, up, mine = scratch[each * at : each * at + 3]
             _, _, rows, columns = mine.shape
@@ -547,9 +560,9 @@
             total = mine.at[0, dx]
             add_rows(_lead(total), terms)
             if dx:
-                net.remote((id(self), at, "x"), total, out.at[net.x], net.device(1, 0)).start()
+                net.remote((id(self), at, "x"), total, spot(at, out), net.device(1, 0)).start()
             else:
-                net.copy_at(self.first_local + at, total, out.at[net.x]).start()
+                net.copy_at(self.first_local + at, total, spot(at, out)).start()
 
         plan = {}
         for place in range(nz):
@@ -591,8 +604,10 @@
             for toward, lines in ((-1, range(nz - 1)), (1, range(1, nz)))
             for line in lines
         ]
-        swaps = [net.remote((id(self), at, "x"), mine.at[0, 1], out.at[net.x], net.device(1, 0)) for at, out, _, _, _, mine in grads]
-        stores = [net.copy_at(self.first_local + at, mine.at[0, 0], out.at[net.x]) for at, out, _, _, _, mine in grads]
+        swaps, stores = [], []
+        for at, out, _, _, _, mine in grads:
+            swaps.append(net.remote((id(self), at, "x"), mine.at[0, 1], spot(at, out), net.device(1, 0)))
+            stores.append(net.copy_at(self.first_local + at, mine.at[0, 0], spot(at, out)))
         yield
         for copy, sends in sent:
             pl.when(sends)(copy.wait_send)
@@ -999,6 +1014,11 @@
     def finish(self, name):
         while name in self.plans:
             self.step(name)
+
+
+def first_block(block, seq_len):
+    longest = seq_len // 2 + BLOCK
+    return jnp.maximum(block - (longest - 1 + BLOCK - 1) // BLOCK, 0)
 
 
 def loop(count, body):
@@ -1103,7 +1123,7 @@
             middle[m, rows, :] = values
             centered = values - jnp.mean(values, axis=-1, keepdims=True)
             spread = lax.rsqrt(jnp.mean(centered * centered, axis=-1, keepdims=True) + EPSILON)
-            n_own[m, rows, :] = (centered * spread * norms[0:1, :] + norms[1:2, :]).astype(BF16)
+            n_own[m, rows, :] = (centered * spread * norms[2:3, :] + norms[3:4, :]).astype(BF16)
 
         def hidden_tile(h):
             def tile_at(at):
@@ -1195,7 +1215,7 @@
             grad = branch[m, rows, :]
             norm_out[0] += grad * unit
             norm_out[1] += grad
-            turned = grad * norms[0:1, :]
+            turned = grad * norms[2:3, :]
             inner = jnp.mean(turned * unit, axis=-1, keepdims=True)
             total = cot_own[m, rows, :].astype(F32) + spread * (
                 turned - jnp.mean(turned, axis=-1, keepdims=True) - unit * inner
@@ -1265,7 +1285,7 @@
     )
 
 
-def front_block(inputs, cotangent, w_query, w_attn_out, w_keyval, w_expand, norms, limits, nz, ny, collective_id, head_dim):
+def front_block(inputs, cotangent, w_query, w_attn_out, w_keyval, w_expand, norms, doc_ids, nz, ny, collective_id, head_dim):
     micro_count, own_rows, width = inputs.shape
     face_rows = own_rows * 4 * ny
     attn = w_query.shape[1] // 2
@@ -1275,7 +1295,9 @@
     tall = heads * BLOCK
     own = jax.ShapeDtypeStruct(inputs.shape, BF16)
     keys_face = jax.ShapeDtypeStruct((micro_count, face_rows, 2 * head_dim), BF16)
-    plane = PlaneGather(norms, nz, ny)
+    shard = norms.shape[1] // 4
+    norms_own = jax.ShapeDtypeStruct((8, shard), F32)
+    plane = PlaneGather(norms_own, nz, ny)
     gather = FaceGather(own, nz, ny)
     gather_c = FaceGather(cotangent, nz, ny, hold_x=True)
     swap_e = HalfSwap([w_expand], ["row"], nz, ny)
@@ -1294,22 +1316,28 @@
         keys.outs[0][0],
         jax.ShapeDtypeStruct((micro_count, face_rows, attn), BF16),
         jax.ShapeDtypeStruct((micro_count, blocks, 1, tall), F32),
+        jax.ShapeDtypeStruct((micro_count, blocks, 2, BLOCK), jnp.int32),
+        own,
     ]
     outs = [(shape, ANY) for shape in kept] + [
-        (plane.outs[0][0], IN_VMEM),
+        (jax.ShapeDtypeStruct((8, width), F32), IN_VMEM),
         gather_c.outs[0],
         line_o.outs[0],
         line_e.outs[0],
     ]
     scratch = [pltpu.VMEM(shape.shape, shape.dtype) for shape in kept] + [
-        pltpu.VMEM(inputs.shape, BF16),
         pltpu.VMEM(keys_face.shape, BF16),
+        pltpu.VMEM((8, shard), F32),
+        pltpu.VMEM((2 * nz, 8, shard), F32),
     ]
 
     def body(net, ins, outs, scratch):
-        inputs, cotangent, w_query, w_attn_out, w_keyval, w_expand, norms, limits = ins
-        norms_out, cot_out, wo_out, first_out = outs[len(kept) :]
-        normed, wkv, wq, given, queries, keys_vals, mixed, logs, n_own, keys_face = scratch
+        inputs, cotangent, w_query, w_attn_out, w_keyval, w_expand, doc_ids, norms_in = ins
+        norm_rows, cot_out, wo_out, first_out = outs[len(kept) :]
+        normed, wkv, wq, given, queries, keys_vals, mixed, logs, limits, n_own, keys_face, norms, norms_out = scratch
+        norms[...] = jnp.zeros_like(norms)
+        for k in range(4):
+            norms[k : k + 1, :] = norms_in[:, k * shard : (k + 1) * shard].astype(F32)
         stores = [net.copy(*pair) for pair in zip(scratch, outs[: len(kept)])]
         weave = Weave()
         weave.add("p", plane.run(net, [norms], [norms_out], []))
@@ -1332,9 +1360,7 @@
         def own_norm(at):
             m = lax.div(at, own_rows // step)
             rows = pl.ds(pl.multiple_of(lax.rem(at, own_rows // step) * step, step), step)
-            gain, shift = (
-                jnp.concatenate([norms_out[d].astype(F32)[k : k + 1] for d in range(2 * nz)], axis=1) for k in (0, 1)
-            )
+            gain, shift = norm_rows[0:1, :], norm_rows[1:2, :]
             values = inputs[m, rows, :].astype(F32)
             centered = values - jnp.mean(values, axis=-1, keepdims=True)
             spread = lax.rsqrt(jnp.mean(centered * centered, axis=-1, keepdims=True) + EPSILON)
@@ -1374,7 +1400,7 @@
                     return new_top, total, out
 
                 top, total, out = lax.fori_loop(
-                    0,
+                    first_block(net.z * blocks + b, seq_len),
                     net.z * blocks + b + 1,
                     body,
                     (
@@ -1390,11 +1416,27 @@
 
             return tile_at
 
+        def limits_tile(m):
+            kinds = lax.broadcasted_iota(jnp.int32, (32, 1), 0)
+            counts = jnp.sum((doc_ids[m : m + 1, :] == kinds).astype(F32), axis=1, keepdims=True)
+            for b in range(blocks):
+                first = pl.multiple_of(net.z * face_rows + b * BLOCK, BLOCK)
+                docs = doc_ids[m : m + 1, pl.ds(first, BLOCK)]
+                starts = jnp.sum(jnp.where(kinds < docs, counts, 0.0), axis=0, keepdims=True)
+                ends = jnp.sum(jnp.where(kinds <= docs, counts, 0.0), axis=0, keepdims=True)
+                limits[m, b, 0:1, :] = starts.astype(jnp.int32)
+                limits[m, b, 1:2, :] = ends.astype(jnp.int32)
+
         def main():
             weave.finish("p")
+            norm_rows[...] = jnp.concatenate([norms_out[d] for d in range(2 * nz)], axis=1)
             loop(micro_count * (own_rows // step), own_norm)
+            stores[9].start()
             yield from gather.run(net, [n_own], [normed], [])
             stores[0].start()
+            for m in range(micro_count):
+                limits_tile(m)
+            stores[8].start()
             yield
             weave.need("a")
             loop(micro_count, keys_tile)
@@ -1423,10 +1465,11 @@
         for store in stores:
             store.wait()
 
-    ins = [inputs, cotangent, w_query, w_attn_out, w_keyval, w_expand, norms, limits]
-    return launch(
+    ins = [inputs, cotangent, w_query, w_attn_out, w_keyval, w_expand, doc_ids, norms]
+    results = launch(
         body, ins, [IN_VMEM] * len(ins), outs, scratch, plans, nz, ny, collective_id, "front_block", extra_locals=len(kept)
     )
+    return results[: len(kept)], results[len(kept) :]
 
 
 def back_block(low, reduced, parts, mixed, wo, wq, normed, queries, keys_vals, logs, limits, nz, ny, collective_id, head_dim):
@@ -1445,7 +1488,7 @@
     scatter_r = FaceScatter(reduced, nz, ny)
     scatter_q = FaceScatter(part, nz, ny, resident=True)
     whole = WholeScatter(jax.ShapeDtypeStruct((micro_count, nz, face_rows, 2 * head_dim), BF16), nz, ny, resident=True)
-    line_e = LineScatter(parts, ["row", "row"], nz, ny, resident=True)
+    line_e = LineScatter(parts, ["row", "row"], nz, ny, resident=True, joined=True)
     attn_parts = [jax.ShapeDtypeStruct((attn, width), BF16), jax.ShapeDtypeStruct((width, attn), BF16)]
     line_a = LineScatter(attn_parts, ["col", "row"], nz, ny, resident=True)
     plans = [gather, scatter_r, scatter_q, whole, line_e, line_a]
@@ -1529,7 +1572,10 @@
                     return grad_query + lax.dot_general(keys, grad_scores, across, preferred_element_type=F32)
 
                 grad_query = lax.fori_loop(
-                    0, net.z * blocks + b + 1, body, jnp.zeros((head_dim, tall), F32)
+                    first_block(net.z * blocks + b, seq_len),
+                    net.z * blocks + b + 1,
+                    body,
+                    jnp.zeros((head_dim, tall), F32),
                 )
                 grad_query = jnp.transpose(grad_query * scale).astype(BF16)
                 for h in range(heads):
@@ -1583,7 +1629,7 @@
             weave.step("q")
             for n in range(width // wide):
                 query_tile(n)
-            weave.add("a", line_a.run(net, [part_out, part_query], line_outs[2:], slots["a"]))
+            weave.add("a", line_a.run(net, [part_out, part_query], line_outs[1:], slots["a"]))
             weave.step("a")
 
         weave.add("m", main())
@@ -1594,7 +1640,7 @@
             copy.start()
         for at in order[:2]:
             loads[at].wait()
-        weave.add("e", line_e.run(net, expand, line_outs[:2], slots["e"]))
+        weave.add("e", line_e.run(net, expand, line_outs[:1], slots["e"]))
         weave.step("e")
         weave.add("r", scatter_r.run(net, [reduced_in], [reduced_out], slots["r"]))
         for name in "".join(BACK_ORDER):
@@ -1609,7 +1655,7 @@
     )
 
 
-def end_block(inputs, grad_middle, from_query, grad_keys, wkv, norms, grad_norm_two, nz, ny, collective_id):
+def end_block(inputs, normed_own, grad_middle, from_query, grad_keys, wkv, norms, grad_norm_two, nz, ny, collective_id):
     micro_count, own_rows, width = inputs.shape
     rows_all = micro_count * own_rows
     side = grad_keys.shape[-1]
@@ -1622,7 +1668,6 @@
     plans = [quick, tiny]
     outs = [(jax.ShapeDtypeStruct(inputs.shape, F32), IN_VMEM)] + quick.outs + tiny.outs
     scratch = [
-        pltpu.VMEM((rows_all, width), BF16),
         pltpu.VMEM((rows_all, side), BF16),
         pltpu.VMEM(part.shape, BF16),
         pltpu.VMEM(small.shape, F32),
@@ -1630,9 +1675,9 @@
     ] + quick.scratch + tiny.scratch
 
     def body(net, ins, outs, scratch):
-        inputs, grad_middle, from_query, grad_keys, wkv, norms, grad_norm_two = ins
+        inputs, n_own, grad_middle, from_query, grad_keys, wkv, norms, grad_norm_two = ins
         grad_out, keyval_out, small_out = outs
-        n_own, low_keys, part, small, sums, *slots = scratch
+        low_keys, part, small, sums, *slots = scratch
         weave = Weave()
 
         def place(at):
@@ -1648,14 +1693,15 @@
 
         def first_rows(at):
             m, rows, flat = place(at)
-            unit, _ = unit_rows(m, rows)
-            n_own[flat, :] = (unit * norms[0:1, :] + norms[1:2, :]).astype(BF16)
             low_keys[flat, :] = grad_keys[m, rows, :].astype(BF16)
 
         def keyval_tile(k):
             columns = pl.ds(pl.multiple_of(k * (width // nz), width // nz), width // nz)
             part[k] = lax.dot_general(
-                n_own[:, columns], low_keys[...], (((0,), (0,)), ((), ())), preferred_element_type=F32
+                n_own[:, :, columns].reshape(rows_all, width // nz),
+                low_keys[...],
+                (((0,), (0,)), ((), ())),
+                preferred_element_type=F32,
             ).astype(BF16)
 
         def last_rows(at):
@@ -1693,7 +1739,7 @@
         for name in "qs":
             weave.finish(name)
 
-    ins = [inputs, grad_middle, from_query, grad_keys, wkv, norms, grad_norm_two]
+    ins = [inputs, normed_own, grad_middle, from_query, grad_keys, wkv, norms, grad_norm_two]
     return launch(body, ins, [IN_VMEM] * len(ins), outs, scratch, plans, nz, ny, collective_id, "end_block")
 
 
@@ -1721,36 +1767,29 @@
     seq_len = doc_ids.shape[1]
     head_dim = w_keyval.shape[1] // 2
     heads = w_query.shape[1] // (2 * head_dim)
-    z = lax.axis_index("dp") // 2
     on = (nz, ny)
 
-    norms = jnp.stack([attn_gain, attn_shift, mlp_gain, mlp_shift])
-    norms = jnp.concatenate([norms, jnp.zeros((4, norms.shape[1]), BF16)])
-    query_doc = lax.dynamic_slice_in_dim(doc_ids, z * face_rows, face_rows, axis=1)
-    blocks = face_rows // BLOCK
-    same = doc_ids[:, None, :]
-    starts = jnp.sum((same < query_doc[:, :, None]).astype(jnp.int32), axis=-1)
-    ends = jnp.sum((same <= query_doc[:, :, None]).astype(jnp.int32), axis=-1)
-    limits = jnp.stack([starts, ends], axis=1).reshape(micro_count, 2, blocks, BLOCK).transpose(0, 2, 1, 3)
-    normed, wkv, wq, expand_given, queries, keys_vals, mixed, log_total, norms, cot_face, wo, wexp_first = front_block(
+    gains = jnp.concatenate([attn_gain, attn_shift, mlp_gain, mlp_shift])[None, :]
+    kept, rest = front_block(
         inputs,
         cotangent,
         w_query,
         w_attn_out,
         w_keyval,
         w_expand,
-        norms,
-        limits,
+        gains,
+        doc_ids,
         *on,
         collective_id=1,
         head_dim=head_dim,
     )
-    norms = norms[:, :4].transpose(1, 0, 2).reshape(4, width).astype(F32)
+    normed, wkv, wq, expand_given, queries, keys_vals, mixed, log_total, limits, normed_own = kept
+    norms, cot_face, wo, wexp_first = rest
     mixed_flat = mixed.reshape(tokens, heads * head_dim)
     middle, grad_middle, low_middle, grad_norm_two, part_expand_a, part_expand_b, reduced, grad_reduce = mlp_block(
-        mixed_flat, wo, inputs, cotangent, cot_face, norms[2:], wexp_first, (w_expand, expand_given), (w_reduce,), *on, collective_id=3
+        mixed_flat, wo, inputs, cotangent, cot_face, norms, wexp_first, (w_expand, expand_given), (w_reduce,), *on, collective_id=3
     )
-    reduced, from_query, grad_keys, grad_expand_a, grad_expand_b, grad_attn_out, grad_query = back_block(
+    reduced, from_query, grad_keys, grad_expand, grad_attn_out, grad_query = back_block(
         low_middle,
         reduced,
         [part_expand_a, part_expand_b],
@@ -1768,30 +1807,24 @@
     )
     outputs = (middle + reduced).astype(BF16)
     grad_inputs, grad_keyval, small = end_block(
-        inputs, grad_middle, from_query, grad_keys, wkv, norms[:2], grad_norm_two, *on, collective_id=8
+        inputs, normed_own, grad_middle, from_query, grad_keys, wkv, norms, grad_norm_two, *on, collective_id=8
     )
     own_width = width // (nz * ranks)
     device = lax.axis_index("dp") * tensor_count + lax.axis_index("tensor")
     small = lax.dynamic_slice_in_dim(small[:4], device * own_width % 128, own_width, axis=1)
-
-    def by_row(halves):
-        return jnp.concatenate([halves[0], halves[1]], axis=1).astype(F32)
-
-    def by_column(halves):
-        return halves.reshape(-1, halves.shape[-1]).astype(F32)
 
     return (
         outputs,
         grad_inputs,
         small[0],
         small[1],
-        by_row(grad_query),
+        grad_query.astype(F32),
         grad_keyval,
-        by_column(grad_attn_out),
+        grad_attn_out.astype(F32),
         small[2],
         small[3],
-        by_row(jnp.concatenate([grad_expand_a, grad_expand_b], axis=2)),
-        by_column(grad_reduce),
+        grad_expand.astype(F32),
+        grad_reduce.astype(F32),
     )
 
 

time: 448 us -> 427 us (0.953)
  Pallas kernels: 428 us -> 414 us
    pallas_call x4, Pallas kernels: 428 us -> 414 us  [launch(): pl.pallas_call(kernel, out_shape=[shape for shape, _ in outs], in_specs=i...]
where the time goes in v6:
time: 427 us
  Pallas kernels  414 us (97%)
  other arithmetic  7.73 us (2%)
    pallas_call x4, Pallas kernels, launch(): pl.pallas_call(kernel, out_shape=[shape for shape, _ in outs], in_specs=i...  414 us

profile of v6, /device:TPU:0, one launch (start us, length us, event | category | flops | bytes accessed | tf_op | source)
XLA Modules:
  0.0 426.5 jit_solution(6681346853833313265)
XLA Ops:
  0.6 0.7 pad_maximum_fusion
  1.4 0.6 broadcast_in_dim.3.refs_7_
  2.0 98.4 %front_block.1 = (bf16[3,512,2048]{2,1,0:T(8,128)(2,1)}, bf16[2048,256]{1,0:T(8,128)(2,1)}, bf16[2048,256]{1,0:T(8,128)(2,1)}, bf16[256,1024]{1,0:T(8,128)(2,1)}...) custom-call(bf16[3,64,2048]{2,1,0:T(8,128)(2,1)} %refs_0_.3, ...), custom_call_target="tpu_custom_call" | custom-call | tf_op jit(solution)/shard_map/front_block/pallas_call | solution.py:942
  100.4 168.1 %mlp_block.1 = (f32[3,64,2048]{2,1,0:T(8,128)}, f32[3,64,2048]{2,1,0:T(8,128)}, bf16[3,64,2048]{2,1,0:T(8,128)(2,1)}, f32[2,16,2048]{2,1,0:T(8,128)}, bf16[2048,...) custom-call(bf16[1536,256]{1,0:T(8,128)(2,1)} %bitcast.9, ...), custom_call_target="tpu_custom_call" | custom-call | tf_op jit(solution)/shard_map/mlp_block/pallas_call | solution.py:942
  268.5 124.6 %back_block.1 = (f32[3,64,2048]{2,1,0:T(8,128)}, f32[3,64,2048]{2,1,0:T(8,128)}, f32[3,64,256]{2,1,0:T(8,128)}, bf16[256,2048]{1,0:T(8,128)(2,1)}, bf16[512,256]{1,0:T(8,128)(2,1)}, /*index=5*/bf16[256,512]{1,0:T(8,128)(2,1)}) custom-call(bf16[3,64,2048]{2,1,0:T(8,128)(2,1)} %get-tuple-element.49.refs_0_, bf16[3,512,2048]{2,1,0:T(8,128)(2,1)} %get-tuple-element.50.refs_1_, ...), custom_call_target="tpu_custom_call" | custom-call | tf_op jit(solution)/shard_map/back_block/pallas_call | solution.py:942
  393.2 23.1 %end_block.1 = (f32[3,64,2048]{2,1,0:T(8,128)}, f32[64,256]{1,0:T(8,128)}, f32[8,128]{1,0:T(8,128)}) custom-call(bf16[3,64,2048]{2,1,0:T(8,128)(2,1)} %refs_0_.3, bf16[3,64,2048]{2,1,0:T(8,128)(2,1)} %get-tuple-element.60.refs_1_, f32[3,64,2048]{2,1,0:T(8,128)} %get-tuple-element.61.refs_2_, f32[3,64,2048]{2,1,0:T(8,128)} %get-tuple-element.62.refs_3_, ...), custom_call_target="tpu_custom_call" | custom-call | tf_op jit(solution)/shard_map/end_block/pallas_call | solution.py:942
  416.2 0.0 copy-start.1
  416.2 0.0 copy-start.2
  416.2 0.8 slice.15
  417.1 0.1 constant_dynamic-slice_fusion
  417.2 0.5 slice_bitcast_fusion
  417.7 2.8 convert_element_type.18
  420.5 0.0 copy-start.5
  420.5 0.0 copy-done.1
  420.5 0.0 copy-done.2
  420.5 0.0 copy-start.4
  420.5 0.0 copy-start.3
  420.5 1.1 add_convert_fusion
  421.6 0.0 copy-done.5
  421.6 0.9 convert_element_type.16
  422.4 0.0 copy-start
  422.4 0.0 copy-done.4
  422.4 0.8 convert_element_type.17
  423.3 0.0 copy-done.3
  423.3 1.5 convert_element_type.19
  424.7 0.0 copy-done
  424.7 0.0 copy-start.6
  424.7 1.1 copy.25
  425.9 0.0 copy-done.6
  425.9 0.6 copy.26
Async XLA Ops:
  416.2 4.3 copy-start.1
  416.2 4.2 copy-start.2
  420.5 1.1 copy-start.5
  420.5 1.9 copy-start.4
  420.5 2.8 copy-start.3
  422.4 2.3 copy-start
  424.7 1.1 copy-start.6

commit v7 on v6

--- a/solution.py
+++ b/solution.py
@@ -14,8 +14,8 @@
 GELU_A = math.sqrt(2.0 / math.pi)
 GELU_B = 0.044715
 LOG2_E = 1.0 / math.log(2.0)
-MLP_ORDER = ("mmmmmmmrmrmemeemememermmmeeermmrmmmmsmmx", "rmsmmxmxsxss",)
-BACK_ORDER = ("rmmemrrmrmermmmremrmeemwwawqaqqwaqawrwqr", "qeaae",)
+MLP_ORDER = ("memmmmeemmrmememmmrmmmmrmmrmmmmmmemmmsxs", "mmmmxxsxxrmm",)
+BACK_ORDER = ("mremmmrrrrmemmmerrmmeemwqqwaawwwqqaqqwaa", "qwearwaerw",)
 FRONT_ORDER = ("omaoaaamaaamcoaammhaaommommokkmekecaceme", "ckceme",)
 MESH = pl.DeviceIdType.MESH
 ANY = pl.BlockSpec(memory_space=pl.ANY)
@@ -57,6 +57,10 @@
         x, y = self.xy(dx, dy)
         return x * (2 * self.ny) + y * 2 + self.flip(self.c, dc)
 
+    def chip_rows(self, dx, dy, rows):
+        first = (self.rank(dx, dy) - self.c) * rows
+        return pl.ds(pl.multiple_of(first, 2 * rows), 2 * rows)
+
     def device(self, dx=0, dy=0, dc=0, z=None):
         x, y = self.xy(dx, dy)
         return ((self.z if z is None else z) * 2 + x, y * 2 + self.flip(self.c, dc))
@@ -110,8 +114,8 @@
     moves = ("x", "y", "c")
     in_spec = IN_VMEM
 
-    def __init__(self, own, nz, ny, hold_x=False):
-        self.ins, self.hold_x = [own], hold_x
+    def __init__(self, own, nz, ny, hold_x=False, report=False):
+        self.ins, self.hold_x, self.report = [own], hold_x, report
         m, t, d = own.shape
         self.outs = [(jax.ShapeDtypeStruct((m, 4 * ny * t, d), own.dtype), ANY)]
         self.scratch = []
@@ -172,10 +176,28 @@
             arrivals.append(on_x + on_y)
         if self.hold_x:
             arrivals = [arrivals[0][1:], arrivals[1][1:], arrivals[0][:1], arrivals[1][:1]]
+        waited = set()
+
+        def shared(*keys):
+            for key in keys:
+                sent[("c",) + key].wait_recv()
+                waited.add(("c",) + key)
+
+        if self.report:
+            yield
+            keep.wait()
+            shared((0,), (1,))
+            yield (0, 0)
         for group in arrivals:
             for arrive in group:
                 yield
                 arrive()
+        if self.report:
+            shared(("x", 0), ("x", 1))
+            yield (1, 0)
+            for dy in dys:
+                shared(("y", dy, 1), ("y", dy, 0))
+                yield (0, -dy % net.ny)
         for dy in dys:
             yield
             sent["xy", dy].wait_recv()
@@ -185,11 +207,15 @@
             share(("yx", dy), 1, -dy % net.ny, 1)
         yield
         for key, copy in sent.items():
-            if key[0] == "c":
+            if key[0] == "c" and key not in waited:
                 copy.wait_recv()
+        if self.report:
+            for dy in dys:
+                yield (1, -dy % net.ny)
+        else:
+            keep.wait()
         for copy in sent.values():
             copy.wait_send()
-        keep.wait()
 
 
 class FaceScatter:
@@ -213,7 +239,7 @@
             self.scratch.append(pltpu.VMEM((2 * ny, m, t, d), BF16))
         self.remotes, self.locals = 6 * ny + 4, 2 * ny
 
-    def run(self, net, ins, outs, scratch):
+    def run(self, net, ins, outs, scratch, produce=None):
         (part,), (out,), half = ins, outs, self.half
         from_core, x_diag, y_diag, x_in, y_in = scratch[:5]
         ny = net.ny
@@ -234,15 +260,15 @@
                 return rows(dx, dy, 0, first, size)
             return scratch[5].at[dx * ny + dy, :, pl.ds(first, size), :]
 
-        for dx, dy in order:
+        def begin(dx, dy):
             at = dx * ny + dy
             if not self.resident:
                 loads[at] = net.copy(rows(dx, dy, 0), work(dx, dy))
                 loads[at].start()
             send(("c", at), rows(dx, dy, 1), from_core.at[at], net.device(0, 0, 1))
-        for dx, dy in order:
+
+        def settle(dx, dy):
             at = dx * ny + dy
-            yield
             if not self.resident:
                 loads[at].wait()
             sent["c", at].wait_recv()
@@ -255,6 +281,18 @@
                 send(("x", 0), top, x_in.at[0], net.device(1, 0))
             elif dy:
                 send(("y", dy, 1), low, y_in.at[1, dy - 1], net.device(0, dy))
+
+        for at, place in enumerate(order):
+            if produce is not None:
+                produce(*place)
+            begin(*place)
+            if produce is not None:
+                yield
+                if at:
+                    settle(*order[at - 1])
+        for place in order if produce is None else order[-1:]:
+            yield
+            settle(*place)
         for dy in dys:
             yield
             sent["xd", dy].wait_recv()
@@ -1033,7 +1071,7 @@
     micro_count, own_rows, width = inputs.shape
     face_rows = cot_face.shape[1]
     tokens = micro_count * face_rows
-    attn = mixed.shape[1]
+    attn = mixed.shape[2]
     units = w_expand[0].shape[1] // 2
     half = units // 2
     tile = min(512, half)
@@ -1042,7 +1080,7 @@
     part_red = jax.ShapeDtypeStruct((units, width), BF16)
     own = (micro_count, own_rows, width)
     scatter_a, scatter_b = (FaceScatter(part, nz, ny, resident=True) for _ in range(2))
-    gather = FaceGather(jax.ShapeDtypeStruct(own, BF16), nz, ny)
+    gather = FaceGather(jax.ShapeDtypeStruct(own, BF16), nz, ny, report=True)
     line_e = LineGather(w_expand[:1], ["row"], nz, ny, share=(1, 2), given=w_expand[1:])
     line_r = LineGather(w_reduce[:1], ["col"], nz, ny, given=w_reduce[1:])
     line_s = LineScatter([part_red], ["col"], nz, ny, resident=True)
@@ -1069,10 +1107,10 @@
         pltpu.VMEM((width, half), BF16),
         pltpu.VMEM((width, half), BF16),
         pltpu.VMEM((units, width), BF16),
-        pltpu.VMEM((tokens, units), BF16),
-        pltpu.VMEM((tokens, units), BF16),
+        pltpu.VMEM((micro_count, face_rows, units), BF16),
+        pltpu.VMEM((micro_count, face_rows, units), BF16),
         pltpu.VMEM((units, width), BF16),
-        pltpu.VMEM((tokens, attn), BF16),
+        pltpu.VMEM((micro_count, face_rows, attn), BF16),
         pltpu.VMEM((attn, width), BF16),
     ]
     shared = len(scratch)
@@ -1106,11 +1144,22 @@
         for load in loads:
             load.start()
 
-        def branch_tile(at):
-            m, n = lax.div(at, width // wide), lax.rem(at, width // wide)
-            columns = pl.ds(pl.multiple_of(n * wide, wide), wide)
-            rows = pl.ds(pl.multiple_of(m * face_rows, face_rows), face_rows)
-            p[m, :, columns] = jnp.dot(mixed[rows, :], wo[:, columns], preferred_element_type=F32).astype(BF16)
+        chip_tokens = micro_count * 2 * own_rows
+
+        def branch_chip(dx, dy):
+            rows = net.chip_rows(dx, dy, own_rows)
+
+            def tile_at(n):
+                columns = pl.ds(pl.multiple_of(n * wide, wide), wide)
+                p[:, rows, columns] = (
+                    jnp.dot(
+                        mixed[:, rows, :].reshape(chip_tokens, attn), wo[:, columns], preferred_element_type=F32
+                    )
+                    .astype(BF16)
+                    .reshape(micro_count, 2 * own_rows, wide)
+                )
+
+            loop(width // wide, tile_at)
 
         row_steps = own_rows // 16
 
@@ -1125,22 +1174,29 @@
             spread = lax.rsqrt(jnp.mean(centered * centered, axis=-1, keepdims=True) + EPSILON)
             n_own[m, rows, :] = (centered * spread * norms[2:3, :] + norms[3:4, :]).astype(BF16)
 
-        def hidden_tile(h):
-            def tile_at(at):
-                m, n = lax.div(at, half // tile), lax.rem(at, half // tile)
-                rows = pl.ds(pl.multiple_of(m * face_rows, face_rows), face_rows)
+        def hidden_chip(dx, dy, h):
+            rows = net.chip_rows(dx, dy, own_rows)
+            block = (micro_count, 2 * own_rows, tile)
+
+            def tile_at(n):
                 columns = pl.ds(pl.multiple_of(n * tile, tile), tile)
                 into = pl.ds(pl.multiple_of(h * half + n * tile, tile), tile)
-                hidden = jnp.dot(n_face[m], we[h][:, columns], preferred_element_type=F32)
+                hidden = jnp.dot(
+                    n_face[:, rows, :].reshape(chip_tokens, width), we[h][:, columns], preferred_element_type=F32
+                )
                 square = hidden * hidden
                 bend = jnp.tanh(GELU_A * hidden * (1.0 + GELU_B * square))
-                active[rows, into] = (0.5 * hidden * (1.0 + bend)).astype(BF16)
-                slope[rows, into] = (
-                    0.5 * (1.0 + bend)
-                    + (0.5 * GELU_A) * hidden * (1.0 - bend * bend) * (1.0 + (3.0 * GELU_B) * square)
-                ).astype(BF16)
-
-            return tile_at
+                active[:, rows, into] = (0.5 * hidden * (1.0 + bend)).astype(BF16).reshape(block)
+                slope[:, rows, into] = (
+                    (
+                        0.5 * (1.0 + bend)
+                        + (0.5 * GELU_A) * hidden * (1.0 - bend * bend) * (1.0 + (3.0 * GELU_B) * square)
+                    )
+                    .astype(BF16)
+                    .reshape(block)
+                )
+
+            loop(half // tile, tile_at)
 
         across = (((0,), (0,)), ((), ()))
         along = (((1,), (1,)), ((), ()))
@@ -1150,7 +1206,7 @@
                 columns = pl.ds(pl.multiple_of(n * wide, wide), wide)
                 rows = pl.ds(pl.multiple_of(first + f * tile, tile), tile)
                 pr[rows, columns] = lax.dot_general(
-                    active[:, rows],
+                    active[:, :, rows].reshape(tokens, tile),
                     cot[:, :, columns].reshape(tokens, wide),
                     across,
                     preferred_element_type=F32,
@@ -1160,24 +1216,32 @@
 
         def slope_tile(at):
             m, n = lax.div(at, units // tile), lax.rem(at, units // tile)
-            rows = pl.ds(pl.multiple_of(m * face_rows, face_rows), face_rows)
             columns = pl.ds(pl.multiple_of(n * tile, tile), tile)
             grad = lax.dot_general(cot[m], wr[columns, :], along, preferred_element_type=F32)
-            slope[rows, columns] = (grad * slope[rows, columns].astype(F32)).astype(BF16)
-
-        def normed_tile(at):
-            m, n = lax.div(at, width // wide), lax.rem(at, width // wide)
-            rows = pl.ds(pl.multiple_of(m * face_rows, face_rows), face_rows)
-            columns = pl.ds(pl.multiple_of(n * wide, wide), wide)
-            grad = lax.dot_general(slope[rows, :half], we0[columns, :], along, preferred_element_type=F32)
-            grad = grad + lax.dot_general(slope[rows, half:], we1[columns, :], along, preferred_element_type=F32)
-            p[m, :, columns] = grad.astype(BF16)
+            slope[m, :, columns] = (grad * slope[m, :, columns].astype(F32)).astype(BF16)
+
+        made = []
+
+        def normed_chip(dx, dy):
+            made.append((dx, dy))
+            rows = net.chip_rows(dx, dy, own_rows)
+
+            def tile_at(n):
+                columns = pl.ds(pl.multiple_of(n * wide, wide), wide)
+                grad = lax.dot_general(
+                    slope[:, rows, :half].reshape(chip_tokens, half), we0[columns, :], along, preferred_element_type=F32
+                )
+                grad = grad + lax.dot_general(
+                    slope[:, rows, half:].reshape(chip_tokens, half), we1[columns, :], along, preferred_element_type=F32
+                )
+                p[:, rows, columns] = grad.astype(BF16).reshape(micro_count, 2 * own_rows, wide)
+
+            loop(width // wide, tile_at)
 
         def reduced_tiles(m):
             def tile_at(n):
-                rows = pl.ds(m * face_rows, face_rows)
                 columns = pl.ds(pl.multiple_of(n * wide, wide), wide)
-                cot[m, :, columns] = jnp.dot(active[rows, :], wr[:, columns], preferred_element_type=F32).astype(BF16)
+                cot[m, :, columns] = jnp.dot(active[m], wr[:, columns], preferred_element_type=F32).astype(BF16)
 
             def act():
                 loop(width // wide, tile_at)
@@ -1194,7 +1258,7 @@
                 grads = pl.ds(pl.multiple_of(h * half + n * tile, tile), tile)
                 we[h][rows, columns] = lax.dot_general(
                     n_face[:, :, rows].reshape(tokens, wide),
-                    slope[:, grads],
+                    slope[:, :, grads].reshape(tokens, tile),
                     across,
                     preferred_element_type=F32,
                 ).astype(BF16)
@@ -1224,6 +1288,8 @@
             n_own[m, rows, :] = total.astype(BF16)
 
         def later():
+            while len(made) < 2 * ny:
+                weave.step("m")
             weave.finish("e")
             for h in (0, 1):
                 expand_tiles(h)()
@@ -1235,20 +1301,25 @@
         def main():
             loads[0].wait()
             loads[1].wait()
-            loop(micro_count * (width // wide), branch_tile)
-            yield
-            yield from scatter_a.run(net, [p], [branch], slots)
+            yield from scatter_a.run(net, [p], [branch], slots, branch_chip)
             loads[2].wait()
             loop(micro_count * row_steps, norm_rows)
             keep_middle = net.copy(middle, middle_out)
             keep_middle.start()
-            yield from gather.run(net, [n_own], [n_face], [])
             loads[4].wait()
-            loop(micro_count * (half // tile), hidden_tile(0))
-            yield
-            weave.need("e")
-            loop(micro_count * (half // tile), hidden_tile(1))
-            yield
+            chips, halved = 0, []
+            for place in gather.run(net, [n_own], [n_face], []):
+                if place is not None:
+                    hidden_chip(*place, 0)
+                    halved.append(place)
+                    chips += 1
+                    if chips > ny:
+                        yield
+                        weave.need("e")
+                        for place in halved:
+                            hidden_chip(*place, 1)
+                        halved = []
+                yield
             loads[5].wait()
             loop((half // tile) * (width // wide), reduce_tile(0))
             yield
@@ -1259,9 +1330,8 @@
             weave.need("r")
             loop(micro_count * (units // tile), slope_tile)
             yield
-            loop(micro_count * (width // wide), normed_tile)
             weave.add("x", later())
-            yield from scatter_b.run(net, [p], [branch], slots)
+            yield from scatter_b.run(net, [p], [branch], slots, normed_chip)
             loads[3].wait()
             keep_middle.wait()
             norm_out[...] = jnp.zeros_like(norm_out)
@@ -1583,12 +1653,23 @@
 
             return tile_at
 
-        def from_tile(at):
-            m, n = lax.div(at, width // wide), lax.rem(at, width // wide)
-            columns = pl.ds(pl.multiple_of(n * wide, wide), wide)
-            face[m, :, columns] = lax.dot_general(
-                grad_queries[m], wq[columns, :], along, preferred_element_type=F32
-            ).astype(BF16)
+        def from_chip(dx, dy):
+            rows = net.chip_rows(dx, dy, own_rows)
+
+            def tile_at(n):
+                columns = pl.ds(pl.multiple_of(n * wide, wide), wide)
+                face[:, rows, columns] = (
+                    lax.dot_general(
+                        grad_queries[:, rows, :].reshape(micro_count * 2 * own_rows, attn),
+                        wq[columns, :],
+                        along,
+                        preferred_element_type=F32,
+                    )
+                    .astype(BF16)
+                    .reshape(micro_count, 2 * own_rows, wide)
+                )
+
+            loop(width // wide, tile_at)
 
         columns_in = [
             net.copy(normed_in.at[:, :, pl.ds(n * wide, wide)], normed.at[n % 2]) for n in range(width // wide)
@@ -1624,8 +1705,7 @@
             loop(width // wide, attn_out_tile)
             weave.add("w", whole.run(net, [grad_keys], [keys_out], slots["w"]))
             weave.step("w")
-            loop(micro_count * (width // wide), from_tile)
-            weave.add("q", scatter_q.run(net, [face], [from_out], slots["q"]))
+            weave.add("q", scatter_q.run(net, [face], [from_out], slots["q"], from_chip))
             weave.step("q")
             for n in range(width // wide):
                 query_tile(n)
@@ -1741,6 +1821,25 @@
 
     ins = [inputs, normed_own, grad_middle, from_query, grad_keys, wkv, norms, grad_norm_two]
     return launch(body, ins, [IN_VMEM] * len(ins), outs, scratch, plans, nz, ny, collective_id, "end_block")
+
+
+def widen(arrays):
+    steps = 4
+
+    def kernel(*refs):
+        for source, target in zip(refs[: len(arrays)], refs[len(arrays) :]):
+            target[...] = source[...].astype(F32)
+
+    specs = [pl.BlockSpec((array.shape[0] // steps, array.shape[1]), lambda step: (step, 0)) for array in arrays]
+    return pl.pallas_call(
+        kernel,
+        out_shape=[jax.ShapeDtypeStruct(array.shape, F32) for array in arrays],
+        grid=(steps,),
+        in_specs=specs,
+        out_specs=specs,
+        compiler_params=pltpu.CompilerParams(vmem_limit_bytes=60 << 20),
+        name="widen",
+    )(*arrays)
 
 
 def local(
@@ -1785,9 +1884,8 @@
     )
     normed, wkv, wq, expand_given, queries, keys_vals, mixed, log_total, limits, normed_own = kept
     norms, cot_face, wo, wexp_first = rest
-    mixed_flat = mixed.reshape(tokens, heads * head_dim)
     middle, grad_middle, low_middle, grad_norm_two, part_expand_a, part_expand_b, reduced, grad_reduce = mlp_block(
-        mixed_flat, wo, inputs, cotangent, cot_face, norms, wexp_first, (w_expand, expand_given), (w_reduce,), *on, collective_id=3
+        mixed, wo, inputs, cotangent, cot_face, norms, wexp_first, (w_expand, expand_given), (w_reduce,), *on, collective_id=3
     )
     reduced, from_query, grad_keys, grad_expand, grad_attn_out, grad_query = back_block(
         low_middle,
@@ -1813,18 +1911,19 @@
     device = lax.axis_index("dp") * tensor_count + lax.axis_index("tensor")
     small = lax.dynamic_slice_in_dim(small[:4], device * own_width % 128, own_width, axis=1)
 
+    grad_query, grad_attn_out, grad_expand, grad_reduce = widen([grad_query, grad_attn_out, grad_expand, grad_reduce])
     return (
         outputs,
         grad_inputs,
         small[0],
         small[1],
-        grad_query.astype(F32),
+        grad_query,
         grad_keyval,
-        grad_attn_out.astype(F32),
+        grad_attn_out,
         small[2],
         small[3],
-        grad_expand.astype(F32),
-        grad_reduce.astype(F32),
+        grad_expand,
+        grad_reduce,
     )
 
 

time: 427 us -> 419 us (0.981)
  other arithmetic: 7.73 us -> 3.17 us
    pallas_call x4, Pallas kernels: 414 us -> 407 us  [launch(): pl.pallas_call(kernel, out_shape=[shape for shape, _ in outs], in_specs=i...]
    convert_element_type x4 -> x0, other arithmetic: 5.95 us -> none  [the longest x1 2.79 us: local(): grad_expand.astype(F32)]
    pallas_call x0 -> x1, Pallas kernels: none -> 4.53 us  [widen(): pl.pallas_call(kernel, out_shape=[jax.ShapeDtypeStruct(array.shape, F32)...]
where the time goes in v7:
time: 419 us
  Pallas kernels  411 us (98%)
    pallas_call x4, Pallas kernels, launch(): pl.pallas_call(kernel, out_shape=[shape for shape, _ in outs], in_specs=i...  407 us

profile of v7, /device:TPU:0, one launch (start us, length us, event | category | flops | bytes accessed | tf_op | source)
XLA Modules:
  0.0 419.1 jit_solution(6386239256269197442)
XLA Ops:
  0.6 0.7 pad_maximum_fusion
  1.4 0.6 broadcast_in_dim.3.refs_7_
  2.0 98.4 %front_block.1 = (bf16[3,512,2048]{2,1,0:T(8,128)(2,1)}, bf16[2048,256]{1,0:T(8,128)(2,1)}, bf16[2048,256]{1,0:T(8,128)(2,1)}, bf16[256,1024]{1,0:T(8,128)(2,1)}...) custom-call(bf16[3,64,2048]{2,1,0:T(8,128)(2,1)} %refs_0_.3, ...), custom_call_target="tpu_custom_call" | custom-call | tf_op jit(solution)/shard_map/front_block/pallas_call | solution.py:980
  100.4 159.7 %mlp_block.1 = (f32[3,64,2048]{2,1,0:T(8,128)}, f32[3,64,2048]{2,1,0:T(8,128)}, bf16[3,64,2048]{2,1,0:T(8,128)(2,1)}, f32[2,16,2048]{2,1,0:T(8,128)}, bf16[2048,...) custom-call(bf16[3,512,256]{2,1,0:T(8,128)(2,1)} %get-tuple-element.46.r, ...), custom_call_target="tpu_custom_call" | custom-call | tf_op jit(solution)/shard_map/mlp_block/pallas_call | solution.py:980
  260.1 124.0 %back_block.1 = (f32[3,64,2048]{2,1,0:T(8,128)}, f32[3,64,2048]{2,1,0:T(8,128)}, f32[3,64,256]{2,1,0:T(8,128)}, bf16[256,2048]{1,0:T(8,128)(2,1)}, bf16[512,256]{1,0:T(8,128)(2,1)}, /*index=5*/bf16[256,512]{1,0:T(8,128)(2,1)}) custom-call(bf16[3,64,2048]{2,1,0:T(8,128)(2,1)} %get-tuple-element.53.refs_0_, bf16[3,512,2048]{2,1,0:T(8,128)(2,1)} %get-tuple-element.54.refs_1_, ...), custom_call_target="tpu_custom_call" | custom-call | tf_op jit(solution)/shard_map/back_block/pallas_call | solution.py:980
  384.2 4.5 %widen.1 = (f32[256,512]{1,0:T(8,128)}, f32[512,256]{1,0:T(8,128)}, f32[256,2048]{1,0:T(8,128)}, f32[2048,256]{1,0:T(8,128)}) custom-call(bf16[256,512]{1,0:T(8,128)(2,1)} %get-tuple-element.72.refs_0_, bf16[512,256]{1,0:T(8,128)(2,1)} %get-tuple-element.73.refs_1_, bf16[256,2048]{1,0:T(8,128)(2,1)} %get-tuple-element.74.refs_2_, ...), custom_call_target="tpu_custom_call" | custom-call | tf_op jit(solution)/shard_map/widen/pallas_call | solution.py:1834
  388.7 0.0 copy-start.1
  388.7 24.7 %end_block.1 = (f32[3,64,2048]{2,1,0:T(8,128)}, f32[64,256]{1,0:T(8,128)}, f32[8,128]{1,0:T(8,128)}) custom-call(bf16[3,64,2048]{2,1,0:T(8,128)(2,1)} %refs_0_.3, bf16[3,64,2048]{2,1,0:T(8,128)(2,1)} %get-tuple-element.64.refs_1_, f32[3,64,2048]{2,1,0:T(8,128)} %get-tuple-element.65.refs_2_, f32[3,64,2048]{2,1,0:T(8,128)} %get-tuple-element.66.refs_3_, ...), custom_call_target="tpu_custom_call" | custom-call | tf_op jit(solution)/shard_map/end_block/pallas_call | solution.py:980
  413.4 0.0 copy-start
  413.5 0.8 slice.15
  414.2 0.1 constant_dynamic-slice_fusion
  414.3 0.5 slice_bitcast_fusion
  414.9 0.0 copy-done.1
  414.9 2.5 add_convert_fusion
  417.3 0.0 copy-done
  417.3 0.0 copy-start.2
  417.3 1.1 copy.25
  418.5 0.0 copy-done.2
  418.5 0.6 copy.26
Async XLA Ops:
  388.7 26.1 %copy-start.1 = (f32[3,64,2048]{2,1,0:T(8,128)S(1)}, f32[3,64,2048]{2,1,0:T(8,128)}, u32[]{:S(2)}) copy-start(f32[3,64,2048]{2,1,0:T(8,128)} %get-tuple-element.52) | copy-start | bytes 4718596
  413.4 3.9 copy-start
  417.3 1.1 copy-start.2

commit v8 on v7

--- a/solution.py
+++ b/solution.py
@@ -1504,9 +1504,6 @@
             stores[9].start()
             yield from gather.run(net, [n_own], [normed], [])
             stores[0].start()
-            for m in range(micro_count):
-                limits_tile(m)
-            stores[8].start()
             yield
             weave.need("a")
             loop(micro_count, keys_tile)
@@ -1515,6 +1512,9 @@
             yield
             for at in (1, 2):
                 stores[at].start()
+            for m in range(micro_count):
+                limits_tile(m)
+            stores[8].start()
             loop(micro_count, queries_tile)
             stores[4].start()
             yield
@@ -1823,23 +1823,28 @@
     return launch(body, ins, [IN_VMEM] * len(ins), outs, scratch, plans, nz, ny, collective_id, "end_block")
 
 
-def widen(arrays):
+def widen(arrays, first, second):
     steps = 4
+    lead, rows, width = first.shape
 
     def kernel(*refs):
-        for source, target in zip(refs[: len(arrays)], refs[len(arrays) :]):
+        sources, (one, two), targets = refs[: len(arrays)], refs[len(arrays) : len(arrays) + 2], refs[len(arrays) + 2 :]
+        for source, target in zip(sources, targets):
             target[...] = source[...].astype(F32)
+        targets[-1][...] = (one[...] + two[...]).astype(BF16)
 
     specs = [pl.BlockSpec((array.shape[0] // steps, array.shape[1]), lambda step: (step, 0)) for array in arrays]
+    wide = pl.BlockSpec((lead, rows // steps, width), lambda step: (0, step, 0))
     return pl.pallas_call(
         kernel,
-        out_shape=[jax.ShapeDtypeStruct(array.shape, F32) for array in arrays],
+        out_shape=[jax.ShapeDtypeStruct(array.shape, F32) for array in arrays]
+        + [jax.ShapeDtypeStruct(first.shape, BF16)],
         grid=(steps,),
-        in_specs=specs,
-        out_specs=specs,
+        in_specs=specs + [wide, wide],
+        out_specs=specs + [wide],
         compiler_params=pltpu.CompilerParams(vmem_limit_bytes=60 << 20),
         name="widen",
-    )(*arrays)
+    )(*arrays, first, second)
 
 
 def local(
@@ -1903,7 +1908,6 @@
         collective_id=6,
         head_dim=head_dim,
     )
-    outputs = (middle + reduced).astype(BF16)
     grad_inputs, grad_keyval, small = end_block(
         inputs, normed_own, grad_middle, from_query, grad_keys, wkv, norms, grad_norm_two, *on, collective_id=8
     )
@@ -1911,7 +1915,9 @@
     device = lax.axis_index("dp") * tensor_count + lax.axis_index("tensor")
     small = lax.dynamic_slice_in_dim(small[:4], device * own_width % 128, own_width, axis=1)
 
-    grad_query, grad_attn_out, grad_expand, grad_reduce = widen([grad_query, grad_attn_out, grad_expand, grad_reduce])
+    grad_query, grad_attn_out, grad_expand, grad_reduce, outputs = widen(
+        [grad_query, grad_attn_out, grad_expand, grad_reduce], middle, reduced
+    )
     return (
         outputs,
         grad_inputs,

time: 419 us -> 417 us (level)
  no operation moved by 1% of the time
where the time goes in v8:
time: 417 us
  Pallas kernels  412 us (99%)
    pallas_call x4, Pallas kernels, launch(): pl.pallas_call(kernel, out_shape=[shape for shape, _ in outs], in_specs=i...  406 us

profile of v8, /device:TPU:0, one launch (start us, length us, event | category | flops | bytes accessed | tf_op | source)
XLA Modules:
  0.0 417.0 jit_solution(1351431230996459261)
XLA Ops:
  0.6 0.7 pad_maximum_fusion
  1.4 0.6 broadcast_in_dim.3.refs_7_
  2.0 98.5 %front_block.1 = (bf16[3,512,2048]{2,1,0:T(8,128)(2,1)}, bf16[2048,256]{1,0:T(8,128)(2,1)}, bf16[2048,256]{1,0:T(8,128)(2,1)}, bf16[256,1024]{1,0:T(8,128)(2,1)}...) custom-call(bf16[3,64,2048]{2,1,0:T(8,128)(2,1)} %refs_0_.3, ...), custom_call_target="tpu_custom_call" | custom-call | tf_op jit(solution)/shard_map/front_block/pallas_call | solution.py:980
  100.4 159.7 %mlp_block.1 = (f32[3,64,2048]{2,1,0:T(8,128)}, f32[3,64,2048]{2,1,0:T(8,128)}, bf16[3,64,2048]{2,1,0:T(8,128)(2,1)}, f32[2,16,2048]{2,1,0:T(8,128)}, bf16[2048,...) custom-call(bf16[3,512,256]{2,1,0:T(8,128)(2,1)} %get-tuple-element.47.r, ...), custom_call_target="tpu_custom_call" | custom-call | tf_op jit(solution)/shard_map/mlp_block/pallas_call | solution.py:980
  260.1 123.6 %back_block.1 = (f32[3,64,2048]{2,1,0:T(8,128)}, f32[3,64,2048]{2,1,0:T(8,128)}, f32[3,64,256]{2,1,0:T(8,128)}, bf16[256,2048]{1,0:T(8,128)(2,1)}, bf16[512,256]{1,0:T(8,128)(2,1)}, /*index=5*/bf16[256,512]{1,0:T(8,128)(2,1)}) custom-call(bf16[3,64,2048]{2,1,0:T(8,128)(2,1)} %get-tuple-element.53.refs_0_, bf16[3,512,2048]{2,1,0:T(8,128)(2,1)} %get-tuple-element.54.refs_1_, ...), custom_call_target="tpu_custom_call" | custom-call | tf_op jit(solution)/shard_map/back_block/pallas_call | solution.py:980
  383.8 24.5 %end_block.1 = (f32[3,64,2048]{2,1,0:T(8,128)}, f32[64,256]{1,0:T(8,128)}, f32[8,128]{1,0:T(8,128)}) custom-call(bf16[3,64,2048]{2,1,0:T(8,128)(2,1)} %refs_0_.3, bf16[3,64,2048]{2,1,0:T(8,128)(2,1)} %get-tuple-element.70.refs_1_, f32[3,64,2048]{2,1,0:T(8,128)} %get-tuple-element.71.refs_2_, f32[3,64,2048]{2,1,0:T(8,128)} %get-tuple-element.72.refs_3_, ...), custom_call_target="tpu_custom_call" | custom-call | tf_op jit(solution)/shard_map/end_block/pallas_call | solution.py:980
  408.3 0.7 slice.15
  408.9 0.1 constant_dynamic-slice_fusion
  409.0 0.5 slice_bitcast_fusion
  409.5 0.0 copy-start
  409.5 5.7 %widen.1 = (f32[256,512]{1,0:T(8,128)}, f32[512,256]{1,0:T(8,128)}, f32[256,2048]{1,0:T(8,128)}, f32[2048,256]{1,0:T(8,128)}, bf16[3,64,2048]{2,1,0:T(8,128)(2,1)}) custom-call(bf16[256,512]{1,0:T(8,128)(2,1)} %get-tuple-element.63.refs_0_, bf16[512,256]{1,0:T(8,128)(2,1)} %get-tuple-element.64.refs_1_, bf16[256,2048]{1,0:T(8,128)(2,1)} %get-tuple-element.65.refs_2_, ...), custom_call_target="tpu_custom_call" | custom-call | tf_op jit(solution)/shard_map/widen/pallas_call | solution.py:1838
  415.2 0.0 copy-start.1
  415.2 0.0 copy-done
  415.2 1.1 copy.25
  416.4 0.0 copy-done.1
  416.4 0.6 copy.26
Async XLA Ops:
  409.5 5.7 %copy-start = (f32[3,64,2048]{2,1,0:T(8,128)S(1)}, f32[3,64,2048]{2,1,0:T(8,128)}, u32[]{:S(2)}) copy-start(f32[3,64,2048]{2,1,0:T(8,128)} %get-tuple-element.99) | copy-start | bytes 4718596
  415.2 1.2 copy-start.1

commit v9 on v8

--- a/solution.py
+++ b/solution.py
@@ -15,7 +15,7 @@
 GELU_B = 0.044715
 LOG2_E = 1.0 / math.log(2.0)
 MLP_ORDER = ("memmmmeemmrmememmmrmmmmrmmrmmmmmmemmmsxs", "mmmmxxsxxrmm",)
-BACK_ORDER = ("mremmmrrrrmemmmerrmmeemwqqwaawwwqqaqqwaa", "qwearwaerw",)
+BACK_ORDER = ("amwwaamewqmarwraqawmwwrqwemwaqqmarwrmmer", "rmmeemmwmwemqqwmqeqmwewwrrarrqaqaqaawewq", "rerrqawrm",)
 FRONT_ORDER = ("omaoaaamaaamcoaammhaaommommokkmekecaceme", "ckceme",)
 MESH = pl.DeviceIdType.MESH
 ANY = pl.BlockSpec(memory_space=pl.ANY)

time: 417 us -> 415 us (level)
  no operation moved by 1% of the time
where the time goes in v9:
time: 415 us
  Pallas kernels  410 us (99%)
    pallas_call x4, Pallas kernels, launch(): pl.pallas_call(kernel, out_shape=[shape for shape, _ in outs], in_specs=i...  404 us

profile of v9, /device:TPU:0, one launch (start us, length us, event | category | flops | bytes accessed | tf_op | source)
XLA Modules:
  0.0 414.7 jit_solution(7244702043951751250)
XLA Ops:
  0.6 0.7 pad_maximum_fusion
  1.4 0.6 broadcast_in_dim.3.refs_7_
  2.0 98.5 %front_block.1 = (bf16[3,512,2048]{2,1,0:T(8,128)(2,1)}, bf16[2048,256]{1,0:T(8,128)(2,1)}, bf16[2048,256]{1,0:T(8,128)(2,1)}, bf16[256,1024]{1,0:T(8,128)(2,1)}...) custom-call(bf16[3,64,2048]{2,1,0:T(8,128)(2,1)} %refs_0_.3, ...), custom_call_target="tpu_custom_call" | custom-call | tf_op jit(solution)/shard_map/front_block/pallas_call | solution.py:980
  100.4 159.7 %mlp_block.1 = (f32[3,64,2048]{2,1,0:T(8,128)}, f32[3,64,2048]{2,1,0:T(8,128)}, bf16[3,64,2048]{2,1,0:T(8,128)(2,1)}, f32[2,16,2048]{2,1,0:T(8,128)}, bf16[2048,...) custom-call(bf16[3,512,256]{2,1,0:T(8,128)(2,1)} %get-tuple-element.47.r, ...), custom_call_target="tpu_custom_call" | custom-call | tf_op jit(solution)/shard_map/mlp_block/pallas_call | solution.py:980
  260.1 120.8 %back_block.1 = (f32[3,64,2048]{2,1,0:T(8,128)}, f32[3,64,2048]{2,1,0:T(8,128)}, f32[3,64,256]{2,1,0:T(8,128)}, bf16[256,2048]{1,0:T(8,128)(2,1)}, bf16[512,256]{1,0:T(8,128)(2,1)}, /*index=5*/bf16[256,512]{1,0:T(8,128)(2,1)}) custom-call(bf16[3,64,2048]{2,1,0:T(8,128)(2,1)} %get-tuple-element.53.refs_0_, bf16[3,512,2048]{2,1,0:T(8,128)(2,1)} %get-tuple-element.54.refs_1_, ...), custom_call_target="tpu_custom_call" | custom-call | tf_op jit(solution)/shard_map/back_block/pallas_call | solution.py:980
  381.0 25.0 %end_block.1 = (f32[3,64,2048]{2,1,0:T(8,128)}, f32[64,256]{1,0:T(8,128)}, f32[8,128]{1,0:T(8,128)}) custom-call(bf16[3,64,2048]{2,1,0:T(8,128)(2,1)} %refs_0_.3, bf16[3,64,2048]{2,1,0:T(8,128)(2,1)} %get-tuple-element.70.refs_1_, f32[3,64,2048]{2,1,0:T(8,128)} %get-tuple-element.71.refs_2_, f32[3,64,2048]{2,1,0:T(8,128)} %get-tuple-element.72.refs_3_, ...), custom_call_target="tpu_custom_call" | custom-call | tf_op jit(solution)/shard_map/end_block/pallas_call | solution.py:980
  405.9 0.7 slice.15
  406.6 0.1 constant_dynamic-slice_fusion
  406.7 0.5 slice_bitcast_fusion
  407.2 0.0 copy-start
  407.2 5.7 %widen.1 = (f32[256,512]{1,0:T(8,128)}, f32[512,256]{1,0:T(8,128)}, f32[256,2048]{1,0:T(8,128)}, f32[2048,256]{1,0:T(8,128)}, bf16[3,64,2048]{2,1,0:T(8,128)(2,1)}) custom-call(bf16[256,512]{1,0:T(8,128)(2,1)} %get-tuple-element.63.refs_0_, bf16[512,256]{1,0:T(8,128)(2,1)} %get-tuple-element.64.refs_1_, bf16[256,2048]{1,0:T(8,128)(2,1)} %get-tuple-element.65.refs_2_, ...), custom_call_target="tpu_custom_call" | custom-call | tf_op jit(solution)/shard_map/widen/pallas_call | solution.py:1838
  412.9 0.0 copy-start.1
  412.9 0.0 copy-done
  412.9 1.1 copy.25
  414.1 0.0 copy-done.1
  414.1 0.6 copy.26
Async XLA Ops:
  407.2 5.7 %copy-start = (f32[3,64,2048]{2,1,0:T(8,128)S(1)}, f32[3,64,2048]{2,1,0:T(8,128)}, u32[]{:S(2)}) copy-start(f32[3,64,2048]{2,1,0:T(8,128)} %get-tuple-element.99) | copy-start | bytes 4718596
  412.9 1.2 copy-start.1
